TPU v7x, 32 devices: a whole 2x2x4 slice. The times are simulated.
32 devices in a mesh: fsdp: 4 (over y, x), context: 4 (over z), tensor: 2 (over core).
Axes of the slice: x: 2, y: 2, z: 4, core: 2. Of those that a mesh axis runs over, the one named last changes fastest.
Arguments:
- layer_input: bfloat16 [4, 1024, 2048], P('fsdp', 'context'), may hold values from -6 to 6
- prefix: int32 [4], P('fsdp'), may hold values from 102 to 512
- attn_gain: float32 [2048], P(('fsdp', 'context')), may hold values from 0.1 to 1.9
- q_weight: float32 [2048, 2048], P(('fsdp', 'context'), 'tensor'), may hold values from -0.125 to 0.125
- k_weight: float32 [2048, 512], P(('fsdp', 'context'), 'tensor'), may hold values from -0.125 to 0.125
- v_weight: float32 [2048, 512], P(('fsdp', 'context'), 'tensor'), may hold values from -0.125 to 0.125
- output_weight: float32 [2048, 2048], P(('fsdp', 'context'), 'tensor'), may hold values from -0.75 to 0.75
- mlp_gain: float32 [2048], P(('fsdp', 'context')), may hold values from 0.1 to 1.9
- gate_weight: float32 [2048, 8192], P(('fsdp', 'context'), 'tensor'), may hold values from -0.125 to 0.125
- up_weight: float32 [2048, 8192], P(('fsdp', 'context'), 'tensor'), may hold values from -0.125 to 0.125
- down_weight: float32 [2048, 8192], P(('fsdp', 'context'), 'tensor'), may hold values from -0.0625 to 0.0625
- cotangent: bfloat16 [4, 1024, 2048], P('fsdp', 'context'), may hold values from -6 to 6
Outputs:
- layer_output: bfloat16 [4, 1024, 2048], P('fsdp', 'context')
- input_grad: bfloat16 [4, 1024, 2048], P('fsdp', 'context')
- attn_gain_grad: float32 [2048], P(('fsdp', 'context'))
- q_weight_grad: float32 [2048, 2048], P(('fsdp', 'context'), 'tensor')
- k_weight_grad: float32 [2048, 512], P(('fsdp', 'context'), 'tensor')
- v_weight_grad: float32 [2048, 512], P(('fsdp', 'context'), 'tensor')
- o_weight_grad: float32 [2048, 2048], P(('fsdp', 'context'), 'tensor')
- mlp_gain_grad: float32 [2048], P(('fsdp', 'context'))
- gate_weight_grad: float32 [2048, 8192], P(('fsdp', 'context'), 'tensor')
- up_weight_grad: float32 [2048, 8192], P(('fsdp', 'context'), 'tensor')
- down_weight_grad: float32 [2048, 8192], P(('fsdp', 'context'), 'tensor')
Inputs may be any that keep to these rules, and one draw needn't show every extreme that they name: prefix counts whole leading tokens of a sequence of 1024.
All inputs are finite; a program needn't handle non-finite values.
Results may differ from a plain program's by a relative error of at most 0.019.
Values may be sent and summed in bfloat16 or wider, within the bound.
No kernel may reach another device: no remote copies, remote signals or barrier semaphores. Data moves between devices by JAX's collectives and lax.ppermute only.
A program may use at most 384 MiB of HBM per device.

v0:
```python
from functools import partial
import math

import jax
import jax.numpy as jnp
from jax import lax
from jax.sharding import PartitionSpec as P

HEADS = 32
KV_HEADS = 8
HEAD_DIM = 64


EPS = 1e-05


def rope_tables(length, head_dim):
    half_dim = head_dim // 2
    freq_index = jnp.arange(half_dim, dtype=jnp.float32)
    base_freq = 1.0 / jnp.power(500000.0, 2.0 * freq_index / head_dim)
    wave_len = 2.0 * math.pi / base_freq
    mix_ratio = jnp.clip((8192.0 / wave_len - 1.0) / 3.0, 0.0, 1.0)
    scaled = (1.0 - mix_ratio) * base_freq / 32.0 + mix_ratio * base_freq
    position = jnp.arange(length, dtype=jnp.float32)
    angles = position[:, None] * scaled[None, :]
    angles = jnp.concatenate([angles, angles], axis=1)
    return (jnp.cos(angles), jnp.sin(angles))


def rotate(tensor_in, cos_table, sin_table):
    half_dim = tensor_in.shape[-1] // 2
    turned = jnp.concatenate([-tensor_in[..., half_dim:], tensor_in[..., :half_dim]], axis=-1)
    return tensor_in * cos_table[:, None, :] + turned * sin_table[:, None, :]


def rotate_rows(flat_in, cos_table, sin_table):
    shaped = flat_in.reshape(flat_in.shape[0], flat_in.shape[1], -1, HEAD_DIM)
    return rotate(shaped, cos_table, sin_table).reshape(flat_in.shape)


def norm_forward(hidden, gain_row):
    inv_rms = lax.rsqrt(jnp.mean(hidden * hidden, axis=-1, keepdims=True) + EPS)
    return ((hidden * inv_rms * gain_row.astype(jnp.float32)).astype(jnp.bfloat16), inv_rms)


def norm_reverse_pass(hidden, inv_rms, gain_row, grad_in):
    weighted = grad_in * gain_row.astype(jnp.float32)
    grad_hidden = inv_rms * weighted - hidden * (inv_rms * inv_rms * inv_rms) * jnp.mean(
        weighted * hidden, axis=-1, keepdims=True
    )
    gain_grad = jnp.sum(grad_in * hidden * inv_rms, axis=(0, 1))
    return (grad_hidden, gain_grad)


def masked_scores(query, keys, prefix_len, first_row):
    row_count = query.shape[0]
    key_count = keys.shape[0]
    kv_local = keys.shape[1] // HEAD_DIM
    grouped = query.reshape(row_count, kv_local, HEADS // KV_HEADS, HEAD_DIM)
    key_heads = keys.reshape(key_count, kv_local, HEAD_DIM)
    logits = jnp.einsum(
        "ikgd,jkd->kgij", grouped, key_heads, preferred_element_type=jnp.float32
    ) * HEAD_DIM ** (-0.5)
    query_pos = first_row + jnp.arange(row_count, dtype=jnp.int32)
    key_pos = jnp.arange(key_count, dtype=jnp.int32)
    allowed = (key_pos[None, :] <= query_pos[:, None]) | (key_pos[None, :] < prefix_len)
    return (jnp.where(allowed, logits, -1e30), grouped, key_heads)


def attend_forward(operands, first_row):
    query, keys, values, prefix_len = operands
    logits, grouped, key_heads = masked_scores(query, keys, prefix_len, first_row)
    row_max = jnp.max(logits, axis=-1, keepdims=True)
    exp_scores = jnp.exp(logits - row_max)
    row_total = jnp.sum(exp_scores, axis=-1, keepdims=True)
    probs_low = (exp_scores / row_total).astype(jnp.bfloat16)
    value_heads = values.reshape(key_heads.shape)
    mixed_out = jnp.einsum(
        "kgij,jkd->ikgd", probs_low, value_heads, preferred_element_type=jnp.float32
    )
    log_total = (row_max + jnp.log(row_total))[..., 0]
    return (mixed_out.reshape(query.shape[0], -1), log_total)


def attend_backward(operands, first_row):
    query, keys, values, prefix_len, log_total, grad_out = operands
    logits, grouped, key_heads = masked_scores(query, keys, prefix_len, first_row)
    probs = jnp.exp(logits - log_total[..., None])
    value_heads = values.reshape(key_heads.shape)
    grad_heads = grad_out.reshape(grouped.shape)
    value_grad = jnp.einsum(
        "kgij,ikgd->jkd", probs.astype(jnp.bfloat16), grad_heads, preferred_element_type=jnp.float32
    )
    grad_probs = jnp.einsum(
        "ikgd,jkd->kgij", grad_heads, value_heads, preferred_element_type=jnp.float32
    )
    delta_rows = jnp.sum(probs * grad_probs, axis=-1, keepdims=True)
    grad_scores = (probs * (grad_probs - delta_rows)).astype(jnp.bfloat16)
    query_grad = jnp.einsum(
        "kgij,jkd->ikgd", grad_scores, key_heads, preferred_element_type=jnp.float32
    ) * HEAD_DIM ** (-0.5)
    key_grad = jnp.einsum(
        "kgij,ikgd->jkd", grad_scores, grouped, preferred_element_type=jnp.float32
    ) * HEAD_DIM ** (-0.5)
    return (
        query_grad.reshape(query.shape[0], -1),
        key_grad.reshape(keys.shape[0], -1),
        value_grad.reshape(keys.shape[0], -1),
    )


def on_device(
    layer_input,
    prefix,
    attn_gain,
    q_weight,
    k_weight,
    v_weight,
    output_weight,
    mlp_gain,
    gate_weight,
    up_weight,
    down_weight,
    cotangent,
):
    row_count = layer_input.shape[1]
    key_count = row_count * lax.axis_size("context")
    first_row = lax.axis_index("context") * row_count
    cos_all, sin_all = rope_tables(key_count, HEAD_DIM)
    cos_table = lax.dynamic_slice_in_dim(cos_all, first_row, row_count, 0)
    sin_table = lax.dynamic_slice_in_dim(sin_all, first_row, row_count, 0)
    gain_one, q_full, k_full, v_full, o_full = (
        lax.all_gather(attn_gain.astype(jnp.bfloat16), ("fsdp", "context"), axis=0, tiled=True),
        lax.all_gather(q_weight.astype(jnp.bfloat16), ("fsdp", "context"), axis=0, tiled=True),
        lax.all_gather(k_weight.astype(jnp.bfloat16), ("fsdp", "context"), axis=0, tiled=True),
        lax.all_gather(v_weight.astype(jnp.bfloat16), ("fsdp", "context"), axis=0, tiled=True),
        lax.all_gather(output_weight.astype(jnp.bfloat16), ("fsdp", "context"), axis=0, tiled=True),
    )
    hidden_in = layer_input.astype(jnp.float32)
    normed_one, rms_one = norm_forward(hidden_in, gain_one)
    query = jnp.einsum("scd,de->sce", normed_one, q_full, preferred_element_type=jnp.float32)
    key_proj = jnp.einsum("scd,de->sce", normed_one, k_full, preferred_element_type=jnp.float32)
    value_low = jnp.einsum(
        "scd,de->sce", normed_one, v_full, preferred_element_type=jnp.float32
    ).astype(jnp.bfloat16)
    query_rot = rotate_rows(query, cos_table, sin_table).astype(jnp.bfloat16)
    key_rot = rotate_rows(key_proj, cos_table, sin_table).astype(jnp.bfloat16)
    keys_all, values_all = (
        lax.all_gather(key_rot, "context", axis=1, tiled=True),
        lax.all_gather(value_low, "context", axis=1, tiled=True),
    )
    attended, log_total = lax.map(
        partial(attend_forward, first_row=first_row), (query_rot, keys_all, values_all, prefix)
    )
    attended_low = attended.astype(jnp.bfloat16)
    attn_branch = lax.psum(
        jnp.einsum("sce,de->scd", attended_low, o_full, preferred_element_type=jnp.float32),
        "tensor",
    )
    resid = hidden_in + attn_branch
    gain_two, gate_full, up_full, down_full = (
        lax.all_gather(mlp_gain.astype(jnp.bfloat16), ("fsdp", "context"), axis=0, tiled=True),
        lax.all_gather(gate_weight.astype(jnp.bfloat16), ("fsdp", "context"), axis=0, tiled=True),
        lax.all_gather(up_weight.astype(jnp.bfloat16), ("fsdp", "context"), axis=0, tiled=True),
        lax.all_gather(down_weight.astype(jnp.bfloat16), ("fsdp", "context"), axis=0, tiled=True),
    )
    normed_two, rms_two = norm_forward(resid, gain_two)
    gate_proj = jnp.einsum("scd,df->scf", normed_two, gate_full, preferred_element_type=jnp.float32)
    up_projection = jnp.einsum(
        "scd,df->scf", normed_two, up_full, preferred_element_type=jnp.float32
    )
    inner_act = (jax.nn.silu(gate_proj) * up_projection).astype(jnp.bfloat16)
    mlp_branch = lax.psum(
        jnp.einsum("scf,df->scd", inner_act, down_full, preferred_element_type=jnp.float32).astype(
            jnp.bfloat16
        ),
        "tensor",
    ).astype(jnp.float32)
    layer_output = (resid + mlp_branch).astype(jnp.bfloat16)
    gain_two, gate_full, up_full, down_full = (
        lax.all_gather(mlp_gain.astype(jnp.bfloat16), ("fsdp", "context"), axis=0, tiled=True),
        lax.all_gather(gate_weight.astype(jnp.bfloat16), ("fsdp", "context"), axis=0, tiled=True),
        lax.all_gather(up_weight.astype(jnp.bfloat16), ("fsdp", "context"), axis=0, tiled=True),
        lax.all_gather(down_weight.astype(jnp.bfloat16), ("fsdp", "context"), axis=0, tiled=True),
    )
    grad_inner = jnp.einsum("scd,df->scf", cotangent, down_full, preferred_element_type=jnp.float32)
    squash = jax.nn.sigmoid(gate_proj)
    grad_gate = (grad_inner * up_projection * squash * (1.0 + gate_proj * (1.0 - squash))).astype(
        jnp.bfloat16
    )
    grad_up = (grad_inner * gate_proj * squash).astype(jnp.bfloat16)
    grad_normed_two = lax.psum(
        (
            jnp.einsum("scf,df->scd", grad_gate, gate_full, preferred_element_type=jnp.float32)
            + jnp.einsum("scf,df->scd", grad_up, up_full, preferred_element_type=jnp.float32)
        ).astype(jnp.bfloat16),
        "tensor",
    ).astype(jnp.float32)
    resid_part, gain_two_grad = norm_reverse_pass(resid, rms_two, gain_two, grad_normed_two)
    grad_resid = cotangent.astype(jnp.float32) + resid_part
    gate_part = jnp.einsum("scd,scf->df", normed_two, grad_gate, preferred_element_type=jnp.float32)
    up_part = jnp.einsum("scd,scf->df", normed_two, grad_up, preferred_element_type=jnp.float32)
    pair_part = jnp.stack([gate_part, up_part], axis=1)
    down_part = jnp.einsum("scd,scf->df", cotangent, inner_act, preferred_element_type=jnp.float32)
    mlp_grads = lax.psum_scatter(
        jnp.concatenate([pair_part, down_part[:, None, :]], axis=1),
        ("fsdp", "context"),
        scatter_dimension=0,
        tiled=True,
    )
    gate_share = mlp_grads[:, 0, :]
    up_share = mlp_grads[:, 1, :]
    down_share = mlp_grads[:, 2, :]
    gain_one, q_full, k_full, v_full, o_full = (
        lax.all_gather(attn_gain.astype(jnp.bfloat16), ("fsdp", "context"), axis=0, tiled=True),
        lax.all_gather(q_weight.astype(jnp.bfloat16), ("fsdp", "context"), axis=0, tiled=True),
        lax.all_gather(k_weight.astype(jnp.bfloat16), ("fsdp", "context"), axis=0, tiled=True),
        lax.all_gather(v_weight.astype(jnp.bfloat16), ("fsdp", "context"), axis=0, tiled=True),
        lax.all_gather(output_weight.astype(jnp.bfloat16), ("fsdp", "context"), axis=0, tiled=True),
    )
    keys_all, values_all = (
        lax.all_gather(key_rot, "context", axis=1, tiled=True),
        lax.all_gather(value_low, "context", axis=1, tiled=True),
    )
    branch_gradient = grad_resid.astype(jnp.bfloat16)
    o_part = jnp.einsum(
        "scd,sce->de", branch_gradient, attended_low, preferred_element_type=jnp.float32
    )
    grad_att = jnp.einsum(
        "scd,de->sce", branch_gradient, o_full, preferred_element_type=jnp.float32
    ).astype(jnp.bfloat16)
    query_grad, every_key_gradient, value_grad_all = lax.map(
        partial(attend_backward, first_row=first_row),
        (query_rot, keys_all, values_all, prefix, log_total, grad_att),
    )
    key_grad, value_grad = (
        lax.psum_scatter(
            every_key_gradient.astype(jnp.bfloat16), "context", scatter_dimension=1, tiled=True
        ).astype(jnp.float32),
        lax.psum_scatter(
            value_grad_all.astype(jnp.bfloat16), "context", scatter_dimension=1, tiled=True
        ).astype(jnp.float32),
    )
    query_low = rotate_rows(query_grad, cos_table, -sin_table).astype(jnp.bfloat16)
    key_low = rotate_rows(key_grad, cos_table, -sin_table).astype(jnp.bfloat16)
    value_grad_low = value_grad.astype(jnp.bfloat16)
    q_part = jnp.einsum("scd,sce->de", normed_one, query_low, preferred_element_type=jnp.float32)
    k_part = jnp.einsum("scd,sce->de", normed_one, key_low, preferred_element_type=jnp.float32)
    v_part = jnp.einsum(
        "scd,sce->de", normed_one, value_grad_low, preferred_element_type=jnp.float32
    )
    local_normed = jnp.einsum("sce,de->scd", query_low, q_full, preferred_element_type=jnp.float32)
    local_normed = local_normed + jnp.einsum(
        "sce,de->scd", key_low, k_full, preferred_element_type=jnp.float32
    )
    local_normed = local_normed + jnp.einsum(
        "sce,de->scd", value_grad_low, v_full, preferred_element_type=jnp.float32
    )
    grad_normed_one = lax.psum(local_normed.astype(jnp.bfloat16), "tensor").astype(jnp.float32)
    input_part, gain_one_grad = norm_reverse_pass(hidden_in, rms_one, gain_one, grad_normed_one)
    input_grad = (grad_resid + input_part).astype(jnp.bfloat16)
    shares = (
        lax.psum_scatter(gain_one_grad, ("fsdp", "context"), scatter_dimension=0, tiled=True),
        lax.psum_scatter(q_part, ("fsdp", "context"), scatter_dimension=0, tiled=True),
        lax.psum_scatter(k_part, ("fsdp", "context"), scatter_dimension=0, tiled=True),
        lax.psum_scatter(v_part, ("fsdp", "context"), scatter_dimension=0, tiled=True),
        lax.psum_scatter(o_part, ("fsdp", "context"), scatter_dimension=0, tiled=True),
        lax.psum_scatter(gain_two_grad, ("fsdp", "context"), scatter_dimension=0, tiled=True),
    )
    return (
        layer_output,
        input_grad,
        shares[0],
        shares[1],
        shares[2],
        shares[3],
        shares[4],
        shares[5],
        gate_share,
        up_share,
        down_share,
    )


def solution(mesh):
    placed = (
        P("fsdp", "context", None),
        P("fsdp"),
        P(("fsdp", "context")),
        P(("fsdp", "context"), "tensor"),
        P(("fsdp", "context"), "tensor"),
        P(("fsdp", "context"), "tensor"),
        P(("fsdp", "context"), "tensor"),
        P(("fsdp", "context")),
        P(("fsdp", "context"), "tensor"),
        P(("fsdp", "context"), "tensor"),
        P(("fsdp", "context"), "tensor"),
        P("fsdp", "context", None),
    )
    return jax.shard_map(
        on_device,
        mesh=mesh,
        in_specs=placed,
        out_specs=(
            P("fsdp", "context", None),
            P("fsdp", "context", None),
            P(("fsdp", "context")),
            P(("fsdp", "context"), "tensor"),
            P(("fsdp", "context"), "tensor"),
            P(("fsdp", "context"), "tensor"),
            P(("fsdp", "context"), "tensor"),
            P(("fsdp", "context")),
            P(("fsdp", "context"), "tensor"),
            P(("fsdp", "context"), "tensor"),
            P(("fsdp", "context"), "tensor"),
        ),
        check_vma=False,
    )
```

profile of v0, /device:TPU:1, one launch (start us, length us, event | category | flops | bytes accessed | tf_op | source)
XLA Modules:
  0.0 3717.9 jit_solution(15053935400837778976)
XLA Ops:
  14.9 34.4 all-gather.2
  54.2 13.3 all-gather.14.cloned.1.call-done
  69.6 55.5 %all-gather.12.cloned.1.call-done = bf16[2048,256]{1,0:T(8,128)(2,1)} async-done(((bf16[128,256]{1,0:T(8,128)(2,1)}), bf16[2048,256]{1,0:T(8,128)(2,1)}) %all-gather.12.cloned.1.call-update) | async-done | bytes 1048592 | tf_op jit(solution)/shard_map/all_gather | solution.py:136
  126.8 13.7 all-gather
  141.5 13.4 all-gather.1
  154.9 49.5 %all-gather.16.cloned.1.call-done = bf16[2048,1024]{1,0:T(8,128)(2,1)} async-done(((bf16[128,1024]{1,0:T(8,128)(2,1)}), bf16[2048,1024]{1,0:T(8,128)(2,1)}) %all-gather.16.cloned.1.call-update) | async-done | bytes 4194320 | tf_op jit(solution)/shard_map/all_gather | solution.py:134
  221.9 8.1 fusion.3
  237.6 44.5 %all-gather.18.cloned.1.call-done = bf16[2048,1024]{1,0:T(8,128)(2,1)} async-done(((bf16[128,1024]{1,0:T(8,128)(2,1)}), bf16[2048,1024]{1,0:T(8,128)(2,1)}) %all-gather.18.cloned.1.call-update) | async-done | bytes 4194320 | tf_op jit(solution)/shard_map/all_gather | solution.py:137
  293.9 32.3 all-gather.3
  328.4 175.7 %all-gather.22.cloned.1.call-done = bf16[2048,4096]{1,0:T(8,128)(2,1)} async-done(((bf16[128,4096]{1,0:T(8,128)(2,1)}), bf16[2048,4096]{1,0:T(8,128)(2,1)}) %all-gather.22.cloned.1.call-update) | async-done | bytes 16777232 | tf_op jit(solution)/shard_map/all_gather | solution.py:164
  504.1 10.1 fusion.81
  514.2 183.5 %all-gather.20.cloned.1.call-done = bf16[2048,4096]{1,0:T(8,128)(2,1)} async-done(((bf16[128,4096]{1,0:T(8,128)(2,1)}), bf16[2048,4096]{1,0:T(8,128)(2,1)}) %all-gather.20.cloned.1.call-update) | async-done | bytes 16777232 | tf_op jit(solution)/shard_map/all_gather | solution.py:163
  697.7 10.2 fusion.80
  707.9 183.3 %all-gather.24.cloned.1.call-done = bf16[2048,4096]{1,0:T(8,128)(2,1)} async-done(((bf16[128,4096]{1,0:T(8,128)(2,1)}), bf16[2048,4096]{1,0:T(8,128)(2,1)}) %all-gather.24.cloned.1.call-update) | async-done | bytes 16777232 | tf_op jit(solution)/shard_map/all_gather | solution.py:165
  891.2 12.5 multiply_convert_fusion
  903.7 13.1 convolution_bitcast_fusion.1
  916.8 13.5 convolution_bitcast_fusion.2
  930.3 12.2 fusion.82
  942.6 12.5 fusion.15
  955.2 15.6 convolution_bitcast_fusion
  970.7 12.2 fusion.14
  990.1 15.6 fusion
  1005.7 8.2 fusion.2
  1021.2 9.4 fusion.36
  1043.5 17.5 reduce-scatter.10.cloned.1.call-done
  1064.4 66.2 %pad_maximum_fusion = f32[2048,3,4096]{2,0,1:T(8,128)} fusion(f32[2048,1,4096]{2,0,1:T(8,128)} %convolution_bitcast_fusion, f32[2048,1,4096]{2,0,1:T(8,128)} %convolution_bitcast_fusion.1, f32[2048,1,4096]{2,0,1:T(8,128)} %convolution_bitcast_fusion.2), kind=kLoop, calls=%fused_computation | loop fusion | flops 50331648 | bytes 201326592 | tf_op jit(solution)/shard_map/concatenate | solution.py:206
  1153.3 72.9 %all-reduce.2 = (f32[2048]{0:T(1024)S(1)}, f32[2048]{0:T(1024)S(1)}) all-reduce(f32[2048]{0:T(1024)S(1)} %get-tuple-element.59, f32[2048]{0:T(1024)S(1)} %get-tuple-element.57), channel_id=6, replica_groups=mesh['fsdp'=4,'context'=4,'tensor'=2] {'fsdp','context'}, use_global_device_ids=true, to_apply=%region_14.15.clone | all-reduce | flops 4096 | bytes 32768
  1231.5 1944.4 %reduce-scatter.20.cloned.1.call-done = f32[128,3,4096]{2,0,1:T(8,128)} async-done(((f32[2048,3,4096]{2,0,1:T(8,128)}), f32[128,3,4096]{2,0,1:T(8,128)}) %reduce-scatter.20.cloned.1.call-update) | async-done | bytes 6291472 | tf_op jit(solution)/shard_map/reduce_scatter | solution.py:205
  3181.6 71.2 %reduce-scatter.16.cloned.1.call-done = f32[128,256]{1,0:T(8,128)} async-done(((f32[2048,256]{1,0:T(8,128)}), f32[128,256]{1,0:T(8,128)}) %reduce-scatter.16.cloned.1.call-update) | async-done | bytes 131088 | tf_op jit(solution)/shard_map/reduce_scatter | solution.py:266
  3252.8 83.4 %reduce-scatter.14.cloned.1.call-done = f32[128,256]{1,0:T(8,128)} async-done(((f32[2048,256]{1,0:T(8,128)}), f32[128,256]{1,0:T(8,128)}) %reduce-scatter.14.cloned.1.call-update) | async-done | bytes 131088 | tf_op jit(solution)/shard_map/reduce_scatter | solution.py:265
  3336.2 192.3 %reduce-scatter.18.cloned.1.call-done = f32[128,1024]{1,0:T(8,128)} async-done(((f32[2048,1024]{1,0:T(8,128)}), f32[128,1024]{1,0:T(8,128)}) %reduce-scatter.18.cloned.1.call-update) | async-done | bytes 524304 | tf_op jit(solution)/shard_map/reduce_scatter | solution.py:267
  3528.6 182.6 %reduce-scatter.12.cloned.1.call-done = f32[128,1024]{1,0:T(8,128)} async-done(((f32[2048,1024]{1,0:T(8,128)}), f32[128,1024]{1,0:T(8,128)}) %reduce-scatter.12.cloned.1.call-update) | async-done | bytes 524304 | tf_op jit(solution)/shard_map/reduce_scatter | solution.py:264
  (188 shorter events, 119.0 us)
Async XLA Ops:
  7.2 60.4 %all-gather.14.cloned.1.call-start = ((), (), s32[]{:S(2)}) async-start(), calls=%async_computation.8 | async-start | bytes 1114112 | tf_op jit(solution)/shard_map/all_gather | solution.py:135
  8.8 116.3 %all-gather.12.cloned.1.call-start = ((), (), s32[]{:S(2)}) async-start(), calls=%async_computation.7 | async-start | bytes 1114112 | tf_op jit(solution)/shard_map/all_gather | solution.py:136
  10.4 194.0 %all-gather.16.cloned.1.call-start = ((), (), s32[]{:S(2)}) async-start(), calls=%async_computation.9 | async-start | bytes 4456448 | tf_op jit(solution)/shard_map/all_gather | solution.py:134
  12.3 269.9 %all-gather.18.cloned.1.call-start = ((), (), s32[]{:S(2)}) async-start(), calls=%async_computation.10 | async-start | bytes 4456448 | tf_op jit(solution)/shard_map/all_gather | solution.py:137
  14.1 312.1 %all-reduce.8.cloned.1.call-start = ((), (), s32[]{:S(2)}) async-start(), calls=%async_computation.11 | async-start | bytes 4194304 | tf_op jit(solution)/shard_map/psum | solution.py:156
  49.2 155.2 %copy-start.21 = (f32[16,1,128]{2,1,0:T(1,128)}, f32[16,1,128]{2,1,0:T(1,128)S(1)}, u32[]{:S(2)}) copy-start(f32[16,1,128]{2,1,0:T(1,128)S(1)} %convert_element_type.260) | copy-start | bytes 24580
  50.3 19.2 copy-start.17
  54.0 150.4 %copy-start.26 = (f32[256]{0:T(256)}, f32[256]{0:T(256)S(1)}, u32[]{:S(2)}) copy-start(f32[256]{0:T(256)S(1)} %get-tuple-element.97) | copy-start | bytes 3076
  154.9 59.8 %copy-start.7 = (bf16[1024,256]{0,1:T(8,128)(2,1)}, bf16[1024,256]{0,1:T(8,128)(2,1)S(1)}, u32[]{:S(2)}) copy-start(bf16[1024,256]{0,1:T(8,128)(2,1)S(1)} %all-gather.1) | copy-start | bytes 1572868
  237.6 44.5 %copy-start.23 = (bf16[4,64,4,256]{3,1,2,0:T(8,128)(2,1)}, bf16[4,64,4,256]{3,1,2,0:T(8,128)(2,1)S(1)}, u32[]{:S(2)}) copy-start(bf16[4,64,4,256]{3,1,2,0:T(8,128)(2,1)S(1)} %fusion.40) | copy-start | bytes 1572868
  287.0 217.1 %all-gather.22.cloned.1.call-start = ((), (), s32[]{:S(2)}) async-start(), calls=%async_computation.13 | async-start | bytes 17825792 | tf_op jit(solution)/shard_map/all_gather | solution.py:164
  289.7 408.0 %all-gather.20.cloned.1.call-start = ((), (), s32[]{:S(2)}) async-start(), calls=%async_computation.12 | async-start | bytes 17825792 | tf_op jit(solution)/shard_map/all_gather | solution.py:163
  292.6 598.6 %all-gather.24.cloned.1.call-start = ((), (), s32[]{:S(2)}) async-start(), calls=%async_computation.14 | async-start | bytes 17825792 | tf_op jit(solution)/shard_map/all_gather | solution.py:165
  293.8 689.1 %all-reduce.10.cloned.1.call-start = ((), (), s32[]{:S(2)}) async-start(), calls=%async_computation.15 | async-start | bytes 2097152 | tf_op jit(solution)/shard_map/psum | solution.py:192
  903.7 13.1 copy-start.12
  903.7 13.1 copy-start.13
  942.6 12.6 copy-start.9
  955.1 83.5 %reduce-scatter.8.cloned.1.call-start = ((), (), s32[]{:S(2)}) async-start(), calls=%async_computation.16 | async-start | bytes 655360 | tf_op jit(solution)/shard_map/reduce_scatter | solution.py:237
  990.1 15.6 slice-start
  990.1 15.6 slice-start.1
  990.1 15.6 slice-start.2
  990.1 15.6 slice-start.3
  1005.7 8.2 copy-start.6
  1019.9 41.0 %reduce-scatter.10.cloned.1.call-start = ((), (), s32[]{:S(2)}) async-start(), calls=%async_computation.17 | async-start | bytes 655360 | tf_op jit(solution)/shard_map/reduce_scatter | solution.py:240
  1030.6 120.8 %all-reduce.12.cloned.1.call-start = ((), (), s32[]{:S(2)}) async-start(), calls=%async_computation.23 | async-start | bytes 4194304 | tf_op jit(solution)/shard_map/psum | solution.py:173
  1033.5 8.1 copy-start.20
  1064.4 2111.4 %reduce-scatter.20.cloned.1.call-start = ((), (), s32[]{:S(2)}) async-start(), calls=%async_computation.22 | async-start | bytes 106954752 | tf_op jit(solution)/shard_map/reduce_scatter | solution.py:205
  1130.7 2122.1 %reduce-scatter.16.cloned.1.call-start = ((), (), s32[]{:S(2)}) async-start(), calls=%async_computation.20 | async-start | bytes 2228224 | tf_op jit(solution)/shard_map/reduce_scatter | solution.py:266
  1133.9 2202.3 %reduce-scatter.14.cloned.1.call-start = ((), (), s32[]{:S(2)}) async-start(), calls=%async_computation.19 | async-start | bytes 2228224 | tf_op jit(solution)/shard_map/reduce_scatter | solution.py:265
  1135.9 2392.6 %reduce-scatter.18.cloned.1.call-start = ((), (), s32[]{:S(2)}) async-start(), calls=%async_computation.21 | async-start | bytes 8912896 | tf_op jit(solution)/shard_map/reduce_scatter | solution.py:267
  1142.3 2568.9 %reduce-scatter.12.cloned.1.call-start = ((), (), s32[]{:S(2)}) async-start(), calls=%async_computation.18 | async-start | bytes 8912896 | tf_op jit(solution)/shard_map/reduce_scatter | solution.py:264
  1149.5 77.8 %copy-start.28 = (f32[256]{0:T(256)S(1)}, f32[256]{0:T(256)}, u32[]{:S(2)}) copy-start(f32[256]{0:T(256)} %get-tuple-element.96) | copy-start | bytes 3076
  (23 other events, 59.3 us)
Sparse Core Ops, SparseCore 0:
  11.3 56.1 all-gather.13
  70.9 54.1 all-gather.11
  128.4 75.9 all-gather.15
  207.6 74.5 all-gather.17
  287.1 21.3 all-reduce.7
  312.1 192.0 all-gather.21
  507.8 189.7 all-gather.19
  701.4 189.7 all-gather.23
  955.3 18.5 all-reduce.9
  1020.1 18.5 reduce-scatter.7
  1040.9 19.9 reduce-scatter.9
  1064.5 21.6 all-reduce.11
  1130.8 2044.9 reduce-scatter.19
  3178.5 74.2 reduce-scatter.15
  3255.5 80.6 reduce-scatter.13
  3338.9 189.5 reduce-scatter.17
  3531.3 179.8 reduce-scatter.11
where the time goes:
time: 3720 us
  waiting for transfers between devices  3200 us (86%)
  matrix products  194 us (5%)
  blocking collectives  167 us (4%)
  other arithmetic  116 us (3%)
    reduce_scatter x1, waiting for transfers between devices, on_device(): lax.psum_scatter(jnp.concatenate([pair_part, down_part[:, None, :]], axis...  1940 us
    reduce_scatter x1, waiting for transfers between devices, on_device(): lax.psum_scatter(o_part, ('fsdp', 'context'), scatter_dimension=0, tiled=...  192 us
    all_gather x1, waiting for transfers between devices, on_device(): lax.all_gather(gate_weight.astype(jnp.bfloat16), ('fsdp', 'context'), axi...  183 us
    all_gather x1, waiting for transfers between devices, on_device(): lax.all_gather(down_weight.astype(jnp.bfloat16), ('fsdp', 'context'), axi...  183 us
    reduce_scatter x1, waiting for transfers between devices, on_device(): lax.psum_scatter(q_part, ('fsdp', 'context'), scatter_dimension=0, tiled=...  183 us
    all_gather x1, waiting for transfers between devices, on_device(): lax.all_gather(up_weight.astype(jnp.bfloat16), ('fsdp', 'context'), axis=...  176 us
    reduce_scatter x1, waiting for transfers between devices, on_device(): lax.psum_scatter(k_part, ('fsdp', 'context'), scatter_dimension=0, tiled=...  83.4 us
  transfers between devices with their start and end apart: 17, of which 14 were waited for; matrix products, arithmetic and copies ran while one was open for 6% of the time, Pallas kernels for 0%

commit v1 on v0

v1 whole, which is shorter than its diff:
```python
import math

import jax
import jax.numpy as jnp
from jax import lax
from jax.sharding import PartitionSpec as P

HEADS = 32
KV_HEADS = 8
HEAD_DIM = 64
GROUP = HEADS // KV_HEADS
EPS = 1e-05
LOW = jnp.bfloat16
WIDE = jnp.float32


def rope_tables(positions, head_dim):
    half_dim = head_dim // 2
    freq_index = jnp.arange(half_dim, dtype=WIDE)
    base_freq = 1.0 / jnp.power(500000.0, 2.0 * freq_index / head_dim)
    wave_len = 2.0 * math.pi / base_freq
    mix_ratio = jnp.clip((8192.0 / wave_len - 1.0) / 3.0, 0.0, 1.0)
    scaled = (1.0 - mix_ratio) * base_freq / 32.0 + mix_ratio * base_freq
    angles = positions.astype(WIDE)[:, None] * scaled[None, :]
    angles = jnp.concatenate([angles, angles], axis=1)
    return (jnp.cos(angles), jnp.sin(angles))


def rotate(flat_in, cos_table, sin_table):
    shaped = flat_in.reshape(flat_in.shape[0], -1, HEAD_DIM)
    half_dim = HEAD_DIM // 2
    turned = jnp.concatenate([-shaped[..., half_dim:], shaped[..., :half_dim]], axis=-1)
    out = shaped * cos_table[:, None, :] + turned * sin_table[:, None, :]
    return out.reshape(flat_in.shape)


def matmul(left, right):
    return lax.dot_general(left, right, (((1,), (0,)), ((), ())), preferred_element_type=WIDE)


def matmul_t(left, right):
    return lax.dot_general(left, right, (((1,), (1,)), ((), ())), preferred_element_type=WIDE)


def outer(left, right):
    return lax.dot_general(left, right, (((0,), (0,)), ((), ())), preferred_element_type=WIDE)


def inverse_rms(hidden):
    return lax.rsqrt(jnp.mean(hidden * hidden, axis=-1, keepdims=True) + EPS)


def norm_reverse(hidden, inv_rms, gain_row, grad_in):
    weighted = grad_in * gain_row
    scale = jnp.mean(weighted * hidden, axis=-1, keepdims=True)
    return inv_rms * weighted - hidden * (inv_rms * inv_rms * inv_rms) * scale


class Groups:
    def __init__(self, mesh):
        self.n_f = mesh.shape["fsdp"]
        self.n_c = mesh.shape["context"]
        self.c = lax.axis_index("context")
        self.f = lax.axis_index("fsdp")
        self.t = lax.axis_index("tensor")

    def shift(self, block, axis, count, amount):
        return lax.ppermute(block, axis, [(i, (i + amount) % count) for i in range(count)])

    def swap(self, block):
        return lax.ppermute(block, "tensor", [(0, 1), (1, 0)])

    def along(self, blocks, index, count):
        return [lax.select_n(lax.rem(index - j + count, count), *blocks) for j in range(count)] if count > 1 else blocks

    def exchange(self, blocks):
        n = self.n_c
        got = []
        for k in range(n):
            mine = lax.dynamic_index_in_dim(blocks, lax.rem(self.c + k, n), 0, keepdims=False)
            got.append(mine if k == 0 else self.shift(mine, "context", n, k))
        return self.along(got, self.c, n)

    def gather_rows(self, mine):
        n = self.n_c
        steps = [mine] + [self.shift(mine, "context", n, k) for k in range(1, n)]
        near = jnp.concatenate(steps, axis=0)
        return jnp.concatenate([near, self.swap(near)], axis=0)

    def gather_copied(self, own_pair):
        n = self.n_c
        steps = [self.shift(own_pair[0], "context", n, k) for k in range(1, n)]
        near = jnp.concatenate(steps, axis=0)
        return jnp.concatenate([own_pair[0], near, own_pair[1], self.swap(near)], axis=0)

    def scatter_sum(self, near, far):
        n = self.n_c
        rows = near.shape[0] // n
        pair = near.astype(WIDE) + self.swap(far).astype(WIDE)
        total = pair[:rows]
        low = pair.astype(LOW)
        for k in range(1, n):
            got = self.shift(low[k * rows : (k + 1) * rows], "context", n, n - k)
            total = total + got.astype(WIDE)
        return total

    def both_halves(self, mine):
        other = self.swap(mine)
        first = self.t == 0
        return jnp.concatenate([jnp.where(first, mine, other), jnp.where(first, other, mine)], axis=0)


def attention(query, keys, values, allowed):
    rows = query.shape[0]
    kv = keys.shape[1] // HEAD_DIM
    grouped = query.reshape(rows, kv, -1, HEAD_DIM)
    key_heads = keys.reshape(rows, kv, HEAD_DIM)
    value_heads = values.reshape(rows, kv, HEAD_DIM)
    logits = jnp.einsum("ikgd,jkd->kgij", grouped, key_heads, preferred_element_type=WIDE)
    logits = jnp.where(allowed, logits * HEAD_DIM ** (-0.5), -1e30)
    row_max = jnp.max(logits, axis=-1, keepdims=True)
    exp_scores = jnp.exp(logits - row_max)
    row_total = jnp.sum(exp_scores, axis=-1, keepdims=True)
    probs_low = (exp_scores / row_total).astype(LOW)
    mixed = jnp.einsum("kgij,jkd->ikgd", probs_low, value_heads, preferred_element_type=WIDE)
    return mixed.reshape(rows, -1).astype(LOW), row_max + jnp.log(row_total)


def attention_reverse(query, keys, values, allowed, log_total, grad_out):
    rows = query.shape[0]
    kv = keys.shape[1] // HEAD_DIM
    grouped = query.reshape(rows, kv, -1, HEAD_DIM)
    grad_heads = grad_out.reshape(grouped.shape)
    key_heads = keys.reshape(rows, kv, HEAD_DIM)
    value_heads = values.reshape(rows, kv, HEAD_DIM)
    logits = jnp.einsum("ikgd,jkd->kgij", grouped, key_heads, preferred_element_type=WIDE)
    logits = jnp.where(allowed, logits * HEAD_DIM ** (-0.5), -1e30)
    probs = jnp.exp(logits - log_total)
    value_grad = jnp.einsum("kgij,ikgd->jkd", probs.astype(LOW), grad_heads, preferred_element_type=WIDE)
    grad_probs = jnp.einsum("ikgd,jkd->kgij", grad_heads, value_heads, preferred_element_type=WIDE)
    delta = jnp.sum(probs * grad_probs, axis=-1, keepdims=True)
    grad_scores = (probs * (grad_probs - delta)).astype(LOW)
    scale = HEAD_DIM ** (-0.5)
    query_grad = jnp.einsum("kgij,jkd->ikgd", grad_scores, key_heads, preferred_element_type=WIDE) * scale
    key_grad = jnp.einsum("kgij,ikgd->jkd", grad_scores, grouped, preferred_element_type=WIDE) * scale
    return (
        query_grad.reshape(rows, -1),
        key_grad.reshape(rows, -1),
        value_grad.reshape(rows, -1),
    )


def by_dest(weight, count):
    rows, columns = weight.shape
    return weight.astype(LOW).reshape(rows, count, columns // count).transpose(1, 0, 2)


def kv_by_dest(weight, count):
    rows, columns = weight.shape
    heads = columns // HEAD_DIM
    if count <= heads:
        return by_dest(weight, count)
    return jnp.repeat(by_dest(weight, heads), count // heads, axis=0)


def make_layer(mesh):
    def on_device(
        layer_input,
        prefix,
        attn_gain,
        q_weight,
        k_weight,
        v_weight,
        output_weight,
        mlp_gain,
        gate_weight,
        up_weight,
        down_weight,
        cotangent,
    ):
        g = Groups(mesh)
        n_c, n_f = g.n_c, g.n_f
        x_own = layer_input[0]
        cot_own = cotangent[0]
        local, width = x_own.shape
        half = local // 2
        rows = q_weight.shape[0]

        def halves(own):
            return (
                lax.dynamic_slice_in_dim(own, g.t * half, half, 0),
                lax.dynamic_slice_in_dim(own, (1 - g.t) * half, half, 0),
            )

        x_pair = halves(x_own)
        cot_pair = halves(cot_own)
        x_all = g.gather_copied(x_pair)

        gains = jnp.stack([attn_gain, mlp_gain]).astype(LOW)
        gain_steps = [gains] + [g.shift(gains, "context", n_c, k) for k in range(1, n_c)]
        gains_c = jnp.concatenate(g.along(gain_steps, g.c, n_c), axis=1)
        gain_steps = [gains_c] + [g.shift(gains_c, "fsdp", n_f, k) for k in range(1, n_f)]
        gains_all = jnp.concatenate(g.along(gain_steps, g.f, n_f), axis=1).astype(WIDE)
        gain_one, gain_two = gains_all[0:1], gains_all[1:2]

        def gather_weight(blocks):
            mine = jnp.concatenate(g.exchange(blocks), axis=0)
            return lax.all_gather(mine, "fsdp", axis=0, tiled=True)

        q_cols = q_weight.shape[1] // n_c
        kv_blocks = kv_by_dest(k_weight, n_c), kv_by_dest(v_weight, n_c)
        kv_cols = kv_blocks[0].shape[2]
        qkv_full = gather_weight(jnp.concatenate([by_dest(q_weight, n_c), *kv_blocks], axis=2))
        o_full = gather_weight(by_dest(output_weight, n_c))
        gu_full = gather_weight(jnp.concatenate([by_dest(gate_weight, n_c), by_dest(up_weight, n_c)], axis=2))
        down_full = gather_weight(by_dest(down_weight, n_c))
        cot_all = g.gather_copied(cot_pair)

        step = jnp.arange(n_c, dtype=jnp.int32)
        block = lax.rem(g.c - step + n_c, n_c) * local
        side = jnp.stack([g.t, 1 - g.t]).astype(jnp.int32) * half
        positions = (
            side[:, None, None] + block[None, :, None] + jnp.arange(half, dtype=jnp.int32)[None, None, :]
        ).reshape(-1)
        cos_table, sin_table = rope_tables(positions, HEAD_DIM)
        allowed = (positions[None, :] <= positions[:, None]) | (positions[None, :] < prefix[0])

        hidden_in = x_all.astype(WIDE)
        rms_one = inverse_rms(hidden_in)
        normed_one = (hidden_in * rms_one * gain_one).astype(LOW)
        qkv = matmul(normed_one, qkv_full)
        query_rot = rotate(qkv[:, :q_cols], cos_table, sin_table).astype(LOW)
        key_rot = rotate(qkv[:, q_cols : q_cols + kv_cols], cos_table, sin_table).astype(LOW)
        value_low = qkv[:, q_cols + kv_cols :].astype(LOW)
        attended, log_total = attention(query_rot, key_rot, value_low, allowed)

        near_rows = n_c * half
        far_part = matmul_t(attended[near_rows:], o_full).astype(LOW)
        near_part = matmul_t(attended[:near_rows], o_full)
        x_mine = x_pair[0].astype(WIDE)
        resid = x_mine + g.scatter_sum(near_part, far_part)
        rms_two = inverse_rms(resid)
        normed_two = g.gather_rows((resid * rms_two * gain_two).astype(LOW))

        gate_up = matmul(normed_two, gu_full)
        hid = gate_up.shape[1] // 2
        gate_proj, up_proj = gate_up[:, :hid], gate_up[:, hid:]
        squash = jax.nn.sigmoid(gate_proj)
        inner = (gate_proj * squash * up_proj).astype(LOW)
        grad_inner = matmul(cot_all, down_full)
        grad_gate = grad_inner * up_proj * squash * (1.0 + gate_proj * (1.0 - squash))
        grad_up = grad_inner * gate_proj * squash
        grad_gu = jnp.concatenate([grad_gate.astype(LOW), grad_up.astype(LOW)], axis=1)
        far_grad = matmul_t(grad_gu[near_rows:], gu_full).astype(LOW)
        near_grad = matmul_t(grad_gu[:near_rows], gu_full)
        grad_normed_two = g.scatter_sum(near_grad, far_grad)
        cot_mine = cot_pair[0].astype(WIDE)
        grad_resid = cot_mine + norm_reverse(resid, rms_two, gain_two, grad_normed_two)
        branch_all = g.gather_rows(grad_resid.astype(LOW))

        far_out = matmul_t(inner[near_rows:], down_full).astype(LOW)
        near_out = matmul_t(inner[:near_rows], down_full)
        layer_output = g.both_halves((resid + g.scatter_sum(near_out, far_out)).astype(LOW))

        def return_weight(part):
            mine = lax.psum_scatter(part.astype(LOW), "fsdp", scatter_dimension=0, tiled=True)
            return g.exchange(mine.reshape(n_c, rows, part.shape[1]))

        gu_blocks = return_weight(outer(normed_two, grad_gu))
        down_blocks = return_weight(outer(cot_all, inner))

        def cols(blocks, start, size):
            return jnp.concatenate([b[:, start : start + size] for b in blocks], axis=1).astype(WIDE)

        gate_grad = cols(gu_blocks, 0, hid)
        up_grad = cols(gu_blocks, hid, hid)
        down_grad = cols(down_blocks, 0, hid)

        grad_att = matmul(branch_all, o_full).astype(LOW)
        o_blocks = return_weight(outer(branch_all, attended))
        o_grad = cols(o_blocks, 0, q_cols)
        q_grad_rot, k_grad_rot, value_grad = attention_reverse(
            query_rot, key_rot, value_low, allowed, log_total, grad_att
        )
        grad_qkv = jnp.concatenate(
            [
                rotate(q_grad_rot, cos_table, -sin_table).astype(LOW),
                rotate(k_grad_rot, cos_table, -sin_table).astype(LOW),
                value_grad.astype(LOW),
            ],
            axis=1,
        )
        far_one = matmul_t(grad_qkv[near_rows:], qkv_full).astype(LOW)
        near_one = matmul_t(grad_qkv[:near_rows], qkv_full)
        grad_normed_one = g.scatter_sum(near_one, far_one)
        qkv_blocks = return_weight(outer(normed_one, grad_qkv))
        q_grad = cols(qkv_blocks, 0, q_cols)

        def kv_grad(start):
            parts = [b[:, start : start + kv_cols].astype(WIDE) for b in qkv_blocks]
            copies = n_c * kv_cols // k_weight.shape[1]
            return jnp.concatenate([sum(parts[j : j + copies]) for j in range(0, n_c, copies)], axis=1)

        k_grad = kv_grad(q_cols)
        v_grad = kv_grad(q_cols + kv_cols)
        rms_mine = inverse_rms(x_mine)
        grad_in = grad_resid + norm_reverse(x_mine, rms_mine, gain_one, grad_normed_one)
        input_grad = g.both_halves(grad_in.astype(LOW))

        def gain_grad(gain, pairs):
            total = sum(jnp.sum(grad * weight.astype(LOW).astype(WIDE), axis=1) for grad, weight in pairs)
            return (total + g.swap(total)) / gain.astype(LOW).astype(WIDE)

        attn_gain_grad = gain_grad(attn_gain, [(q_grad, q_weight), (k_grad, k_weight), (v_grad, v_weight)])
        mlp_gain_grad = gain_grad(mlp_gain, [(gate_grad, gate_weight), (up_grad, up_weight)])
        return (
            layer_output[None],
            input_grad[None],
            attn_gain_grad,
            q_grad,
            k_grad,
            v_grad,
            o_grad,
            mlp_gain_grad,
            gate_grad,
            up_grad,
            down_grad,
        )

    return on_device


def solution(mesh):
    tokens = P("fsdp", "context", None)
    gain = P(("fsdp", "context"))
    weight = P(("fsdp", "context"), "tensor")
    return jax.shard_map(
        make_layer(mesh),
        mesh=mesh,
        in_specs=(tokens, P("fsdp"), gain, weight, weight, weight, weight, gain, weight, weight, weight, tokens),
        out_specs=(tokens, tokens, gain, weight, weight, weight, weight, gain, weight, weight, weight),
        check_vma=False,
    )
```

time: 3720 us -> 873 us (0.23)
  waiting for transfers between devices: 3200 us -> 458 us
  blocking collectives: 167 us -> 0 us
  starting transfers between devices: 0.96 us -> 122 us
  matrix products: 194 us -> 145 us
  other arithmetic: 116 us -> 70 us
    reduce_scatter x7 -> x4, waiting for transfers between devices: 2490 us -> 78.5 us  [return_weight(): lax.psum_scatter(part.astype(LOW), 'fsdp', scatter_dimension=0, tiled=True)]
    all_gather x7 -> x4, waiting for transfers between devices: 705 us -> 0.04 us  [gather_weight(): return lax.all_gather(mine, 'fsdp', axis=0, tiled=True)]
    ppermute x0 -> x66, waiting for transfers between devices: none -> 379 us  [the longest x54 371 us: shift(): lax.ppermute(block, axis, [(i, (i + amount) % count) for i in range(count)])]
    ppermute x0 -> x66, starting transfers between devices: none -> 122 us  [the longest x54 110 us: shift(): lax.ppermute(block, axis, [(i, (i + amount) % count) for i in range(count)])]
    all_gather x4 -> x0, blocking collectives: 93.8 us -> none  [the longest x1 34.4 us: on_device(): lax.all_gather(attn_gain.astype(jnp.bfloat16), ('fsdp', 'context'), axis=...]
    unnamed x1 -> x0, blocking collectives: 72.9 us -> none
    concatenate x5 -> x15, other arithmetic: 67.8 us -> 7.18 us  [the longest x4 4.12 us: gather_weight(): mine = jnp.concatenate(g.exchange(blocks), axis=0)]
    dot_general x27 -> x22, matrix products: 194 us -> 145 us  [the longest x8 40.6 us: matmul_t(): lax.dot_general(left, right, (((1,), (1,)), ((), ())), preferred_element_...]
  transfers between devices with their start and end apart: 17 -> 74, of which waited for: 14 -> 28; matrix products, arithmetic and copies ran while one was open for 6% -> 23% of each run, Pallas kernels for 0% -> 0%
where the time goes in v1:
time: 873 us; the launch traced here: 864 us
  waiting for transfers between devices  458 us (52%)
  matrix products  145 us (17%)
  starting transfers between devices  122 us (14%)
  other arithmetic  70 us (8%)
  local copies, waits for them, and re-layouts  52.6 us (6%)
  between operations  16.6 us (2%)
    ppermute x54, waiting for transfers between devices, shift(): lax.ppermute(block, axis, [(i, (i + amount) % count) for i in range(count)])  371 us
    ppermute x54, starting transfers between devices, shift(): lax.ppermute(block, axis, [(i, (i + amount) % count) for i in range(count)])  110 us
    reduce_scatter x4, waiting for transfers between devices, return_weight(): lax.psum_scatter(part.astype(LOW), 'fsdp', scatter_dimension=0, tiled=True)  78.5 us
    dot_general x8, matrix products, matmul_t(): lax.dot_general(left, right, (((1,), (1,)), ((), ())), preferred_element_...  40.6 us
    dot_general x4, matrix products, matmul(): lax.dot_general(left, right, (((1,), (0,)), ((), ())), preferred_element_...  34.4 us
    unnamed x140, local copies, waits for them, and re-layouts  31.3 us
    dot_general x4, matrix products, outer(): lax.dot_general(left, right, (((0,), (0,)), ((), ())), preferred_element_...  29.7 us
  transfers between devices with their start and end apart: 74, of which 28 were waited for; matrix products, arithmetic and copies ran while one was open for 23% of the time, Pallas kernels for 0%

profile of v1, /device:TPU:1, one launch (start us, length us, event | category | flops | bytes accessed | tf_op | source)
XLA Modules:
  0.0 864.3 jit_solution(9038102085584383436)
XLA Ops:
  52.8 26.2 %collective-permute-done.4 = bf16[2,128]{1,0:T(2,128)(2,1)S(1)} collective-permute-done((bf16[2,128]{1,0:T(2,128)(2,1)S(1)}, bf16[2,128]{1,0:T(2,128)(2,1)S(1)}, u32[]{:S(2)}, u32[]{:S(2)}) %collective-permute-start.4) | collective-permute-done | bytes 544 | tf_op jit(solution)/shard_map/ppermute | solution.py:68
  78.9 20.4 %collective-permute-start.1 = (bf16[128,2048]{1,0:T(8,128)(2,1)S(1)}, bf16[128,2048]{1,0:T(8,128)(2,1)}, u32[]{:S(2)}, u32[]{:S(2)}) collective-permute-start(bf16[128,2048]{1,0:T(8,128)(2,1)S(1)} %get-tuple-element.46), channel_id=1, source_target_pairs={{0,4},{2,6},{4,0},{6,2},{1,5},{3,7},{5,1},{7,3},{8,12},{10,14},{12... | collective-permute-start | bytes 1572872 | tf_op jit(solution)/shard_map/ppermute | solution.py:68
  110.5 27.3 %collective-permute-done.1 = bf16[128,2048]{1,0:T(8,128)(2,1)} collective-permute-done((bf16[128,2048]{1,0:T(8,128)(2,1)S(1)}, bf16[128,2048]{1,0:T(8,128)(2,1)}, u32[]{:S(2)}, u32[]{:S(2)}) %collective-permute-start.1) | collective-permute-done | bytes 524320 | tf_op jit(solution)/shard_map/ppermute | solution.py:68
  157.9 8.1 fusion.136
  166.0 8.0 fusion.3
  174.0 7.4 fusion.22
  192.3 12.7 %collective-permute-done.29 = bf16[128,1024]{1,0:T(8,128)(2,1)S(1)} collective-permute-done((bf16[128,1024]{1,0:T(8,128)(2,1)S(1)}, bf16[128,1024]{1,0:T(8,128)(2,1)S(1)}, u32[]{:S(2)}, u32[]{:S(2)}) %collective-permute-start.29) | collective-permute-done | bytes 262176 | tf_op jit(solution)/shard_map/ppermute | solution.py:68
  205.0 8.2 collective-permute-done.28
  234.4 12.2 %collective-permute-done.19 = bf16[128,2048]{1,0:T(8,128)(2,1)} collective-permute-done((bf16[128,2048]{1,0:T(8,128)(2,1)}, bf16[128,2048]{1,0:T(8,128)(2,1)}, u32[]{:S(2)}, u32[]{:S(2)}) %collective-permute-start.19) | collective-permute-done | bytes 524320 | tf_op jit(solution)/shard_map/ppermute | solution.py:68
  246.6 20.6 %collective-permute-done.18 = bf16[128,2048]{1,0:T(8,128)(2,1)} collective-permute-done((bf16[128,2048]{1,0:T(8,128)(2,1)}, bf16[128,2048]{1,0:T(8,128)(2,1)}, u32[]{:S(2)}, u32[]{:S(2)}) %collective-permute-start.18) | collective-permute-done | bytes 524320 | tf_op jit(solution)/shard_map/ppermute | solution.py:68
  270.1 24.5 %collective-permute-start.22 = (bf16[128,2048]{1,0:T(8,128)(2,1)S(1)}, bf16[128,2048]{1,0:T(8,128)(2,1)S(1)}, u32[]{:S(2)}, u32[]{:S(2)}) collective-permute-start(bf16[128,2048]{1,0:T(8,128)(2,1)S(1)} %get-tuple-element.36), channel_id=1, source_target_pairs={{0,6},{2,0},{4,2},{6,4},{1,7},{3,1},{5,3},{7,5},{8,14},{10,8},{12,... | collective-permute-start | bytes 1572872 | tf_op jit(solution)/shard_map/ppermute | solution.py:68
  301.0 33.5 %collective-permute-done.36 = bf16[128,2048]{1,0:T(8,128)(2,1)S(1)} collective-permute-done((bf16[128,2048]{1,0:T(8,128)(2,1)S(1)}, bf16[128,2048]{1,0:T(8,128)(2,1)S(1)}, u32[]{:S(2)}, u32[]{:S(2)}) %collective-permute-start.36) | collective-permute-done | bytes 524320 | tf_op jit(solution)/shard_map/ppermute | solution.py:68
  337.0 20.0 %collective-permute-done.21 = bf16[128,2048]{1,0:T(8,128)(2,1)S(1)} collective-permute-done((bf16[128,2048]{1,0:T(8,128)(2,1)S(1)}, bf16[128,2048]{1,0:T(8,128)(2,1)S(1)}, u32[]{:S(2)}, u32[]{:S(2)}) %collective-permute-start.21) | collective-permute-done | bytes 524320 | tf_op jit(solution)/shard_map/ppermute | solution.py:68
  363.9 14.6 %fusion.140 = f32[1024,2048]{1,0:T(8,128)} fusion(bf16[1024,2048]{1,0:T(8,128)(2,1)} %constant_dynamic-update-slice_fusion.5, bf16[2048,2048]{1,0:T(8,128)(2,1)} %all-gather.9.cloned.1.call-done), kind=kOutput, calls=%fused_computation.352 | convolution fusion | flops 8589934592 | bytes 20971520 | tf_op jit(solution)/shard_map/dot_general | solution.py:38
  378.5 14.0 %multiply_convert_fusion = (bf16[1024,1024]{1,0:T(8,128)(2,1)}, bf16[1024,1024]{1,0:T(8,128)(2,1)}, bf16[1024,1024]{1,0:T(8,128)(2,1)S(1)}) fusion(f32[1024,2048]{1,0:T(8,128)} %fusion.140, bf16[1024,2048]{1,0:T(8,128)(2,1)} %copy-done.41, bf16[2048,1024]{1,0:T(8,128)(2,1)} %all-gather.11.cloned.1.call-done), kind=kOutput, calls=%fused_computation.30 | convolution fusion | flops 4311744512 | bytes 23068672 | tf_op jit(solution)/shard_map/dot_general | solution.py:38
  396.6 7.7 convolution_convert_fusion.5
  412.8 9.2 %fusion.137 = (bf16[512,2048]{1,0:T(8,128)(2,1)S(1)}, f32[512,2048]{1,0:T(8,128)S(1)}) fusion(bf16[512,2048]{1,0:T(8,128)(2,1)} %collective-permute-done.39, bf16[2048,2048]{1,0:T(8,128)(2,1)} %all-gather.9.cloned.1.call-done, bf16[1024,1024]{1,0:T(8,128)(2,1)} %get-tuple-element.48, bf16[1024,1024]{1,0:T(8,128)(2,1)} %get-tuple-element.47), kind=kOutput, calls=%fused_computation.349 | convolution fusion | flops 4302307328 | bytes 20971520 | tf_op jit(solution)/shard_map/dot_general | solution.py:42
  424.7 11.0 %collective-permute-done.33 = bf16[128,2048]{1,0:T(8,128)(2,1)S(1)} collective-permute-done((bf16[128,2048]{1,0:T(8,128)(2,1)S(1)}, bf16[128,2048]{1,0:T(8,128)(2,1)S(1)}, u32[]{:S(2)}, u32[]{:S(2)}) %collective-permute-start.33) | collective-permute-done | bytes 524320 | tf_op jit(solution)/shard_map/ppermute | solution.py:68
  435.7 21.5 %collective-permute-done.32 = bf16[128,2048]{1,0:T(8,128)(2,1)S(1)} collective-permute-done((bf16[128,2048]{1,0:T(8,128)(2,1)S(1)}, bf16[128,2048]{1,0:T(8,128)(2,1)S(1)}, u32[]{:S(2)}, u32[]{:S(2)}) %collective-permute-start.32) | collective-permute-done | bytes 524320 | tf_op jit(solution)/shard_map/ppermute | solution.py:68
  457.2 12.3 %collective-permute-done.42 = bf16[128,2048]{1,0:T(8,128)(2,1)S(1)} collective-permute-done((bf16[128,2048]{1,0:T(8,128)(2,1)S(1)}, bf16[128,2048]{1,0:T(8,128)(2,1)S(1)}, u32[]{:S(2)}, u32[]{:S(2)}) %collective-permute-start.42) | collective-permute-done | bytes 524320 | tf_op jit(solution)/shard_map/ppermute | solution.py:68
  469.5 32.7 %collective-permute-done.41 = bf16[128,2048]{1,0:T(8,128)(2,1)S(1)} collective-permute-done((bf16[128,2048]{1,0:T(8,128)(2,1)S(1)}, bf16[128,2048]{1,0:T(8,128)(2,1)S(1)}, u32[]{:S(2)}, u32[]{:S(2)}) %collective-permute-start.41) | collective-permute-done | bytes 524320 | tf_op jit(solution)/shard_map/ppermute | solution.py:68
  506.7 11.2 %collective-permute-done.45 = bf16[128,2048]{1,0:T(8,128)(2,1)S(1)} collective-permute-done((bf16[128,2048]{1,0:T(8,128)(2,1)S(1)}, bf16[128,2048]{1,0:T(8,128)(2,1)S(1)}, u32[]{:S(2)}, u32[]{:S(2)}) %collective-permute-start.45) | collective-permute-done | bytes 524320 | tf_op jit(solution)/shard_map/ppermute | solution.py:68
  517.9 32.1 %collective-permute-done.44 = bf16[128,2048]{1,0:T(8,128)(2,1)S(1)} collective-permute-done((bf16[128,2048]{1,0:T(8,128)(2,1)S(1)}, bf16[128,2048]{1,0:T(8,128)(2,1)S(1)}, u32[]{:S(2)}, u32[]{:S(2)}) %collective-permute-start.44) | collective-permute-done | bytes 524320 | tf_op jit(solution)/shard_map/ppermute | solution.py:68
  559.5 8.6 fusion
  568.1 10.5 %fusion.11 = bf16[4,1024,1024]{1,2,0:T(8,128)(2,1)} fusion(f32[1024,1024,4]{1,0,2:T(8,128)} %get-tuple-element.178, f32[1,4,1024,1024]{2,3,1,0:T(8,128)S(1)} %bitcast.298, f32[4,1024]{1,0:T(4,128)S(1)} %get-tuple-element.177, f32[4,1024]{1,0:T(4,128)S(1)} %log_add_fusion), kind=kLoop, calls=%fused_computation.18 | loop fusion | flops 16777216 | bytes 41975808 | tf_op jit(solution)/shard_map/reshape.20
  592.0 8.6 fusion.36
  604.8 9.6 %convolution_convert_fusion.1 = bf16[2048,1024]{1,0:T(8,128)(2,1)} fusion(bf16[1024,2048]{1,0:T(8,128)(2,1)} %copy-done.41, bf16[1024,1024]{1,0:T(8,128)(2,1)} %copy-done.50), kind=kOutput, calls=%fused_computation.37 | convolution fusion | flops 4297064448 | bytes 10485760 | tf_op jit(solution)/shard_map/dot_general | solution.py:46
  615.9 13.8 %convolution_convert_fusion = bf16[2048,2048]{1,0:T(8,128)(2,1)} fusion(bf16[1024,2048]{1,0:T(8,128)(2,1)} %constant_dynamic-update-slice_fusion.5, bf16[1024,1024]{1,0:T(8,128)(2,1)S(1)} %copy-done.51, bf16[1024,1024]{1,0:T(8,128)(2,1)} %get-tuple-element.48), kind=kOutput, calls=%fused_computation.22 | convolution fusion | flops 8602517504 | bytes 16777216 | tf_op jit(solution)/shard_map/dot_general | solution.py:46
  662.0 11.9 %collective-permute-done.50 = bf16[128,2048]{1,0:T(8,128)(2,1)} collective-permute-done((bf16[128,2048]{1,0:T(8,128)(2,1)}, bf16[128,2048]{1,0:T(8,128)(2,1)}, u32[]{:S(2)}, u32[]{:S(2)}) %collective-permute-start.50) | collective-permute-done | bytes 524320 | tf_op jit(solution)/shard_map/ppermute | solution.py:68
  673.9 24.4 %collective-permute-done.49 = bf16[128,2048]{1,0:T(8,128)(2,1)} collective-permute-done((bf16[128,2048]{1,0:T(8,128)(2,1)}, bf16[128,2048]{1,0:T(8,128)(2,1)}, u32[]{:S(2)}, u32[]{:S(2)}) %collective-permute-start.49) | collective-permute-done | bytes 524320 | tf_op jit(solution)/shard_map/ppermute | solution.py:68
  720.0 78.5 %reduce-scatter.9.cloned.1.call-done = bf16[512,2048]{1,0:T(8,128)(2,1)} async-done(((bf16[2048,2048]{1,0:T(8,128)(2,1)}), bf16[512,2048]{1,0:T(8,128)(2,1)}) %reduce-scatter.9.cloned.1.call-update) | async-done | bytes 2097168 | tf_op jit(solution)/shard_map/reduce_scatter | solution.py:266
  814.8 33.5 %collective-permute-done.60 = bf16[128,2048]{1,0:T(8,128)(2,1)S(1)} collective-permute-done((bf16[128,2048]{1,0:T(8,128)(2,1)S(1)}, bf16[128,2048]{1,0:T(8,128)(2,1)S(1)}, u32[]{:S(2)}, u32[]{:S(2)}) %collective-permute-start.60) | collective-permute-done | bytes 524320 | tf_op jit(solution)/shard_map/ppermute | solution.py:68
  (416 shorter events, 253.2 us)
Async XLA Ops:
  7.2 143.6 %all-gather.5.cloned.1.call-start = ((), (), s32[]{:S(2)}) async-start(), calls=%async_computation.4 | async-start | bytes 1966080 | tf_op jit(solution)/shard_map/all_gather | solution.py:208
  31.5 150.8 %all-gather.7.cloned.1.call-start = ((), (), s32[]{:S(2)}) async-start(), calls=%async_computation.5 | async-start | bytes 1310720 | tf_op jit(solution)/shard_map/all_gather | solution.py:208
  43.1 56.3 %collective-permute-start.24 = (bf16[128,2048]{1,0:T(8,128)(2,1)}, bf16[128,2048]{1,0:T(8,128)(2,1)S(1)}, u32[]{:S(2)}, u32[]{:S(2)}) collective-permute-start(bf16[128,2048]{1,0:T(8,128)(2,1)} %get-tuple-element.69), channel_id=1, source_target_pairs={{0,2},{2,4},{4,6},{6,0},{1,3},{3,5},{5,7},{7,1},{8,10},{10,12},{12... | collective-permute-start | bytes 1572872 | tf_op jit(solution)/shard_map/ppermute | solution.py:68
  44.7 54.8 %collective-permute-start.25 = (bf16[128,2048]{1,0:T(8,128)(2,1)}, bf16[128,2048]{1,0:T(8,128)(2,1)}, u32[]{:S(2)}, u32[]{:S(2)}) collective-permute-start(bf16[128,2048]{1,0:T(8,128)(2,1)} %get-tuple-element.70), channel_id=1, source_target_pairs={{0,4},{2,6},{4,0},{6,2},{1,5},{3,7},{5,1},{7,3},{8,12},{10,14},{12... | collective-permute-start | bytes 1572872 | tf_op jit(solution)/shard_map/ppermute | solution.py:68
  44.7 56.1 %collective-permute-start.26 = (bf16[128,2048]{1,0:T(8,128)(2,1)}, bf16[128,2048]{1,0:T(8,128)(2,1)}, u32[]{:S(2)}, u32[]{:S(2)}) collective-permute-start(bf16[128,2048]{1,0:T(8,128)(2,1)} %get-tuple-element.71), channel_id=1, source_target_pairs={{0,6},{2,0},{4,2},{6,4},{1,7},{3,1},{5,3},{7,5},{8,14},{10,8},{12,... | collective-permute-start | bytes 1572872 | tf_op jit(solution)/shard_map/ppermute | solution.py:68
  49.4 314.5 %all-gather.9.cloned.1.call-start = ((), (), s32[]{:S(2)}) async-start(), calls=%async_computation.6 | async-start | bytes 10485760 | tf_op jit(solution)/shard_map/all_gather | solution.py:208
  49.5 61.0 %collective-permute-start.2 = (bf16[128,2048]{1,0:T(8,128)(2,1)S(1)}, bf16[128,2048]{1,0:T(8,128)(2,1)}, u32[]{:S(2)}, u32[]{:S(2)}) collective-permute-start(bf16[128,2048]{1,0:T(8,128)(2,1)S(1)} %get-tuple-element.46), channel_id=1, source_target_pairs={{0,6},{2,0},{4,2},{6,4},{1,7},{3,1},{5,3},{7,5},{8,14},{10,8},{12,... | collective-permute-start | bytes 1572872 | tf_op jit(solution)/shard_map/ppermute | solution.py:68
  78.9 58.9 %collective-permute-start.1 = (bf16[128,2048]{1,0:T(8,128)(2,1)S(1)}, bf16[128,2048]{1,0:T(8,128)(2,1)}, u32[]{:S(2)}, u32[]{:S(2)}) collective-permute-start(bf16[128,2048]{1,0:T(8,128)(2,1)S(1)} %get-tuple-element.46), channel_id=1, source_target_pairs={{0,4},{2,6},{4,0},{6,2},{1,5},{3,7},{5,1},{7,3},{8,12},{10,14},{12... | collective-permute-start | bytes 1572872 | tf_op jit(solution)/shard_map/ppermute | solution.py:68
  105.2 273.3 %all-gather.11.cloned.1.call-start = ((), (), s32[]{:S(2)}) async-start(), calls=%async_computation.7 | async-start | bytes 5242880 | tf_op jit(solution)/shard_map/all_gather | solution.py:208
  223.2 44.0 %collective-permute-start.18 = (bf16[128,2048]{1,0:T(8,128)(2,1)}, bf16[128,2048]{1,0:T(8,128)(2,1)}, u32[]{:S(2)}, u32[]{:S(2)}) collective-permute-start(bf16[128,2048]{1,0:T(8,128)(2,1)} %get-tuple-element.74), channel_id=1, source_target_pairs={{0,4},{2,6},{4,0},{6,2},{1,5},{3,7},{5,1},{7,3},{8,12},{10,14},{12... | collective-permute-start | bytes 1572872 | tf_op jit(solution)/shard_map/ppermute | solution.py:68
  224.6 426.4 %reduce-scatter.7.cloned.1.call-start = ((), (), s32[]{:S(2)}) async-start(), calls=%async_computation.9 | async-start | bytes 1310720 | tf_op jit(solution)/shard_map/reduce_scatter | solution.py:266
  225.0 69.7 %collective-permute-start.37 = (bf16[128,2048]{1,0:T(8,128)(2,1)S(1)}, bf16[128,2048]{1,0:T(8,128)(2,1)S(1)}, u32[]{:S(2)}, u32[]{:S(2)}) collective-permute-start(bf16[128,2048]{1,0:T(8,128)(2,1)S(1)} %get-tuple-element.32), channel_id=1, source_target_pairs={{0,6},{2,0},{4,2},{6,4},{1,7},{3,1},{5,3},{7,5},{8,14},{10,8},{12,... | collective-permute-start | bytes 1572872 | tf_op jit(solution)/shard_map/ppermute | solution.py:68
  228.0 106.5 %collective-permute-start.36 = (bf16[128,2048]{1,0:T(8,128)(2,1)S(1)}, bf16[128,2048]{1,0:T(8,128)(2,1)S(1)}, u32[]{:S(2)}, u32[]{:S(2)}) collective-permute-start(bf16[128,2048]{1,0:T(8,128)(2,1)S(1)} %get-tuple-element.32), channel_id=1, source_target_pairs={{0,4},{2,6},{4,0},{6,2},{1,5},{3,7},{5,1},{7,3},{8,12},{10,14},{12... | collective-permute-start | bytes 1572872 | tf_op jit(solution)/shard_map/ppermute | solution.py:68
  234.4 100.2 %collective-permute-start.35 = (bf16[128,2048]{1,0:T(8,128)(2,1)S(1)}, bf16[128,2048]{1,0:T(8,128)(2,1)S(1)}, u32[]{:S(2)}, u32[]{:S(2)}) collective-permute-start(bf16[128,2048]{1,0:T(8,128)(2,1)S(1)} %get-tuple-element.32), channel_id=1, source_target_pairs={{0,2},{2,4},{4,6},{6,0},{1,3},{3,5},{5,7},{7,1},{8,10},{10,12},{12... | collective-permute-start | bytes 1572872 | tf_op jit(solution)/shard_map/ppermute | solution.py:68
  270.1 66.9 %collective-permute-start.22 = (bf16[128,2048]{1,0:T(8,128)(2,1)S(1)}, bf16[128,2048]{1,0:T(8,128)(2,1)S(1)}, u32[]{:S(2)}, u32[]{:S(2)}) collective-permute-start(bf16[128,2048]{1,0:T(8,128)(2,1)S(1)} %get-tuple-element.36), channel_id=1, source_target_pairs={{0,6},{2,0},{4,2},{6,4},{1,7},{3,1},{5,3},{7,5},{8,14},{10,8},{12,... | collective-permute-start | bytes 1572872 | tf_op jit(solution)/shard_map/ppermute | solution.py:68
  294.7 62.3 %collective-permute-start.21 = (bf16[128,2048]{1,0:T(8,128)(2,1)S(1)}, bf16[128,2048]{1,0:T(8,128)(2,1)S(1)}, u32[]{:S(2)}, u32[]{:S(2)}) collective-permute-start(bf16[128,2048]{1,0:T(8,128)(2,1)S(1)} %get-tuple-element.36), channel_id=1, source_target_pairs={{0,4},{2,6},{4,0},{6,2},{1,5},{3,7},{5,1},{7,3},{8,12},{10,14},{12... | collective-permute-start | bytes 1572872 | tf_op jit(solution)/shard_map/ppermute | solution.py:68
  294.7 62.3 %collective-permute-start.20 = (bf16[128,2048]{1,0:T(8,128)(2,1)S(1)}, bf16[128,2048]{1,0:T(8,128)(2,1)S(1)}, u32[]{:S(2)}, u32[]{:S(2)}) collective-permute-start(bf16[128,2048]{1,0:T(8,128)(2,1)S(1)} %get-tuple-element.36), channel_id=1, source_target_pairs={{0,2},{2,4},{4,6},{6,0},{1,3},{3,5},{5,7},{7,1},{8,10},{10,12},{12... | collective-permute-start | bytes 1572872 | tf_op jit(solution)/shard_map/ppermute | solution.py:68
  411.3 45.9 %collective-permute-start.32 = (bf16[128,2048]{1,0:T(8,128)(2,1)S(1)}, bf16[128,2048]{1,0:T(8,128)(2,1)S(1)}, u32[]{:S(2)}, u32[]{:S(2)}) collective-permute-start(bf16[128,2048]{1,0:T(8,128)(2,1)S(1)} %get-tuple-element.65), channel_id=1, source_target_pairs={{0,4},{2,6},{4,0},{6,2},{1,5},{3,7},{5,1},{7,3},{8,12},{10,14},{12... | collective-permute-start | bytes 1572872 | tf_op jit(solution)/shard_map/ppermute | solution.py:68
  423.1 46.3 %collective-permute-start.42 = (bf16[128,2048]{1,0:T(8,128)(2,1)S(1)}, bf16[128,2048]{1,0:T(8,128)(2,1)S(1)}, u32[]{:S(2)}, u32[]{:S(2)}) collective-permute-start(bf16[128,2048]{1,0:T(8,128)(2,1)S(1)} %get-tuple-element.61), channel_id=1, source_target_pairs={{0,2},{2,4},{4,6},{6,0},{1,3},{3,5},{5,7},{7,1},{8,10},{10,12},{12... | collective-permute-start | bytes 1572872 | tf_op jit(solution)/shard_map/ppermute | solution.py:68
  423.6 78.5 %collective-permute-start.41 = (bf16[128,2048]{1,0:T(8,128)(2,1)S(1)}, bf16[128,2048]{1,0:T(8,128)(2,1)S(1)}, u32[]{:S(2)}, u32[]{:S(2)}) collective-permute-start(bf16[128,2048]{1,0:T(8,128)(2,1)S(1)} %get-tuple-element.62), channel_id=1, source_target_pairs={{0,4},{2,6},{4,0},{6,2},{1,5},{3,7},{5,1},{7,3},{8,12},{10,14},{12... | collective-permute-start | bytes 1572872 | tf_op jit(solution)/shard_map/ppermute | solution.py:68
  589.5 117.2 %reduce-scatter.5.cloned.1.call-start = ((), (), s32[]{:S(2)}) async-start(), calls=%async_computation.8 | async-start | bytes 1966080 | tf_op jit(solution)/shard_map/reduce_scatter | solution.py:266
  604.7 108.1 %reduce-scatter.11.cloned.1.call-start = ((), (), s32[]{:S(2)}) async-start(), calls=%async_computation.11 | async-start | bytes 5242880 | tf_op jit(solution)/shard_map/reduce_scatter | solution.py:266
  614.4 184.1 %reduce-scatter.9.cloned.1.call-start = ((), (), s32[]{:S(2)}) async-start(), calls=%async_computation.10 | async-start | bytes 10485760 | tf_op jit(solution)/shard_map/reduce_scatter | solution.py:266
  647.6 50.7 %collective-permute-start.49 = (bf16[128,2048]{1,0:T(8,128)(2,1)}, bf16[128,2048]{1,0:T(8,128)(2,1)}, u32[]{:S(2)}, u32[]{:S(2)}) collective-permute-start(bf16[128,2048]{1,0:T(8,128)(2,1)} %get-tuple-element.59), channel_id=1, source_target_pairs={{0,4},{2,6},{4,0},{6,2},{1,5},{3,7},{5,1},{7,3},{8,12},{10,14},{12... | collective-permute-start | bytes 1572872 | tf_op jit(solution)/shard_map/ppermute | solution.py:68
  651.9 53.0 %collective-permute-start.58 = (bf16[128,256]{1,0:T(8,128)(2,1)S(1)}, bf16[128,256]{1,0:T(8,128)(2,1)S(1)}, u32[]{:S(2)}, u32[]{:S(2)}) collective-permute-start(bf16[128,256]{1,0:T(8,128)(2,1)S(1)} %get-tuple-element.129), channel_id=1, source_target_pairs={{0,6},{2,0},{4,2},{6,4},{1,7},{3,1},{5,3},{7,5},{8,14},{10,8},{12,... | collective-permute-start | bytes 196616 | tf_op jit(solution)/shard_map/ppermute | solution.py:68
  652.9 52.1 %collective-permute-start.57 = (bf16[128,256]{1,0:T(8,128)(2,1)S(1)}, bf16[128,256]{1,0:T(8,128)(2,1)S(1)}, u32[]{:S(2)}, u32[]{:S(2)}) collective-permute-start(bf16[128,256]{1,0:T(8,128)(2,1)S(1)} %get-tuple-element.130), channel_id=1, source_target_pairs={{0,4},{2,6},{4,0},{6,2},{1,5},{3,7},{5,1},{7,3},{8,12},{10,14},{12... | collective-permute-start | bytes 196616 | tf_op jit(solution)/shard_map/ppermute | solution.py:68
  659.4 45.5 %collective-permute-start.56 = (bf16[128,256]{1,0:T(8,128)(2,1)S(1)}, bf16[128,256]{1,0:T(8,128)(2,1)S(1)}, u32[]{:S(2)}, u32[]{:S(2)}) collective-permute-start(bf16[128,256]{1,0:T(8,128)(2,1)S(1)} %get-tuple-element.131), channel_id=1, source_target_pairs={{0,2},{2,4},{4,6},{6,0},{1,3},{3,5},{5,7},{7,1},{8,10},{10,12},{12... | collective-permute-start | bytes 196616 | tf_op jit(solution)/shard_map/ppermute | solution.py:68
  714.8 89.0 %collective-permute-start.65 = (bf16[128,1024]{1,0:T(8,128)(2,1)S(1)}, bf16[128,1024]{1,0:T(8,128)(2,1)S(1)}, u32[]{:S(2)}, u32[]{:S(2)}) collective-permute-start(bf16[128,1024]{1,0:T(8,128)(2,1)S(1)} %get-tuple-element.79), channel_id=1, source_target_pairs={{0,6},{2,0},{4,2},{6,4},{1,7},{3,1},{5,3},{7,5},{8,14},{10,8},{12,... | collective-permute-start | bytes 786440 | tf_op jit(solution)/shard_map/ppermute | solution.py:68
  715.1 93.0 %collective-permute-start.64 = (bf16[128,1024]{1,0:T(8,128)(2,1)}, bf16[128,1024]{1,0:T(8,128)(2,1)}, u32[]{:S(2)}, u32[]{:S(2)}) collective-permute-start(bf16[128,1024]{1,0:T(8,128)(2,1)} %get-tuple-element.80), channel_id=1, source_target_pairs={{0,4},{2,6},{4,0},{6,2},{1,5},{3,7},{5,1},{7,3},{8,12},{10,14},{12... | collective-permute-start | bytes 786440 | tf_op jit(solution)/shard_map/ppermute | solution.py:68
  716.3 91.8 %collective-permute-start.63 = (bf16[128,1024]{1,0:T(8,128)(2,1)}, bf16[128,1024]{1,0:T(8,128)(2,1)}, u32[]{:S(2)}, u32[]{:S(2)}) collective-permute-start(bf16[128,1024]{1,0:T(8,128)(2,1)} %get-tuple-element.81), channel_id=1, source_target_pairs={{0,2},{2,4},{4,6},{6,0},{1,3},{3,5},{5,7},{7,1},{8,10},{10,12},{12... | collective-permute-start | bytes 786440 | tf_op jit(solution)/shard_map/ppermute | solution.py:68
  718.4 85.4 %collective-permute-start.55 = (f32[128]{0:T(128)S(1)}, f32[128]{0:T(128)S(1)}, u32[]{:S(2)}, u32[]{:S(2)}) collective-permute-start(f32[128]{0:T(128)S(1)} %add_add_fusion), channel_id=1, source_target_pairs={{0,1},{1,0},{2,3},{3,2},{4,5},{5,4},{6,7},{7,6},{8,9},{9,8},{10,11... | collective-permute-start | bytes 1544 | tf_op jit(solution)/shard_map/ppermute | solution.py:71
  803.8 44.5 %collective-permute-start.60 = (bf16[128,2048]{1,0:T(8,128)(2,1)S(1)}, bf16[128,2048]{1,0:T(8,128)(2,1)S(1)}, u32[]{:S(2)}, u32[]{:S(2)}) collective-permute-start(bf16[128,2048]{1,0:T(8,128)(2,1)S(1)} %get-tuple-element.55), channel_id=1, source_target_pairs={{0,4},{2,6},{4,0},{6,2},{1,5},{3,7},{5,1},{7,3},{8,12},{10,14},{12... | collective-permute-start | bytes 1572872 | tf_op jit(solution)/shard_map/ppermute | solution.py:68
  (98 other events, 1851.8 us)
Sparse Core Ops, SparseCore 0:
  31.6 32.5 all-gather.4
  66.6 26.6 all-gather.6
  105.3 101.2 all-gather.8
  224.7 54.6 all-gather.10
  589.6 28.7 reduce-scatter.6
  622.1 30.9 reduce-scatter.4
  656.3 52.6 reduce-scatter.10
  712.1 86.3 reduce-scatter.8

commit v2 on v1

v2 whole, which is shorter than its diff:
```python
import math

import jax
import jax.numpy as jnp
from jax import lax
from jax.experimental import pallas as pl
from jax.experimental.pallas import tpu as pltpu
from jax.sharding import PartitionSpec as P

HEADS = 32
KV_HEADS = 8
HEAD_DIM = 64
GROUP = HEADS // KV_HEADS
EPS = 1e-05
LOW = jnp.bfloat16
WIDE = jnp.float32


def rope_tables(positions, head_dim):
    half_dim = head_dim // 2
    freq_index = jnp.arange(half_dim, dtype=WIDE)
    base_freq = 1.0 / jnp.power(500000.0, 2.0 * freq_index / head_dim)
    wave_len = 2.0 * math.pi / base_freq
    mix_ratio = jnp.clip((8192.0 / wave_len - 1.0) / 3.0, 0.0, 1.0)
    scaled = (1.0 - mix_ratio) * base_freq / 32.0 + mix_ratio * base_freq
    angles = positions.astype(WIDE)[:, None] * scaled[None, :]
    angles = jnp.concatenate([angles, angles], axis=1)
    return (jnp.cos(angles), jnp.sin(angles))


def matmul(left, right):
    return lax.dot_general(left, right, (((1,), (0,)), ((), ())), preferred_element_type=WIDE)


def matmul_t(left, right):
    return lax.dot_general(left, right, (((1,), (1,)), ((), ())), preferred_element_type=WIDE)


def outer(left, right):
    return lax.dot_general(left, right, (((0,), (0,)), ((), ())), preferred_element_type=WIDE)


def inverse_rms(hidden):
    return lax.rsqrt(jnp.mean(hidden * hidden, axis=-1, keepdims=True) + EPS)


def norm_reverse(hidden, inv_rms, gain_row, grad_in):
    weighted = grad_in * gain_row
    scale = jnp.mean(weighted * hidden, axis=-1, keepdims=True)
    return inv_rms * weighted - hidden * (inv_rms * inv_rms * inv_rms) * scale


def after(value, *earlier):
    return lax.optimization_barrier((value, *earlier))[0]


class Groups:
    def __init__(self, mesh):
        self.n_f = mesh.shape["fsdp"]
        self.n_c = mesh.shape["context"]
        self.c = lax.axis_index("context")
        self.t = lax.axis_index("tensor")
        self.bits = [self.n_c >> (i + 1) for i in range(self.n_c.bit_length() - 1)]
        self.order = [0]
        for bit in self.bits:
            self.order = self.order + [o ^ bit for o in self.order]

    def flip(self, block, mask):
        return lax.ppermute(block, "context", [(i, i ^ mask) for i in range(self.n_c)])

    def swap(self, block):
        return lax.ppermute(block, "tensor", [(0, 1), (1, 0)])

    def exchange(self, blocks):
        got = [lax.dynamic_index_in_dim(blocks, self.c ^ mask, 0, keepdims=False) for mask in range(self.n_c)]
        return [self.flip(mine, mask) if mask else mine for mask, mine in enumerate(got)]

    def by_source(self, got):
        return [lax.select_n(self.c ^ j, *got) for j in range(self.n_c)]

    def add_far(self, near, far):
        return near.astype(WIDE) + self.swap(far).astype(WIDE)

    def with_far(self, near):
        return jnp.concatenate([near, self.swap(near)], axis=0)

    def gather_near(self, near):
        for bit in self.bits:
            near = jnp.concatenate([near, self.flip(near, bit)], axis=0)
        return near

    def scatter_step(self, total, bit):
        keep = total.shape[0] // 2
        return total[:keep], self.flip(total[keep:].astype(LOW), bit)

    def scatter_near(self, total):
        for bit in reversed(self.bits):
            kept, got = self.scatter_step(total, bit)
            total = kept + got.astype(WIDE)
        return total

    def scatter_and_gather(self, total, near):
        for low_bit, high_bit in zip(reversed(self.bits), self.bits):
            kept, got = self.scatter_step(total, low_bit)
            there = self.flip(near, high_bit)
            got, there = lax.optimization_barrier((got, there))
            total = kept + got.astype(WIDE)
            near = jnp.concatenate([near, there], axis=0)
        return total, near

    def both_halves(self, mine):
        other = self.swap(mine)
        first = self.t == 0
        return jnp.concatenate([jnp.where(first, mine, other), jnp.where(first, other, mine)], axis=0)


def halves_turned(pair):
    lane = lax.broadcasted_iota(jnp.int32, pair.shape, 1) % HEAD_DIM
    half_dim = HEAD_DIM // 2
    ahead = pltpu.roll(pair, pair.shape[1] - half_dim, 1)
    behind = pltpu.roll(pair, half_dim, 1)
    return jnp.where(lane < half_dim, ahead, behind)


def turn(pair, cos_pair, sin_pair):
    return pair * cos_pair + halves_turned(pair) * sin_pair


def on_lanes(pair, side):
    lane = lax.broadcasted_iota(jnp.int32, pair.shape, 1)
    return jnp.where((lane >= HEAD_DIM) == bool(side), pair, jnp.zeros_like(pair))


def masked(scores, key_pos, limit):
    return jnp.where(key_pos <= limit, scores * HEAD_DIM ** (-0.5), -1e30)


def dot_nt(left, right):
    return lax.dot_general(left, right, (((1,), (1,)), ((), ())), preferred_element_type=WIDE)


def dot_nn(left, right):
    return lax.dot_general(left, right, (((1,), (0,)), ((), ())), preferred_element_type=WIDE)


def dot_tn(left, right):
    return lax.dot_general(left, right, (((0,), (0,)), ((), ())), preferred_element_type=WIDE)


def attention_kernel(
    prefix, limit_ref, key_pos_ref, cos_ref, sin_ref, kv_cos_ref, kv_sin_ref, q_ref, kv_ref,
    q_out, kv_out, mixed_out, log_out, keys, values,
):
    @pl.when(pl.program_id(0) == 0)
    def _():
        kv = turn(kv_ref[...], kv_cos_ref[...], kv_sin_ref[...])
        kv_out[...] = kv.astype(LOW)
        kv = kv.astype(LOW).astype(WIDE)
        first = on_lanes(kv, 0)
        second = on_lanes(kv, 1)
        keys[0] = first.astype(LOW)
        keys[1] = pltpu.roll(first, HEAD_DIM, 1).astype(LOW)
        values[0] = jnp.transpose(pltpu.roll(second, HEAD_DIM, 1)).astype(LOW)
        values[1] = jnp.transpose(second).astype(LOW)

    limit = jnp.maximum(limit_ref[...], prefix[0] - 1)
    key_pos = key_pos_ref[...]
    for pair in range(q_ref.shape[1] // 128):
        lanes = slice(pair * 128, pair * 128 + 128)
        query = turn(q_ref[:, lanes], cos_ref[...], sin_ref[...]).astype(LOW)
        q_out[:, lanes] = query
        mixed = None
        for side in range(2):
            scores = masked(dot_nt(keys[side], query), key_pos, limit)
            top = jnp.max(scores, axis=0, keepdims=True)
            powers = jnp.exp(scores - top)
            total = jnp.sum(powers, axis=0, keepdims=True)
            part = dot_nn(values[side], (powers * (1.0 / total)).astype(LOW))
            mixed = part if mixed is None else mixed + part
            log_out[2 * pair + side : 2 * pair + side + 1, :] = top + jnp.log(total)
        mixed_out[:, lanes] = jnp.transpose(mixed).astype(LOW)


def attention_back_kernel(
    prefix, limit_ref, key_pos_ref, cos_ref, sin_ref, kv_cos_ref, kv_sin_ref, log_ref, q_ref, kv_ref, grad_ref,
    out_ref, keys, values, total,
):
    step = pl.program_id(0)
    width = q_ref.shape[1]
    rows = q_ref.shape[0]

    @pl.when(step == 0)
    def _():
        kv = kv_ref[...].astype(WIDE)
        first = on_lanes(kv, 0)
        second = on_lanes(kv, 1)
        keys[0] = first.astype(LOW)
        keys[1] = pltpu.roll(first, HEAD_DIM, 1).astype(LOW)
        values[0] = pltpu.roll(second, HEAD_DIM, 1).astype(LOW)
        values[1] = second.astype(LOW)
        total[...] = jnp.zeros_like(total)

    limit = jnp.maximum(limit_ref[...], prefix[0] - 1)
    key_pos = key_pos_ref[...]
    for pair in range(width // 128):
        lanes = slice(pair * 128, pair * 128 + 128)
        query = q_ref[:, lanes]
        grad = grad_ref[:, lanes]
        q_grad = None
        for side in range(2):
            head = 2 * pair + side
            scores = masked(dot_nt(keys[side], query), key_pos, limit)
            probs = jnp.exp(scores - log_ref[head : head + 1, :])
            grad_probs = dot_nt(values[side], grad)
            delta = jnp.sum(probs * grad_probs, axis=0, keepdims=True)
            grad_scores = (probs * (grad_probs - delta)).astype(LOW)
            mine = on_lanes(grad.astype(WIDE), side)
            asked = on_lanes(query.astype(WIDE), side)
            mine = mine if side else pltpu.roll(mine, HEAD_DIM, 1)
            asked = pltpu.roll(asked, HEAD_DIM, 1) if side else asked
            total[...] += dot_nn(probs.astype(LOW), mine.astype(LOW)) + dot_nn(grad_scores, asked.astype(LOW))
            part = dot_tn(grad_scores, keys[side])
            q_grad = part if q_grad is None else q_grad + part
        turned = turn(q_grad * HEAD_DIM ** (-0.5), cos_ref[...], -sin_ref[...])
        out_ref[pl.ds(step * rows, rows), lanes] = turned.astype(LOW)

    @pl.when(step == pl.num_programs(0) - 1)
    def _():
        kv = total[...]
        lane = lax.broadcasted_iota(jnp.int32, kv.shape, 1)
        kv = jnp.where(lane < HEAD_DIM, kv * HEAD_DIM ** (-0.5), kv)
        out_ref[:, width:] = turn(kv, kv_cos_ref[...], -kv_sin_ref[...]).astype(LOW)


def attention_specs(tokens, width, rows):
    whole = lambda *shape: pl.BlockSpec(shape, lambda i: (0,) * len(shape))
    per_row = lambda cols: pl.BlockSpec((rows, cols), lambda i: (i, 0))
    shared = [
        pl.BlockSpec(memory_space=pltpu.SMEM),
        pl.BlockSpec((1, rows), lambda i: (0, i)),
        whole(tokens, 1),
        per_row(128),
        per_row(128),
        whole(tokens, 128),
        whole(tokens, 128),
    ]
    return whole, per_row, shared


ROWS = 256


def attention_cost(tokens, width, dots):
    heads = width // HEAD_DIM
    return pl.CostEstimate(
        flops=dots * 2 * heads * tokens * tokens * 128,
        bytes_accessed=tokens * width * 12,
        transcendentals=heads * tokens * tokens,
    )


def attention(qkv, shared):
    tokens = qkv.shape[0]
    width = qkv.shape[1] - 128
    whole, per_row, specs = attention_specs(tokens, width, ROWS)
    return pl.pallas_call(
        attention_kernel,
        grid=(tokens // ROWS,),
        in_specs=specs
        + [per_row(width), pl.BlockSpec((tokens, 128), lambda i: (0, width // 128))],
        out_specs=[per_row(width), whole(tokens, 128), per_row(width), pl.BlockSpec((8, ROWS), lambda i: (0, i))],
        out_shape=[
            jax.ShapeDtypeStruct((tokens, width), LOW),
            jax.ShapeDtypeStruct((tokens, 128), LOW),
            jax.ShapeDtypeStruct((tokens, width), LOW),
            jax.ShapeDtypeStruct((8, tokens), WIDE),
        ],
        scratch_shapes=[pltpu.VMEM((2, tokens, 128), LOW), pltpu.VMEM((2, 128, tokens), LOW)],
        compiler_params=pltpu.CompilerParams(vmem_limit_bytes=40 << 20),
        cost_estimate=attention_cost(tokens, width, 2),
        name="attention",
    )(*shared, qkv, qkv)


def attention_back(query, kv, logs, grad, shared):
    tokens, width = query.shape
    whole, per_row, specs = attention_specs(tokens, width, ROWS)
    return pl.pallas_call(
        attention_back_kernel,
        grid=(tokens // ROWS,),
        in_specs=specs
        + [pl.BlockSpec((8, ROWS), lambda i: (0, i)), per_row(width), whole(tokens, 128), per_row(width)],
        out_specs=whole(tokens, width + 128),
        out_shape=jax.ShapeDtypeStruct((tokens, width + 128), LOW),
        scratch_shapes=[
            pltpu.VMEM((2, tokens, 128), LOW),
            pltpu.VMEM((2, tokens, 128), LOW),
            pltpu.VMEM((tokens, 128), WIDE),
        ],
        compiler_params=pltpu.CompilerParams(vmem_limit_bytes=40 << 20),
        cost_estimate=attention_cost(tokens, width, 5),
        name="attention_back",
    )(*shared, logs, query, kv, grad)


def by_dest(weight, count):
    rows, columns = weight.shape
    return weight.astype(LOW).reshape(rows, count, columns // count).transpose(1, 0, 2)


def kv_by_dest(weight, count):
    rows, columns = weight.shape
    heads = columns // HEAD_DIM
    if count <= heads:
        return by_dest(weight, count)
    return jnp.repeat(by_dest(weight, heads), count // heads, axis=0)


def make_layer(mesh):
    def on_device(
        layer_input,
        prefix,
        attn_gain,
        q_weight,
        k_weight,
        v_weight,
        output_weight,
        mlp_gain,
        gate_weight,
        up_weight,
        down_weight,
        cotangent,
    ):
        g = Groups(mesh)
        n_c = g.n_c
        x_own = layer_input[0]
        local, width = x_own.shape
        half = local // 2
        rows = q_weight.shape[0]

        def join_weight(got):
            return lax.all_gather(jnp.concatenate(g.by_source(got), axis=0), "fsdp", axis=0, tiled=True)

        x_mine = lax.dynamic_slice_in_dim(x_own, g.t * half, half, 0)
        cot_mine = lax.dynamic_slice_in_dim(cotangent[0], g.t * half, half, 0)
        q_cols = q_weight.shape[1] // n_c
        kv_blocks = kv_by_dest(k_weight, n_c), kv_by_dest(v_weight, n_c)
        kv_cols = kv_blocks[0].shape[2]
        wide = q_cols + 2 * kv_cols
        gains = jnp.pad(jnp.stack([attn_gain, mlp_gain], axis=1).astype(LOW), ((0, 0), (0, 126)))
        gain_blocks = jnp.broadcast_to(gains[None], (n_c, *gains.shape))
        attn_got = g.exchange(
            jnp.concatenate(
                [by_dest(q_weight, n_c), *kv_blocks, gain_blocks, by_dest(output_weight, n_c)], axis=2
            )
        )
        x_near = x_mine
        for place, bit in enumerate(g.bits):
            there = g.flip(x_near, bit)
            if place == 0:
                there, *attn_got = lax.optimization_barrier((there, *attn_got))
                gu_got = g.exchange(
                    after(
                        jnp.concatenate([by_dest(gate_weight, n_c), by_dest(up_weight, n_c)], axis=2), there
                    )
                )
            x_near = jnp.concatenate([x_near, there], axis=0)
        attn_full = join_weight(attn_got)
        x_all = g.with_far(x_near)
        gains_all = attn_full[:, wide : wide + 2].T.astype(WIDE)
        qkv_full = attn_full[:, :wide]
        o_full = attn_full[:, wide + 128 :]
        gain_one, gain_two = gains_all[0:1], gains_all[1:2]

        block = (g.c ^ jnp.array(g.order, jnp.int32)) * local
        side = jnp.stack([g.t, 1 - g.t]).astype(jnp.int32) * half
        positions = (
            side[:, None, None] + block[None, :, None] + jnp.arange(half, dtype=jnp.int32)[None, None, :]
        ).reshape(-1)
        cos_table, sin_table = rope_tables(positions, HEAD_DIM)
        half_dim = HEAD_DIM // 2
        sin_table = jnp.concatenate([-sin_table[:, :half_dim], sin_table[:, half_dim:]], axis=1)
        tables = (
            prefix,
            positions[None, :],
            positions[:, None],
            jnp.tile(cos_table, (1, 2)),
            jnp.tile(sin_table, (1, 2)),
            jnp.concatenate([cos_table, jnp.ones_like(cos_table)], axis=1),
            jnp.concatenate([sin_table, jnp.zeros_like(sin_table)], axis=1),
        )

        hidden_in = x_all.astype(WIDE)
        rms_one = inverse_rms(hidden_in)
        normed_one = (hidden_in * rms_one * gain_one).astype(LOW)
        qkv = matmul(normed_one, qkv_full)
        down_got = g.exchange(after(by_dest(down_weight, n_c), qkv))
        query_rot, kv_rot, attended, logs = attention(qkv, tables)
        gu_got, down_got, attended = lax.optimization_barrier((gu_got, down_got, attended))
        gu_full = join_weight(gu_got)
        down_full = join_weight(down_got)
        near_rows = n_c * half
        far_part = matmul_t(attended[near_rows:], o_full).astype(LOW)
        near_part = matmul_t(attended[:near_rows], o_full)
        x_mine = x_mine.astype(WIDE)
        branch, cot_near = g.scatter_and_gather(g.add_far(near_part, far_part), after(cot_mine, attended))
        cot_all = g.with_far(cot_near)
        resid = x_mine + branch
        rms_two = inverse_rms(resid)
        normed_two = g.with_far(g.gather_near((resid * rms_two * gain_two).astype(LOW)))

        gate_up = matmul(normed_two, gu_full)
        hid = gate_up.shape[1] // 2
        gate_proj, up_proj = gate_up[:, :hid], gate_up[:, hid:]
        squash = jax.nn.sigmoid(gate_proj)
        inner = (gate_proj * squash * up_proj).astype(LOW)
        grad_inner = matmul(cot_all, down_full)
        grad_gate = grad_inner * up_proj * squash * (1.0 + gate_proj * (1.0 - squash))
        grad_up = grad_inner * gate_proj * squash
        grad_gu = jnp.concatenate([grad_gate.astype(LOW), grad_up.astype(LOW)], axis=1)
        far_grad = matmul_t(grad_gu[near_rows:], gu_full).astype(LOW)
        near_grad = matmul_t(grad_gu[:near_rows], gu_full)
        gu_part = outer(normed_two, grad_gu).astype(LOW)
        down_part = outer(cot_all, inner).astype(LOW)
        far_out = matmul_t(inner[near_rows:], down_full).astype(LOW)
        near_out = matmul_t(inner[:near_rows], down_full)
        out_total = g.add_far(near_out, far_out)
        grad_normed_two = g.scatter_near(g.add_far(near_grad, far_grad))
        grad_normed_two, _, _, out_total = lax.optimization_barrier(
            (grad_normed_two, gu_part, down_part, out_total)
        )
        grad_resid = cot_mine.astype(WIDE) + norm_reverse(resid, rms_two, gain_two, grad_normed_two)

        def sum_weight(part):
            return lax.psum_scatter(part, "fsdp", scatter_dimension=0, tiled=True)

        def return_weight(mine):
            return g.exchange(mine.reshape(n_c, rows, mine.shape[1]))

        gu_sum = sum_weight(gu_part)
        out_sum, branch_near = g.scatter_and_gather(out_total, grad_resid.astype(LOW))
        branch_all = g.with_far(branch_near)
        branch_all, gu_sum = lax.optimization_barrier((branch_all, gu_sum))
        down_sum = sum_weight(after(down_part, gu_sum))
        layer_output = g.both_halves((resid + out_sum).astype(LOW))
        gu_got = return_weight(gu_sum)

        def cols(blocks, start, size):
            return jnp.concatenate([b[:, start : start + size] for b in blocks], axis=1).astype(WIDE)

        grad_att = matmul(branch_all, o_full).astype(LOW)
        o_part = outer(branch_all, attended).astype(LOW)
        grad_qkv = attention_back(query_rot, kv_rot, logs, grad_att, tables)
        o_sum = sum_weight(after(o_part, down_sum))
        qkv_part = outer(normed_one, grad_qkv).astype(LOW)
        grad_qkv, down_sum, _, *gu_got = lax.optimization_barrier((grad_qkv, down_sum, qkv_part, *gu_got))
        qkv_sum = sum_weight(after(qkv_part, o_sum))
        gu_blocks = g.by_source(gu_got)
        gate_grad = cols(gu_blocks, 0, hid)
        up_grad = cols(gu_blocks, hid, hid)
        down_got = return_weight(down_sum)
        far_one = matmul_t(grad_qkv[near_rows:], qkv_full).astype(LOW)
        near_one = matmul_t(grad_qkv[:near_rows], qkv_full)
        grad_normed_one = g.scatter_near(g.add_far(near_one, far_one))
        grad_normed_one, o_sum, *down_got = lax.optimization_barrier((grad_normed_one, o_sum, *down_got))
        down_grad = cols(g.by_source(down_got), 0, hid)
        o_grad = cols(g.by_source(return_weight(o_sum)), 0, q_cols)
        qkv_blocks = g.by_source(return_weight(qkv_sum))
        q_grad = cols(qkv_blocks, 0, q_cols)

        def kv_grad(start):
            parts = [b[:, start : start + kv_cols].astype(WIDE) for b in qkv_blocks]
            copies = n_c * kv_cols // k_weight.shape[1]
            return jnp.concatenate([sum(parts[j : j + copies]) for j in range(0, n_c, copies)], axis=1)

        k_grad = kv_grad(q_cols)
        v_grad = kv_grad(q_cols + kv_cols)
        rms_mine = inverse_rms(x_mine)
        grad_in = grad_resid + norm_reverse(x_mine, rms_mine, gain_one, grad_normed_one)
        input_grad = g.both_halves(grad_in.astype(LOW))

        def gain_grad(gain, pairs):
            total = sum(jnp.sum(grad * weight.astype(LOW).astype(WIDE), axis=1) for grad, weight in pairs)
            return (total + g.swap(total)) / gain.astype(LOW).astype(WIDE)

        attn_gain_grad = gain_grad(attn_gain, [(q_grad, q_weight), (k_grad, k_weight), (v_grad, v_weight)])
        mlp_gain_grad = gain_grad(mlp_gain, [(gate_grad, gate_weight), (up_grad, up_weight)])
        return (
            layer_output[None],
            input_grad[None],
            attn_gain_grad,
            q_grad,
            k_grad,
            v_grad,
            o_grad,
            mlp_gain_grad,
            gate_grad,
            up_grad,
            down_grad,
        )

    return on_device


def solution(mesh):
    tokens = P("fsdp", "context", None)
    gain = P(("fsdp", "context"))
    weight = P(("fsdp", "context"), "tensor")
    return jax.shard_map(
        make_layer(mesh),
        mesh=mesh,
        in_specs=(tokens, P("fsdp"), gain, weight, weight, weight, weight, gain, weight, weight, weight, tokens),
        out_specs=(tokens, tokens, gain, weight, weight, weight, weight, gain, weight, weight, weight),
        check_vma=False,
    )
```

time: 873 us -> 687 us (0.79)
  waiting for transfers between devices: 458 us -> 366 us
  matrix products: 145 us -> 96.2 us
  starting transfers between devices: 122 us -> 78.4 us
  Pallas kernels: 0 us -> 27.1 us
  other arithmetic: 70 us -> 50.2 us
  local copies, waits for them, and re-layouts: 52.6 us -> 43.1 us
    reduce_scatter x4, waiting for transfers between devices: 78.5 us -> 0.03 us  [sum_weight(): return lax.psum_scatter(part, 'fsdp', scatter_dimension=0, tiled=True)]
    ppermute x54 -> x37, starting transfers between devices: 110 us -> 63.1 us  [flip(): lax.ppermute(block, 'context', [(i, i ^ mask) for i in range(self.n_c)])]
    dot_general x6 -> x0, matrix products: 40.5 us -> none  [the longest x1 8.64 us: attention_reverse(): jnp.einsum('kgij,ikgd->jkd', probs.astype(LOW), grad_heads, preferred_ele...]
    pallas_call x0 -> x2, Pallas kernels: none -> 27.1 us  [the longest x1 15.6 us: attention_back(): pl.pallas_call(attention_back_kernel, grid=(tokens // ROWS,), in_specs=sp...]
    ppermute x54 -> x37, waiting for transfers between devices: 371 us -> 353 us  [flip(): lax.ppermute(block, 'context', [(i, i ^ mask) for i in range(self.n_c)])]
    another operation x3 -> x2, other arithmetic: 11.2 us -> 0.77 us  [on_device(): jnp.stack([attn_gain, mlp_gain], axis=1).astype(LOW)]
    unnamed x140 -> x134, local copies, waits for them, and re-layouts: 31.3 us -> 25.5 us
  transfers between devices with their start and end apart: 74 -> 56, of which waited for: 28 -> 27; matrix products, arithmetic and copies ran while one was open for 23% -> 21% of each run, Pallas kernels for 0% -> 4%
where the time goes in v2:
time: 687 us; the launch traced here: 678 us
  waiting for transfers between devices  366 us (53%)
  matrix products  96.2 us (14%)
  starting transfers between devices  78.4 us (11%)
  other arithmetic  50.2 us (7%)
  local copies, waits for them, and re-layouts  43.1 us (6%)
  Pallas kernels  27.1 us (4%)
  between operations  16.3 us (2%)
    ppermute x37, waiting for transfers between devices, flip(): lax.ppermute(block, 'context', [(i, i ^ mask) for i in range(self.n_c)])  353 us
    ppermute x37, starting transfers between devices, flip(): lax.ppermute(block, 'context', [(i, i ^ mask) for i in range(self.n_c)])  63.1 us
    dot_general x4, matrix products, matmul(): lax.dot_general(left, right, (((1,), (0,)), ((), ())), preferred_element_...  35.7 us
    dot_general x8, matrix products, matmul_t(): lax.dot_general(left, right, (((1,), (1,)), ((), ())), preferred_element_...  34.3 us
    dot_general x4, matrix products, outer(): lax.dot_general(left, right, (((0,), (0,)), ((), ())), preferred_element_...  26.2 us
    unnamed x134, local copies, waits for them, and re-layouts  25.5 us
    pallas_call x1, Pallas kernels, attention_back(): pl.pallas_call(attention_back_kernel, grid=(tokens // ROWS,), in_specs=sp...  15.6 us
    ppermute x12, starting transfers between devices, swap(): return lax.ppermute(block, 'tensor', [(0, 1), (1, 0)])  14.4 us
  transfers between devices with their start and end apart: 56, of which 27 were waited for; matrix products, arithmetic and copies ran while one was open for 21% of the time, Pallas kernels for 4%

profile of v2, /device:TPU:1, one launch (start us, length us, event | category | flops | bytes accessed | tf_op | source)
XLA Modules:
  0.0 677.6 jit_solution(4553191904001692444)
XLA Ops:
  21.5 4.9 collective-permute-done.1
  26.4 20.7 %collective-permute-done.2 = bf16[128,768]{1,0:T(8,128)(2,1)S(1)} collective-permute-done((bf16[128,768]{1,0:T(8,128)(2,1)S(1)}, bf16[128,768]{1,0:T(8,128)(2,1)S(1)}, u32[]{:S(2)}, u32[]{:S(2)}) %collective-permute-start.2) | collective-permute-done | bytes 196640 | tf_op jit(solution)/shard_map/ppermute | solution.py:69
  49.3 5.4 collective-permute-start.7
  58.1 20.0 %collective-permute-done.7 = bf16[256,2048]{1,0:T(8,128)(2,1)} collective-permute-done((bf16[256,2048]{1,0:T(8,128)(2,1)}, bf16[256,2048]{1,0:T(8,128)(2,1)}, u32[]{:S(2)}, u32[]{:S(2)}) %collective-permute-start.7) | collective-permute-done | bytes 1048608 | tf_op jit(solution)/shard_map/ppermute | solution.py:69
  92.3 5.0 all-gather.4.cloned.1.call-done
  99.4 6.0 fusion.11.q_ref.kv_ref
  109.4 15.0 %collective-permute-start.9 = (bf16[128,1024]{1,0:T(8,128)(2,1)}, bf16[128,1024]{1,0:T(8,128)(2,1)}, u32[]{:S(2)}, u32[]{:S(2)}) collective-permute-start(bf16[128,1024]{1,0:T(8,128)(2,1)} %get-tuple-element.178), channel_id=1, source_target_pairs={{0,2},{2,0},{4,6},{6,4},{1,3},{3,1},{5,7},{7,5},{8,10},{10,8},{12,... | collective-permute-start | bytes 786440 | tf_op jit(solution)/shard_map/ppermute | solution.py:69
  127.8 11.5 %attention.1 = (bf16[1024,256]{1,0:T(8,128)(2,1)S(1)}, bf16[1024,128]{1,0:T(8,128)(2,1)S(1)}, bf16[1024,256]{1,0:T(8,128)(2,1)S(1)}, f32[8,1024]{1,0:T(8,128)S(1)}) custom-call(s32[1]{0:T(128)S(6)} %copy.98.prefix, s32[1,1024]{1,0:T(1,128)S(1)} %bitcast.147, s32[1024,1]{1,0:T(8,128)S(1)} %copy.68.key_pos_ref, f32[1024,128]{1,0:T(8,128)S(1)} %copy.69.cos_ref, ...), custom_call_target="tpu_custom_call" | custom-call | flops 2147483648 | bytes 3145728 | tf_op jit(solution)/shard_map/attention/pallas_call | solution.py:266
  140.1 6.2 collective-permute-done.5
  146.3 11.2 %collective-permute-done.10 = bf16[128,1024]{1,0:T(8,128)(2,1)} collective-permute-done((bf16[128,1024]{1,0:T(8,128)(2,1)}, bf16[128,1024]{1,0:T(8,128)(2,1)}, u32[]{:S(2)}, u32[]{:S(2)}) %collective-permute-start.10) | collective-permute-done | bytes 262176 | tf_op jit(solution)/shard_map/ppermute | solution.py:69
  172.7 31.0 %collective-permute-done.14 = bf16[128,2048]{1,0:T(8,128)(2,1)S(1)} collective-permute-done((bf16[128,2048]{1,0:T(8,128)(2,1)S(1)}, bf16[128,2048]{1,0:T(8,128)(2,1)S(1)}, u32[]{:S(2)}, u32[]{:S(2)}) %collective-permute-start.14) | collective-permute-done | bytes 524320 | tf_op jit(solution)/shard_map/ppermute | solution.py:69
  214.2 27.0 %collective-permute-done.15 = bf16[128,2048]{1,0:T(8,128)(2,1)} collective-permute-done((bf16[128,2048]{1,0:T(8,128)(2,1)}, bf16[128,2048]{1,0:T(8,128)(2,1)}, u32[]{:S(2)}, u32[]{:S(2)}) %collective-permute-start.15) | collective-permute-done | bytes 524320 | tf_op jit(solution)/shard_map/ppermute | solution.py:69
  247.3 22.6 %collective-permute-done.18 = bf16[128,2048]{1,0:T(8,128)(2,1)S(1)} collective-permute-done((bf16[128,2048]{1,0:T(8,128)(2,1)S(1)}, bf16[128,2048]{1,0:T(8,128)(2,1)S(1)}, u32[]{:S(2)}, u32[]{:S(2)}) %collective-permute-start.18) | collective-permute-done | bytes 524320 | tf_op jit(solution)/shard_map/ppermute | solution.py:69
  273.2 20.1 %collective-permute-done.19 = bf16[256,2048]{1,0:T(8,128)(2,1)S(1)} collective-permute-done((bf16[256,2048]{1,0:T(8,128)(2,1)S(1)}, bf16[256,2048]{1,0:T(8,128)(2,1)S(1)}, u32[]{:S(2)}, u32[]{:S(2)}) %collective-permute-start.19) | collective-permute-done | bytes 1048608 | tf_op jit(solution)/shard_map/ppermute | solution.py:69
  299.9 14.5 %fusion.32 = f32[1024,2048]{0,1:T(8,128)} fusion(bf16[2048,2048]{1,0:T(8,128)(2,1)} %all-gather.8.cloned.1.call-done, bf16[512,2048]{1,0:T(8,128)(2,1)} %collective-permute-done.20, bf16[256,2048]{1,0:T(8,128)(2,1)} %copy-done.40, bf16[128,2048]{1,0:T(8,128)(2,1)} %copy-done.36, bf16[128,2048]{1,0:T(8,128)(2,1)} %copy-done.23), kind=kOutput, calls=%fused_computation.100 | convolution fusion | flops 8606711808 | bytes 20971520 | tf_op jit(solution)/shard_map/dot_general | solution.py:32
  314.4 12.8 %multiply_convert_fusion.1 = (bf16[1024,1024]{0,1:T(8,128)(2,1)S(1)}, bf16[1024,1024]{0,1:T(8,128)(2,1)S(1)}, bf16[1024,1024]{0,1:T(8,128)(2,1)}) fusion(f32[1024,2048]{0,1:T(8,128)} %fusion.32, bf16[1024,2048]{1,0:T(8,128)(2,1)} %copy-done.49, bf16[2048,1024]{1,0:T(8,128)(2,1)} %all-gather.6.cloned.1.call-done), kind=kOutput, calls=%fused_computation.18 | convolution fusion | flops 4311744512 | bytes 23068672 | tf_op jit(solution)/shard_map/dot_general | solution.py:32
  329.3 12.5 %convolution_convert_fusion = bf16[2048,2048]{1,0:T(8,128)(2,1)} fusion(bf16[1024,1024]{0,1:T(8,128)(2,1)S(1)} %get-tuple-element.141, bf16[1024,1024]{0,1:T(8,128)(2,1)S(1)} %get-tuple-element.142, bf16[512,2048]{1,0:T(8,128)(2,1)} %collective-permute-done.20, bf16[256,2048]{1,0:T(8,128)(2,1)S(1)} %copy-done.41, bf16[128,2048]{1,0:T(8,128)(2,1)S(1)} %copy-done.37, ...), kind=kOutput, calls=%fused_computation.5 | convolution fusion | flops 8619294720 | bytes 16777216 | tf_op jit(solution)/shard_map/dot_general | solution.py:40
  341.8 8.7 %convolution_convert_fusion.5 = bf16[512,2048]{1,0:T(8,128)(2,1)S(1)} fusion(bf16[2048,2048]{1,0:T(8,128)(2,1)} %all-gather.8.cloned.1.call-done, bf16[1024,1024]{0,1:T(8,128)(2,1)} %copy-done.59, bf16[1024,1024]{0,1:T(8,128)(2,1)} %copy-done.58), kind=kOutput, calls=%fused_computation.26 | convolution fusion | flops 4300210176 | bytes 14680064 | tf_op jit(solution)/shard_map/dot_general | solution.py:36
  354.9 8.2 %convert_add_fusion.2 = f32[512,2048]{1,0:T(8,128)S(1)} fusion(bf16[512,2048]{1,0:T(8,128)(2,1)S(1)} %collective-permute-done.21, bf16[2048,2048]{1,0:T(8,128)(2,1)} %all-gather.8.cloned.1.call-done, bf16[1024,1024]{0,1:T(8,128)(2,1)} %copy-done.59, bf16[1024,1024]{0,1:T(8,128)(2,1)} %copy-done.58), kind=kOutput, calls=%fused_computation.17 | convolution fusion | flops 4301258752 | bytes 18874368 | tf_op jit(solution)/shard_map/dot_general | solution.py:36
  366.3 6.3 convolution_convert_fusion.1
  372.6 18.1 %collective-permute-done.22 = bf16[256,2048]{1,0:T(8,128)(2,1)} collective-permute-done((bf16[256,2048]{1,0:T(8,128)(2,1)}, bf16[256,2048]{1,0:T(8,128)(2,1)}, u32[]{:S(2)}, u32[]{:S(2)}) %collective-permute-start.22) | collective-permute-done | bytes 1048608 | tf_op jit(solution)/shard_map/ppermute | solution.py:69
  394.0 4.0 convert_add_fusion.1
  398.1 20.8 %collective-permute-done.23 = bf16[128,2048]{1,0:T(8,128)(2,1)S(1)} collective-permute-done((bf16[128,2048]{1,0:T(8,128)(2,1)S(1)}, bf16[128,2048]{1,0:T(8,128)(2,1)S(1)}, u32[]{:S(2)}, u32[]{:S(2)}) %collective-permute-start.23) | collective-permute-done | bytes 524320 | tf_op jit(solution)/shard_map/ppermute | solution.py:69
  423.1 29.7 %collective-permute-done.26 = bf16[128,2048]{1,0:T(8,128)(2,1)S(1)} collective-permute-done((bf16[128,2048]{1,0:T(8,128)(2,1)S(1)}, bf16[128,2048]{1,0:T(8,128)(2,1)S(1)}, u32[]{:S(2)}, u32[]{:S(2)}) %collective-permute-start.26) | collective-permute-done | bytes 524320 | tf_op jit(solution)/shard_map/ppermute | solution.py:69
  458.8 29.8 %collective-permute-done.27 = bf16[128,2048]{1,0:T(8,128)(2,1)S(1)} collective-permute-done((bf16[128,2048]{1,0:T(8,128)(2,1)S(1)}, bf16[128,2048]{1,0:T(8,128)(2,1)S(1)}, u32[]{:S(2)}, u32[]{:S(2)}) %collective-permute-start.27) | collective-permute-done | bytes 524320 | tf_op jit(solution)/shard_map/ppermute | solution.py:69
  510.2 15.6 %attention_back.1 = bf16[1024,384]{1,0:T(8,128)(2,1)S(1)} custom-call(s32[1]{0:T(128)S(6)} %copy.98.prefix, s32[1,1024]{1,0:T(1,128)S(1)} %bitcast.148, s32[1024,1]{1,0:T(8,128)S(1)} %copy.68.key_pos_ref, f32[1024,128]{1,0:T(8,128)S(1)} %copy.69.cos_ref, f32[1024,128]{1,0:T(8,128)S(1)} %copy.70.sin_ref, f32[1024,128]{1,0:T(8,128)S(1)} %concatenate.124.kv_cos_ref, ...), custom_call_target="tpu_custom_call" | custom-call | flops 5368709120 | bytes 3145728 | tf_op jit(solution)/shard_map/attention_back/pallas_call | solution.py:288
  526.8 5.0 convolution_convert_fusion.6
  531.7 22.0 %collective-permute-done.32 = bf16[128,2048]{1,0:T(8,128)(2,1)} collective-permute-done((bf16[128,2048]{1,0:T(8,128)(2,1)}, bf16[128,2048]{1,0:T(8,128)(2,1)}, u32[]{:S(2)}, u32[]{:S(2)}) %collective-permute-start.32) | collective-permute-done | bytes 524320 | tf_op jit(solution)/shard_map/ppermute | solution.py:69
  553.7 4.1 convolution_convert_fusion.4
  570.6 21.9 %collective-permute-done.35 = bf16[256,2048]{1,0:T(8,128)(2,1)S(1)} collective-permute-done((bf16[256,2048]{1,0:T(8,128)(2,1)S(1)}, bf16[256,2048]{1,0:T(8,128)(2,1)S(1)}, u32[]{:S(2)}, u32[]{:S(2)}) %collective-permute-start.35) | collective-permute-done | bytes 1048608 | tf_op jit(solution)/shard_map/ppermute | solution.py:69
  602.1 29.1 %collective-permute-done.36 = bf16[128,2048]{1,0:T(8,128)(2,1)} collective-permute-done((bf16[128,2048]{1,0:T(8,128)(2,1)}, bf16[128,2048]{1,0:T(8,128)(2,1)}, u32[]{:S(2)}, u32[]{:S(2)}) %collective-permute-start.36) | collective-permute-done | bytes 524320 | tf_op jit(solution)/shard_map/ppermute | solution.py:69
  632.3 10.1 %collective-permute-done.38 = bf16[128,1024]{1,0:T(8,128)(2,1)} collective-permute-done((bf16[128,1024]{1,0:T(8,128)(2,1)}, bf16[128,1024]{1,0:T(8,128)(2,1)}, u32[]{:S(2)}, u32[]{:S(2)}) %collective-permute-start.38) | collective-permute-done | bytes 262176 | tf_op jit(solution)/shard_map/ppermute | solution.py:69
  (364 shorter events, 181.7 us)
Async XLA Ops:
  7.2 90.1 %all-gather.4.cloned.1.call-start = ((), (), s32[]{:S(2)}) async-start(), calls=%async_computation.4 | async-start | bytes 3932160 | tf_op jit(solution)/shard_map/all_gather | solution.py:342
  8.3 38.7 %collective-permute-start = (bf16[128,2048]{1,0:T(8,128)(2,1)S(1)}, bf16[128,2048]{1,0:T(8,128)(2,1)S(1)}, u32[]{:S(2)}, u32[]{:S(2)}) collective-permute-start(bf16[128,2048]{1,0:T(8,128)(2,1)S(1)} %dynamic-slice_bitcast_fusion.9), channel_id=1, source_target_pairs={{0,4},{2,6},{4,0},{6,2},{1,5},{3,7},{5,1},{7,3},{8,12},{10,14},{12... | collective-permute-start | bytes 1572872 | tf_op jit(solution)/shard_map/ppermute | solution.py:69
  18.8 28.2 %collective-permute-start.2 = (bf16[128,768]{1,0:T(8,128)(2,1)S(1)}, bf16[128,768]{1,0:T(8,128)(2,1)S(1)}, u32[]{:S(2)}, u32[]{:S(2)}) collective-permute-start(bf16[128,768]{1,0:T(8,128)(2,1)S(1)} %bitcast.166), channel_id=1, source_target_pairs={{0,4},{2,6},{4,0},{6,2},{1,5},{3,7},{5,1},{7,3},{8,12},{10,14},{12... | collective-permute-start | bytes 589832 | tf_op jit(solution)/shard_map/ppermute | solution.py:69
  19.1 27.9 %collective-permute-start.3 = (bf16[128,768]{1,0:T(8,128)(2,1)S(1)}, bf16[128,768]{1,0:T(8,128)(2,1)S(1)}, u32[]{:S(2)}, u32[]{:S(2)}) collective-permute-start(bf16[128,768]{1,0:T(8,128)(2,1)S(1)} %bitcast.167), channel_id=1, source_target_pairs={{0,6},{2,4},{4,2},{6,0},{1,7},{3,5},{5,3},{7,1},{8,14},{10,12},{12... | collective-permute-start | bytes 589832 | tf_op jit(solution)/shard_map/ppermute | solution.py:69
  48.2 251.7 %all-gather.8.cloned.1.call-start = ((), (), s32[]{:S(2)}) async-start(), calls=%async_computation.6 | async-start | bytes 10485760 | tf_op jit(solution)/shard_map/all_gather | solution.py:342
  49.3 28.8 %collective-permute-start.7 = (bf16[256,2048]{1,0:T(8,128)(2,1)}, bf16[256,2048]{1,0:T(8,128)(2,1)}, u32[]{:S(2)}, u32[]{:S(2)}) collective-permute-start(bf16[256,2048]{1,0:T(8,128)(2,1)} %pad_maximum_fusion.11), channel_id=1, source_target_pairs={{0,2},{2,0},{4,6},{6,4},{1,3},{3,1},{5,7},{7,5},{8,10},{10,8},{12,... | collective-permute-start | bytes 3145736 | tf_op jit(solution)/shard_map/ppermute | solution.py:69
  88.5 57.8 %collective-permute-start.5 = (bf16[128,2048]{1,0:T(8,128)(2,1)}, bf16[128,2048]{1,0:T(8,128)(2,1)}, u32[]{:S(2)}, u32[]{:S(2)}) collective-permute-start(bf16[128,2048]{1,0:T(8,128)(2,1)} %get-tuple-element.157), channel_id=1, source_target_pairs={{0,4},{2,6},{4,0},{6,2},{1,5},{3,7},{5,1},{7,3},{8,12},{10,14},{12... | collective-permute-start | bytes 1572872 | tf_op jit(solution)/shard_map/ppermute | solution.py:69
  88.7 57.6 %collective-permute-start.4 = (bf16[128,2048]{1,0:T(8,128)(2,1)}, bf16[128,2048]{1,0:T(8,128)(2,1)}, u32[]{:S(2)}, u32[]{:S(2)}) collective-permute-start(bf16[128,2048]{1,0:T(8,128)(2,1)} %get-tuple-element.158), channel_id=1, source_target_pairs={{0,2},{2,0},{4,6},{6,4},{1,3},{3,1},{5,7},{7,5},{8,10},{10,8},{12,... | collective-permute-start | bytes 1572872 | tf_op jit(solution)/shard_map/ppermute | solution.py:69
  106.3 40.0 %collective-permute-start.11 = (bf16[128,1024]{1,0:T(8,128)(2,1)}, bf16[128,1024]{1,0:T(8,128)(2,1)}, u32[]{:S(2)}, u32[]{:S(2)}) collective-permute-start(bf16[128,1024]{1,0:T(8,128)(2,1)} %get-tuple-element.176), channel_id=1, source_target_pairs={{0,6},{2,4},{4,2},{6,0},{1,7},{3,5},{5,3},{7,1},{8,14},{10,12},{12... | collective-permute-start | bytes 786440 | tf_op jit(solution)/shard_map/ppermute | solution.py:69
  109.4 48.2 %collective-permute-start.10 = (bf16[128,1024]{1,0:T(8,128)(2,1)}, bf16[128,1024]{1,0:T(8,128)(2,1)}, u32[]{:S(2)}, u32[]{:S(2)}) collective-permute-start(bf16[128,1024]{1,0:T(8,128)(2,1)} %get-tuple-element.177), channel_id=1, source_target_pairs={{0,4},{2,6},{4,0},{6,2},{1,5},{3,7},{5,1},{7,3},{8,12},{10,14},{12... | collective-permute-start | bytes 786440 | tf_op jit(solution)/shard_map/ppermute | solution.py:69
  109.4 48.1 %collective-permute-start.9 = (bf16[128,1024]{1,0:T(8,128)(2,1)}, bf16[128,1024]{1,0:T(8,128)(2,1)}, u32[]{:S(2)}, u32[]{:S(2)}) collective-permute-start(bf16[128,1024]{1,0:T(8,128)(2,1)} %get-tuple-element.178), channel_id=1, source_target_pairs={{0,2},{2,0},{4,6},{6,4},{1,3},{3,1},{5,7},{7,5},{8,10},{10,8},{12,... | collective-permute-start | bytes 786440 | tf_op jit(solution)/shard_map/ppermute | solution.py:69
  160.7 153.6 %all-gather.6.cloned.1.call-start = ((), (), s32[]{:S(2)}) async-start(), calls=%async_computation.5 | async-start | bytes 5242880 | tf_op jit(solution)/shard_map/all_gather | solution.py:342
  169.8 35.8 %collective-permute-start.13 = (bf16[256,2048]{1,0:T(8,128)(2,1)S(1)}, bf16[256,2048]{1,0:T(8,128)(2,1)S(1)}, u32[]{:S(2)}, u32[]{:S(2)}) collective-permute-start(bf16[256,2048]{1,0:T(8,128)(2,1)S(1)} %slice.348), channel_id=1, source_target_pairs={{0,2},{2,0},{4,6},{6,4},{1,3},{3,1},{5,7},{7,5},{8,10},{10,8},{12,... | collective-permute-start | bytes 3145736 | tf_op jit(solution)/shard_map/ppermute | solution.py:69
  170.0 33.6 %collective-permute-start.14 = (bf16[128,2048]{1,0:T(8,128)(2,1)S(1)}, bf16[128,2048]{1,0:T(8,128)(2,1)S(1)}, u32[]{:S(2)}, u32[]{:S(2)}) collective-permute-start(bf16[128,2048]{1,0:T(8,128)(2,1)S(1)} %dynamic-slice_bitcast_fusion.4), channel_id=1, source_target_pairs={{0,4},{2,6},{4,0},{6,2},{1,5},{3,7},{5,1},{7,3},{8,12},{10,14},{12... | collective-permute-start | bytes 1572872 | tf_op jit(solution)/shard_map/ppermute | solution.py:69
  206.7 35.1 %collective-permute-start.16 = (bf16[256,2048]{1,0:T(8,128)(2,1)}, bf16[256,2048]{1,0:T(8,128)(2,1)}, u32[]{:S(2)}, u32[]{:S(2)}) collective-permute-start(bf16[256,2048]{1,0:T(8,128)(2,1)} %pad_maximum_fusion.12), channel_id=1, source_target_pairs={{0,2},{2,0},{4,6},{6,4},{1,3},{3,1},{5,7},{7,5},{8,10},{10,8},{12,... | collective-permute-start | bytes 3145736 | tf_op jit(solution)/shard_map/ppermute | solution.py:69
  210.6 30.6 %collective-permute-start.15 = (bf16[128,2048]{1,0:T(8,128)(2,1)}, bf16[128,2048]{1,0:T(8,128)(2,1)}, u32[]{:S(2)}, u32[]{:S(2)}) collective-permute-start(bf16[128,2048]{1,0:T(8,128)(2,1)} %slice.352), channel_id=1, source_target_pairs={{0,4},{2,6},{4,0},{6,2},{1,5},{3,7},{5,1},{7,3},{8,12},{10,14},{12... | collective-permute-start | bytes 1572872 | tf_op jit(solution)/shard_map/ppermute | solution.py:69
  214.1 283.9 %reduce-scatter.5.cloned.1.call-start = ((), (), s32[]{:S(2)}) async-start(), calls=%async_computation.7 | async-start | bytes 10485760 | tf_op jit(solution)/shard_map/reduce_scatter | solution.py:435
  341.8 211.9 %reduce-scatter.7.cloned.1.call-start = ((), (), s32[]{:S(2)}) async-start(), calls=%async_computation.8 | async-start | bytes 5242880 | tf_op jit(solution)/shard_map/reduce_scatter | solution.py:435
  354.8 39.3 %collective-permute-start.24 = (bf16[512,2048]{1,0:T(8,128)(2,1)}, bf16[512,2048]{1,0:T(8,128)(2,1)}, u32[]{:S(2)}, u32[]{:S(2)}) collective-permute-start(bf16[512,2048]{1,0:T(8,128)(2,1)} %convolution_convert_fusion.2), channel_id=1, source_target_pairs={{0,1},{1,0},{2,3},{3,2},{4,5},{5,4},{6,7},{7,6},{8,9},{9,8},{10,11... | collective-permute-start | bytes 6291464 | tf_op jit(solution)/shard_map/ppermute | solution.py:72
  419.2 35.5 %collective-permute-start.25 = (bf16[256,2048]{1,0:T(8,128)(2,1)S(1)}, bf16[256,2048]{1,0:T(8,128)(2,1)S(1)}, u32[]{:S(2)}, u32[]{:S(2)}) collective-permute-start(bf16[256,2048]{1,0:T(8,128)(2,1)S(1)} %slice.346), channel_id=1, source_target_pairs={{0,2},{2,0},{4,6},{6,4},{1,3},{3,1},{5,7},{7,5},{8,10},{10,8},{12,... | collective-permute-start | bytes 3145736 | tf_op jit(solution)/shard_map/ppermute | solution.py:69
  420.9 31.9 %collective-permute-start.26 = (bf16[128,2048]{1,0:T(8,128)(2,1)S(1)}, bf16[128,2048]{1,0:T(8,128)(2,1)S(1)}, u32[]{:S(2)}, u32[]{:S(2)}) collective-permute-start(bf16[128,2048]{1,0:T(8,128)(2,1)S(1)} %get-tuple-element.137), channel_id=1, source_target_pairs={{0,4},{2,6},{4,0},{6,2},{1,5},{3,7},{5,1},{7,3},{8,12},{10,14},{12... | collective-permute-start | bytes 1572872 | tf_op jit(solution)/shard_map/ppermute | solution.py:69
  454.8 34.7 %collective-permute-start.28 = (bf16[256,2048]{1,0:T(8,128)(2,1)S(1)}, bf16[256,2048]{1,0:T(8,128)(2,1)S(1)}, u32[]{:S(2)}, u32[]{:S(2)}) collective-permute-start(bf16[256,2048]{1,0:T(8,128)(2,1)S(1)} %pad_maximum_fusion.15), channel_id=1, source_target_pairs={{0,2},{2,0},{4,6},{6,4},{1,3},{3,1},{5,7},{7,5},{8,10},{10,8},{12,... | collective-permute-start | bytes 3145736 | tf_op jit(solution)/shard_map/ppermute | solution.py:69
  457.6 31.0 %collective-permute-start.27 = (bf16[128,2048]{1,0:T(8,128)(2,1)S(1)}, bf16[128,2048]{1,0:T(8,128)(2,1)S(1)}, u32[]{:S(2)}, u32[]{:S(2)}) collective-permute-start(bf16[128,2048]{1,0:T(8,128)(2,1)S(1)} %slice.350), channel_id=1, source_target_pairs={{0,4},{2,6},{4,0},{6,2},{1,5},{3,7},{5,1},{7,3},{8,12},{10,14},{12... | collective-permute-start | bytes 1572872 | tf_op jit(solution)/shard_map/ppermute | solution.py:69
  498.0 104.0 %reduce-scatter.9.cloned.1.call-start = ((), (), s32[]{:S(2)}) async-start(), calls=%async_computation.9 | async-start | bytes 1310720 | tf_op jit(solution)/shard_map/reduce_scatter | solution.py:435
  500.9 57.5 %collective-permute-start.29 = (bf16[128,2048]{1,0:T(8,128)(2,1)}, bf16[128,2048]{1,0:T(8,128)(2,1)}, u32[]{:S(2)}, u32[]{:S(2)}) collective-permute-start(bf16[128,2048]{1,0:T(8,128)(2,1)} %fusion.23), channel_id=1, source_target_pairs={{0,1},{1,0},{2,3},{3,2},{4,5},{5,4},{6,7},{7,6},{8,9},{9,8},{10,11... | collective-permute-start | bytes 1572872 | tf_op jit(solution)/shard_map/ppermute | solution.py:72
  506.2 47.6 %collective-permute-start.32 = (bf16[128,2048]{1,0:T(8,128)(2,1)}, bf16[128,2048]{1,0:T(8,128)(2,1)}, u32[]{:S(2)}, u32[]{:S(2)}) collective-permute-start(bf16[128,2048]{1,0:T(8,128)(2,1)} %get-tuple-element.149), channel_id=1, source_target_pairs={{0,4},{2,6},{4,0},{6,2},{1,5},{3,7},{5,1},{7,3},{8,12},{10,14},{12... | collective-permute-start | bytes 1572872 | tf_op jit(solution)/shard_map/ppermute | solution.py:69
  507.4 46.3 %collective-permute-start.31 = (bf16[128,2048]{1,0:T(8,128)(2,1)}, bf16[128,2048]{1,0:T(8,128)(2,1)}, u32[]{:S(2)}, u32[]{:S(2)}) collective-permute-start(bf16[128,2048]{1,0:T(8,128)(2,1)} %get-tuple-element.150), channel_id=1, source_target_pairs={{0,2},{2,0},{4,6},{6,4},{1,3},{3,1},{5,7},{7,5},{8,10},{10,8},{12,... | collective-permute-start | bytes 1572872 | tf_op jit(solution)/shard_map/ppermute | solution.py:69
  563.4 90.5 %reduce-scatter.11.cloned.1.call-start = ((), (), s32[]{:S(2)}) async-start(), calls=%async_computation.10 | async-start | bytes 1966080 | tf_op jit(solution)/shard_map/reduce_scatter | solution.py:435
  593.7 37.5 %collective-permute-start.36 = (bf16[128,2048]{1,0:T(8,128)(2,1)}, bf16[128,2048]{1,0:T(8,128)(2,1)}, u32[]{:S(2)}, u32[]{:S(2)}) collective-permute-start(bf16[128,2048]{1,0:T(8,128)(2,1)} %slice.349), channel_id=1, source_target_pairs={{0,4},{2,6},{4,0},{6,2},{1,5},{3,7},{5,1},{7,3},{8,12},{10,14},{12... | collective-permute-start | bytes 1572872 | tf_op jit(solution)/shard_map/ppermute | solution.py:69
  598.0 34.4 %collective-permute-start.39 = (bf16[128,1024]{1,0:T(8,128)(2,1)}, bf16[128,1024]{1,0:T(8,128)(2,1)}, u32[]{:S(2)}, u32[]{:S(2)}) collective-permute-start(bf16[128,1024]{1,0:T(8,128)(2,1)} %get-tuple-element.166), channel_id=1, source_target_pairs={{0,6},{2,4},{4,2},{6,0},{1,7},{3,5},{5,3},{7,1},{8,14},{10,12},{12... | collective-permute-start | bytes 786440 | tf_op jit(solution)/shard_map/ppermute | solution.py:69
  599.3 43.1 %collective-permute-start.38 = (bf16[128,1024]{1,0:T(8,128)(2,1)}, bf16[128,1024]{1,0:T(8,128)(2,1)}, u32[]{:S(2)}, u32[]{:S(2)}) collective-permute-start(bf16[128,1024]{1,0:T(8,128)(2,1)} %get-tuple-element.167), channel_id=1, source_target_pairs={{0,4},{2,6},{4,0},{6,2},{1,5},{3,7},{5,1},{7,3},{8,12},{10,14},{12... | collective-permute-start | bytes 786440 | tf_op jit(solution)/shard_map/ppermute | solution.py:69
  600.6 41.8 %collective-permute-start.37 = (bf16[128,1024]{1,0:T(8,128)(2,1)}, bf16[128,1024]{1,0:T(8,128)(2,1)}, u32[]{:S(2)}, u32[]{:S(2)}) collective-permute-start(bf16[128,1024]{1,0:T(8,128)(2,1)} %get-tuple-element.168), channel_id=1, source_target_pairs={{0,2},{2,0},{4,6},{6,4},{1,3},{3,1},{5,7},{7,5},{8,10},{10,8},{12,... | collective-permute-start | bytes 786440 | tf_op jit(solution)/shard_map/ppermute | solution.py:69
  (84 other events, 1226.7 us)
Sparse Core Ops, SparseCore 0:
  48.3 48.9 all-gather.3
  160.8 87.7 all-gather.7
  251.1 52.6 all-gather.5
  341.9 86.0 reduce-scatter.4
  498.2 53.0 reduce-scatter.6
  563.5 27.0 reduce-scatter.8
  602.2 30.1 reduce-scatter.10

commit v3 on v2

--- a/solution.py
+++ b/solution.py
@@ -78,35 +78,28 @@
     def by_source(self, got):
         return [lax.select_n(self.c ^ j, *got) for j in range(self.n_c)]
 
-    def add_far(self, near, far):
-        return near.astype(WIDE) + self.swap(far).astype(WIDE)
+    def exchange_pieces(self, piece):
+        return [piece(mask) if mask == 0 else self.flip(piece(mask), mask) for mask in range(self.n_c)]
+
+    def of_device(self, rows, mask):
+        count = rows.shape[0] // (2 * self.n_c)
+        place = self.order.index(mask)
+        parts = [rows[(h * self.n_c + place) * count :][:count] for h in range(2)]
+        return jnp.concatenate(parts, axis=0)
 
     def with_far(self, near):
         return jnp.concatenate([near, self.swap(near)], axis=0)
 
-    def gather_near(self, near):
-        for bit in self.bits:
-            near = jnp.concatenate([near, self.flip(near, bit)], axis=0)
-        return near
-
-    def scatter_step(self, total, bit):
-        keep = total.shape[0] // 2
-        return total[:keep], self.flip(total[keep:].astype(LOW), bit)
-
-    def scatter_near(self, total):
-        for bit in reversed(self.bits):
-            kept, got = self.scatter_step(total, bit)
-            total = kept + got.astype(WIDE)
-        return total
-
-    def scatter_and_gather(self, total, near):
-        for low_bit, high_bit in zip(reversed(self.bits), self.bits):
-            kept, got = self.scatter_step(total, low_bit)
-            there = self.flip(near, high_bit)
-            got, there = lax.optimization_barrier((got, there))
-            total = kept + got.astype(WIDE)
-            near = jnp.concatenate([near, there], axis=0)
-        return total, near
+    def by_mask(self, near):
+        count = near.shape[0] // self.n_c
+        blocks = [near[i * count : (i + 1) * count] for i in range(self.n_c)]
+        return [blocks[self.order.index(mask)] for mask in range(self.n_c)]
+
+    def gather_step(self, near, place):
+        return self.flip(near, self.bits[place])
+
+    def scatter_step(self, send, place):
+        return self.flip(send, self.bits[-1 - place])
 
     def both_halves(self, mine):
         other = self.swap(mine)
@@ -182,9 +175,9 @@
 
 
 def attention_back_kernel(
-    prefix, limit_ref, key_pos_ref, cos_ref, sin_ref, kv_cos_ref, kv_sin_ref, log_ref, q_ref, kv_ref, grad_ref,
-    out_ref, keys, values, total,
+    prefix, limit_ref, key_pos_ref, cos_ref, sin_ref, kv_cos_ref, kv_sin_ref, log_ref, q_ref, kv_ref, *refs
 ):
+    pieces, (out_ref, keys, values, total, grad_all) = refs[:-5], refs[-5:]
     step = pl.program_id(0)
     width = q_ref.shape[1]
     rows = q_ref.shape[0]
@@ -199,13 +192,18 @@
         values[0] = pltpu.roll(second, HEAD_DIM, 1).astype(LOW)
         values[1] = second.astype(LOW)
         total[...] = jnp.zeros_like(total)
+        half = pieces[0].shape[0] // 2
+        for place, piece in enumerate(pieces):
+            for side in range(2):
+                first = (side * len(pieces) + place) * half
+                grad_all[first : first + half, :] = piece[side * half : (side + 1) * half, :]
 
     limit = jnp.maximum(limit_ref[...], prefix[0] - 1)
     key_pos = key_pos_ref[...]
     for pair in range(width // 128):
         lanes = slice(pair * 128, pair * 128 + 128)
         query = q_ref[:, lanes]
-        grad = grad_ref[:, lanes]
+        grad = grad_all[pl.ds(pl.multiple_of(step * rows, rows), rows), lanes]
         q_grad = None
         for side in range(2):
             head = 2 * pair + side
@@ -282,25 +280,157 @@
     )(*shared, qkv, qkv)
 
 
-def attention_back(query, kv, logs, grad, shared):
+def attention_back(query, kv, logs, pieces, shared):
     tokens, width = query.shape
     whole, per_row, specs = attention_specs(tokens, width, ROWS)
     return pl.pallas_call(
         attention_back_kernel,
         grid=(tokens // ROWS,),
         in_specs=specs
-        + [pl.BlockSpec((8, ROWS), lambda i: (0, i)), per_row(width), whole(tokens, 128), per_row(width)],
+        + [pl.BlockSpec((8, ROWS), lambda i: (0, i)), per_row(width), whole(tokens, 128)]
+        + [whole(*piece.shape) for piece in pieces],
         out_specs=whole(tokens, width + 128),
         out_shape=jax.ShapeDtypeStruct((tokens, width + 128), LOW),
         scratch_shapes=[
             pltpu.VMEM((2, tokens, 128), LOW),
             pltpu.VMEM((2, tokens, 128), LOW),
             pltpu.VMEM((tokens, 128), WIDE),
+            pltpu.VMEM((tokens, width), LOW),
         ],
         compiler_params=pltpu.CompilerParams(vmem_limit_bytes=40 << 20),
         cost_estimate=attention_cost(tokens, width, 5),
         name="attention_back",
-    )(*shared, logs, query, kv, grad)
+    )(*shared, logs, query, kv, *pieces)
+
+
+def feed_forward_kernel(*refs):
+    pieces, (cot_ref, gate_ref, up_ref, down_ref, inner_out, grad_out) = refs[:-6], refs[-6:]
+    hidden = grad_out.shape[1] // 2
+    place_gate = pl.ds(pl.multiple_of(pl.program_id(0) * HID, HID), HID)
+    place_up = pl.ds(pl.multiple_of(hidden + pl.program_id(0) * HID, HID), HID)
+    for place, piece in enumerate(pieces):
+        rows = slice(place * piece.shape[0], (place + 1) * piece.shape[0])
+        gate = dot_nn(piece[...], gate_ref[...])
+        up = dot_nn(piece[...], up_ref[...])
+        grad = dot_nn(cot_ref[rows, :], down_ref[...])
+        squash = lax.logistic(gate)
+        act = gate * squash
+        inner_out[rows, :] = (act * up).astype(LOW)
+        grad_out[rows, place_gate] = (grad * up * squash * (1.0 + gate * (1.0 - squash))).astype(LOW)
+        grad_out[rows, place_up] = (grad * act).astype(LOW)
+
+
+HID = 256
+
+
+def feed_forward(pieces, cot, gu, down):
+    tokens, width = cot.shape
+    hidden = down.shape[1]
+    once = lambda rows: pl.BlockSpec((rows, width), lambda j: (0, 0), pipeline_mode=pl.Buffered(1))
+    return pl.pallas_call(
+        feed_forward_kernel,
+        grid=(hidden // HID,),
+        in_specs=[once(piece.shape[0]) for piece in pieces]
+        + [
+            once(tokens),
+            pl.BlockSpec((width, HID), lambda j: (0, j)),
+            pl.BlockSpec((width, HID), lambda j: (0, j + hidden // HID)),
+            pl.BlockSpec((width, HID), lambda j: (0, j)),
+        ],
+        out_specs=[
+            pl.BlockSpec((tokens, HID), lambda j: (0, j)),
+            pl.BlockSpec((tokens, 2 * hidden), lambda j: (0, 0)),
+        ],
+        out_shape=[
+            jax.ShapeDtypeStruct((tokens, hidden), LOW),
+            jax.ShapeDtypeStruct((tokens, 2 * hidden), LOW),
+        ],
+        compiler_params=pltpu.CompilerParams(vmem_limit_bytes=48 << 20),
+        cost_estimate=pl.CostEstimate(
+            flops=6 * tokens * width * hidden, bytes_accessed=20 << 20, transcendentals=tokens * hidden
+        ),
+        name="feed_forward",
+    )(*pieces, cot, gu, gu, down)
+
+
+def far_kernel(left, right, out):
+    out[...] = dot_nt(left[...], right[...]).astype(LOW)
+
+
+def near_kernel(left, right, far, keep, send):
+    total = dot_nt(left[...], right[...]) + far[...].astype(WIDE)
+    keep[...] = total[: keep.shape[0]]
+    send[...] = total[keep.shape[0] :].astype(LOW)
+
+
+def partial_rows(g, left, right, depth):
+    rows = left.shape[0] // 2
+    width = right.shape[0]
+    cols = 256
+    grid = (width // cols,)
+    right_spec = pl.BlockSpec((cols, depth), lambda j: (j, 0))
+    out_spec = lambda count: pl.BlockSpec((count, cols), lambda j: (0, j))
+    params = pltpu.CompilerParams(vmem_limit_bytes=32 << 20)
+    cost = pl.CostEstimate(flops=2 * rows * width * depth, bytes_accessed=2 * width * depth, transcendentals=0)
+    far = pl.pallas_call(
+        far_kernel,
+        grid=grid,
+        in_specs=[pl.BlockSpec((rows, depth), lambda j: (1, 0)), right_spec],
+        out_specs=out_spec(rows),
+        out_shape=jax.ShapeDtypeStruct((rows, width), LOW),
+        compiler_params=params,
+        cost_estimate=cost,
+        name="far_rows",
+    )(left, right)
+    return pl.pallas_call(
+        near_kernel,
+        grid=grid,
+        in_specs=[pl.BlockSpec((rows, depth), lambda j: (0, 0)), right_spec, out_spec(rows)],
+        out_specs=[out_spec(rows // 2), out_spec(rows // 2)],
+        out_shape=[
+            jax.ShapeDtypeStruct((rows // 2, width), WIDE),
+            jax.ShapeDtypeStruct((rows // 2, width), LOW),
+        ],
+        compiler_params=params,
+        cost_estimate=cost,
+        name="near_rows",
+    )(left, right, g.swap(far))
+
+
+def own_kernel(left, right, far, out):
+    out[...] = dot_nt(left[...], right[...]) + far[...].astype(WIDE)
+
+
+def own_rows(g, left, right):
+    rows = left.shape[0] // 2
+    width, depth = right.shape[0], left.shape[1]
+    cols = 512
+    grid = (width // cols,)
+    left_spec = lambda place: pl.BlockSpec((rows, depth), lambda j: (place, 0))
+    right_spec = pl.BlockSpec((cols, depth), lambda j: (j, 0))
+    out_spec = pl.BlockSpec((rows, cols), lambda j: (0, j))
+    params = pltpu.CompilerParams(vmem_limit_bytes=32 << 20)
+    cost = pl.CostEstimate(flops=2 * rows * width * depth, bytes_accessed=2 * width * depth, transcendentals=0)
+    far = pl.pallas_call(
+        far_kernel,
+        grid=grid,
+        in_specs=[left_spec(1), right_spec],
+        out_specs=out_spec,
+        out_shape=jax.ShapeDtypeStruct((rows, width), LOW),
+        compiler_params=params,
+        cost_estimate=cost,
+        name="far_own",
+    )(left, right)
+    return pl.pallas_call(
+        own_kernel,
+        grid=grid,
+        in_specs=[left_spec(0), right_spec, out_spec],
+        out_specs=out_spec,
+        out_shape=jax.ShapeDtypeStruct((rows, width), WIDE),
+        compiler_params=params,
+        cost_estimate=cost,
+        name="own_rows",
+    )(left, right, g.swap(far))
 
 
 def by_dest(weight, count):
@@ -341,6 +471,10 @@
         def join_weight(got):
             return lax.all_gather(jnp.concatenate(g.by_source(got), axis=0), "fsdp", axis=0, tiled=True)
 
+        def joined(near, there):
+            return jnp.concatenate([near, there], axis=0)
+
+        steps = len(g.bits)
         x_mine = lax.dynamic_slice_in_dim(x_own, g.t * half, half, 0)
         cot_mine = lax.dynamic_slice_in_dim(cotangent[0], g.t * half, half, 0)
         q_cols = q_weight.shape[1] // n_c
@@ -349,87 +483,106 @@
         wide = q_cols + 2 * kv_cols
         gains = jnp.pad(jnp.stack([attn_gain, mlp_gain], axis=1).astype(LOW), ((0, 0), (0, 126)))
         gain_blocks = jnp.broadcast_to(gains[None], (n_c, *gains.shape))
-        attn_got = g.exchange(
-            jnp.concatenate(
-                [by_dest(q_weight, n_c), *kv_blocks, gain_blocks, by_dest(output_weight, n_c)], axis=2
-            )
-        )
-        x_near = x_mine
-        for place, bit in enumerate(g.bits):
-            there = g.flip(x_near, bit)
+        qkv_got = g.exchange(jnp.concatenate([by_dest(q_weight, n_c), *kv_blocks, gain_blocks], axis=2))
+        o_near = output_weight.astype(LOW)
+        beside = g.gather_step(o_near, 0)
+        beside, qkv_got = lax.optimization_barrier((beside, qkv_got))
+        qkv_full = join_weight(qkv_got)
+        hid = gate_weight.shape[1] // n_c
+        gate_late, up_late = after((gate_weight, up_weight), qkv_got)
+        gu_blocks = jnp.concatenate([by_dest(gate_late, n_c), by_dest(up_late, n_c)], axis=2)
+        gu_got = g.exchange(gu_blocks)
+        for place in range(1, steps):
+            o_near = joined(o_near, beside)
+            beside = g.gather_step(o_near, place)
+        beside, gu_got = lax.optimization_barrier((beside, gu_got))
+        o_full = join_weight(g.by_mask(joined(o_near, beside)))
+        gu_full = join_weight(gu_got)
+        x_near = after(x_mine, beside)
+        for place in range(steps):
+            there = g.gather_step(x_near, place)
             if place == 0:
-                there, *attn_got = lax.optimization_barrier((there, *attn_got))
-                gu_got = g.exchange(
-                    after(
-                        jnp.concatenate([by_dest(gate_weight, n_c), by_dest(up_weight, n_c)], axis=2), there
-                    )
+                block = after((g.c ^ jnp.array(g.order, jnp.int32)) * local, gu_got)
+                side = jnp.stack([g.t, 1 - g.t]).astype(jnp.int32) * half
+                positions = (
+                    side[:, None, None] + block[None, :, None] + jnp.arange(half, dtype=jnp.int32)[None, None, :]
+                ).reshape(-1)
+                cos_table, sin_table = rope_tables(positions, HEAD_DIM)
+                half_dim = HEAD_DIM // 2
+                sin_table = jnp.concatenate([-sin_table[:, :half_dim], sin_table[:, half_dim:]], axis=1)
+                tables = (
+                    prefix,
+                    positions[None, :],
+                    positions[:, None],
+                    jnp.tile(cos_table, (1, 2)),
+                    jnp.tile(sin_table, (1, 2)),
+                    jnp.concatenate([cos_table, jnp.ones_like(cos_table)], axis=1),
+                    jnp.concatenate([sin_table, jnp.zeros_like(sin_table)], axis=1),
                 )
-            x_near = jnp.concatenate([x_near, there], axis=0)
-        attn_full = join_weight(attn_got)
+                down_blocks = by_dest(after(down_weight, gu_got), n_c)
+                there, tables, down_blocks = lax.optimization_barrier((there, tables, down_blocks))
+                down_got = g.exchange(down_blocks)
+            if place == steps - 1:
+                there, down_got = lax.optimization_barrier((there, down_got))
+            x_near = joined(x_near, there)
+        down_full = join_weight(down_got)
+        cot_near = after(cot_mine, x_near)
+        cot_got = g.gather_step(cot_near, 0)
         x_all = g.with_far(x_near)
-        gains_all = attn_full[:, wide : wide + 2].T.astype(WIDE)
-        qkv_full = attn_full[:, :wide]
-        o_full = attn_full[:, wide + 128 :]
+        gains_all = qkv_full[:, wide : wide + 2].T.astype(WIDE)
         gain_one, gain_two = gains_all[0:1], gains_all[1:2]
-
-        block = (g.c ^ jnp.array(g.order, jnp.int32)) * local
-        side = jnp.stack([g.t, 1 - g.t]).astype(jnp.int32) * half
-        positions = (
-            side[:, None, None] + block[None, :, None] + jnp.arange(half, dtype=jnp.int32)[None, None, :]
-        ).reshape(-1)
-        cos_table, sin_table = rope_tables(positions, HEAD_DIM)
-        half_dim = HEAD_DIM // 2
-        sin_table = jnp.concatenate([-sin_table[:, :half_dim], sin_table[:, half_dim:]], axis=1)
-        tables = (
-            prefix,
-            positions[None, :],
-            positions[:, None],
-            jnp.tile(cos_table, (1, 2)),
-            jnp.tile(sin_table, (1, 2)),
-            jnp.concatenate([cos_table, jnp.ones_like(cos_table)], axis=1),
-            jnp.concatenate([sin_table, jnp.zeros_like(sin_table)], axis=1),
-        )
 
         hidden_in = x_all.astype(WIDE)
         rms_one = inverse_rms(hidden_in)
         normed_one = (hidden_in * rms_one * gain_one).astype(LOW)
-        qkv = matmul(normed_one, qkv_full)
-        down_got = g.exchange(after(by_dest(down_weight, n_c), qkv))
+        qkv = matmul(normed_one, qkv_full[:, :wide])
         query_rot, kv_rot, attended, logs = attention(qkv, tables)
-        gu_got, down_got, attended = lax.optimization_barrier((gu_got, down_got, attended))
-        gu_full = join_weight(gu_got)
-        down_full = join_weight(down_got)
-        near_rows = n_c * half
-        far_part = matmul_t(attended[near_rows:], o_full).astype(LOW)
-        near_part = matmul_t(attended[:near_rows], o_full)
+        attended, cot_got = lax.optimization_barrier((attended, cot_got))
+        mixed_own = jnp.concatenate(
+            g.by_source(g.exchange_pieces(lambda mask: g.of_device(attended, mask))), axis=1
+        )
         x_mine = x_mine.astype(WIDE)
-        branch, cot_near = g.scatter_and_gather(g.add_far(near_part, far_part), after(cot_mine, attended))
-        cot_all = g.with_far(cot_near)
-        resid = x_mine + branch
+        resid = x_mine + own_rows(g, mixed_own, o_full)
         rms_two = inverse_rms(resid)
-        normed_two = g.with_far(g.gather_near((resid * rms_two * gain_two).astype(LOW)))
-
-        gate_up = matmul(normed_two, gu_full)
-        hid = gate_up.shape[1] // 2
-        gate_proj, up_proj = gate_up[:, :hid], gate_up[:, hid:]
-        squash = jax.nn.sigmoid(gate_proj)
-        inner = (gate_proj * squash * up_proj).astype(LOW)
-        grad_inner = matmul(cot_all, down_full)
-        grad_gate = grad_inner * up_proj * squash * (1.0 + gate_proj * (1.0 - squash))
-        grad_up = grad_inner * gate_proj * squash
-        grad_gu = jnp.concatenate([grad_gate.astype(LOW), grad_up.astype(LOW)], axis=1)
-        far_grad = matmul_t(grad_gu[near_rows:], gu_full).astype(LOW)
-        near_grad = matmul_t(grad_gu[:near_rows], gu_full)
-        gu_part = outer(normed_two, grad_gu).astype(LOW)
-        down_part = outer(cot_all, inner).astype(LOW)
-        far_out = matmul_t(inner[near_rows:], down_full).astype(LOW)
-        near_out = matmul_t(inner[:near_rows], down_full)
-        out_total = g.add_far(near_out, far_out)
-        grad_normed_two = g.scatter_near(g.add_far(near_grad, far_grad))
-        grad_normed_two, _, _, out_total = lax.optimization_barrier(
-            (grad_normed_two, gu_part, down_part, out_total)
-        )
-        grad_resid = cot_mine.astype(WIDE) + norm_reverse(resid, rms_two, gain_two, grad_normed_two)
+
+        def gather_pieces(near, beside=None):
+            for place in range(steps - 1):
+                there = g.gather_step(near, place)
+                if beside is not None:
+                    there = beside(there, place)
+                near = joined(near, there)
+            there = g.gather_step(near, steps - 1)
+            if beside is not None:
+                there = beside(there, steps - 1)
+            return near, there, g.swap(near), g.swap(there)
+
+        state = {"cot": joined(cot_near, cot_got)}
+
+        def with_cot(there, place):
+            if place < steps - 1:
+                there, beside = lax.optimization_barrier((there, g.gather_step(state["cot"], place + 1)))
+                state["cot"] = joined(state["cot"], beside)
+            return there
+
+        n2_pieces = gather_pieces((resid * rms_two * gain_two).astype(LOW), with_cot)
+        n2_pieces, gu_full = lax.optimization_barrier((n2_pieces, gu_full))
+        cot_all = g.with_far(state["cot"])
+        normed_two = jnp.concatenate(n2_pieces, axis=0)
+
+        inner, grad_gu = feed_forward(n2_pieces, cot_all, gu_full, down_full)
+        keep, send = partial_rows(g, grad_gu, gu_full, 2 * hid)
+        gu_part = outer(normed_two, after(grad_gu, send)).astype(LOW)
+        for place in range(steps):
+            got = g.scatter_step(send, place)
+            if place == 0:
+                out_keep, out_send = partial_rows(g, after(inner, gu_part), down_full, hid)
+                got, out_send = lax.optimization_barrier((got, out_send))
+                down_part = outer(cot_all, after(inner, got)).astype(LOW)
+            if place == steps - 1:
+                got, out_got, _ = lax.optimization_barrier((got, g.scatter_step(out_send, 0), down_part))
+            total = keep + got.astype(WIDE)
+            keep, send = total[: total.shape[0] // 2], total[total.shape[0] // 2 :].astype(LOW)
+        grad_resid = cot_mine.astype(WIDE) + norm_reverse(resid, rms_two, gain_two, total)
 
         def sum_weight(part):
             return lax.psum_scatter(part, "fsdp", scatter_dimension=0, tiled=True)
@@ -438,35 +591,52 @@
             return g.exchange(mine.reshape(n_c, rows, mine.shape[1]))
 
         gu_sum = sum_weight(gu_part)
-        out_sum, branch_near = g.scatter_and_gather(out_total, grad_resid.astype(LOW))
-        branch_all = g.with_far(branch_near)
-        branch_all, gu_sum = lax.optimization_barrier((branch_all, gu_sum))
-        down_sum = sum_weight(after(down_part, gu_sum))
-        layer_output = g.both_halves((resid + out_sum).astype(LOW))
-        gu_got = return_weight(gu_sum)
-
+        down_sum = sum_weight(down_part)
         def cols(blocks, start, size):
             return jnp.concatenate([b[:, start : start + size] for b in blocks], axis=1).astype(WIDE)
 
-        grad_att = matmul(branch_all, o_full).astype(LOW)
-        o_part = outer(branch_all, attended).astype(LOW)
+        branch_mine = grad_resid.astype(LOW)
+        for place in range(1, steps):
+            out_total = out_keep + out_got.astype(WIDE)
+            cut = out_total.shape[0] // 2
+            out_keep, out_got = out_total[:cut], g.scatter_step(out_total[cut:].astype(LOW), place)
+        branch_far, out_got = lax.optimization_barrier((g.swap(branch_mine), out_got))
+        branch_own = joined(branch_mine, branch_far)
+        grad_mixed = matmul(branch_own, o_full).astype(LOW)
+        o_part = outer(branch_own, mixed_own).astype(LOW)
+        grad_att = g.exchange_pieces(
+            lambda mask: lax.dynamic_slice_in_dim(grad_mixed, (g.c ^ mask) * q_cols, q_cols, 1)
+        )
+        grad_att = [grad_att[mask] for mask in g.order]
+        grad_att, _, gu_sum = lax.optimization_barrier((grad_att, o_part, gu_sum))
+        o_sum = sum_weight(o_part)
+        gu_got = return_weight(gu_sum)
         grad_qkv = attention_back(query_rot, kv_rot, logs, grad_att, tables)
-        o_sum = sum_weight(after(o_part, down_sum))
         qkv_part = outer(normed_one, grad_qkv).astype(LOW)
-        grad_qkv, down_sum, _, *gu_got = lax.optimization_barrier((grad_qkv, down_sum, qkv_part, *gu_got))
-        qkv_sum = sum_weight(after(qkv_part, o_sum))
+        grad_qkv, gu_got, down_sum, _ = lax.optimization_barrier((grad_qkv, gu_got, down_sum, qkv_part))
+        qkv_sum = sum_weight(qkv_part)
+        down_got = return_weight(down_sum)
+        keep, send = partial_rows(g, grad_qkv, qkv_full, wide)
+        for place in range(steps):
+            got = g.scatter_step(send, place)
+            if place == 0:
+                got, down_got, o_sum = lax.optimization_barrier((got, down_got, o_sum))
+                o_got = return_weight(o_sum)
+            if place == steps - 1:
+                got, o_got, qkv_sum = lax.optimization_barrier((got, o_got, qkv_sum))
+            total = keep + got.astype(WIDE)
+            keep, send = total[: total.shape[0] // 2], total[total.shape[0] // 2 :].astype(LOW)
+        out_total = out_keep + out_got.astype(WIDE)
+        layer_output = g.both_halves((resid + out_total).astype(LOW))
+        grad_normed_one = total
+
         gu_blocks = g.by_source(gu_got)
         gate_grad = cols(gu_blocks, 0, hid)
         up_grad = cols(gu_blocks, hid, hid)
-        down_got = return_weight(down_sum)
-        far_one = matmul_t(grad_qkv[near_rows:], qkv_full).astype(LOW)
-        near_one = matmul_t(grad_qkv[:near_rows], qkv_full)
-        grad_normed_one = g.scatter_near(g.add_far(near_one, far_one))
-        grad_normed_one, o_sum, *down_got = lax.optimization_barrier((grad_normed_one, o_sum, *down_got))
         down_grad = cols(g.by_source(down_got), 0, hid)
-        o_grad = cols(g.by_source(return_weight(o_sum)), 0, q_cols)
         qkv_blocks = g.by_source(return_weight(qkv_sum))
         q_grad = cols(qkv_blocks, 0, q_cols)
+        o_grad = sum(block.astype(WIDE) for block in o_got)
 
         def kv_grad(start):
             parts = [b[:, start : start + kv_cols].astype(WIDE) for b in qkv_blocks]

time: 687 us -> 662 us (0.964)
  matrix products: 96.2 us -> 36.2 us
  Pallas kernels: 27.1 us -> 84 us
  waiting for transfers between devices: 366 us -> 328 us
  local copies, waits for them, and re-layouts: 43.1 us -> 61.4 us
    pallas_call x0 -> x9, Pallas kernels: none -> 57.2 us  [the longest x1 20.3 us: feed_forward(): pl.pallas_call(feed_forward_kernel, grid=(hidden // HID,), in_specs=[once...]
    ppermute x37 -> x41, waiting for transfers between devices: 353 us -> 319 us  [flip(): lax.ppermute(block, 'context', [(i, i ^ mask) for i in range(self.n_c)])]
    dot_general x8 -> x0, matrix products: 34.3 us -> none  [matmul_t(): lax.dot_general(left, right, (((1,), (1,)), ((), ())), preferred_element_...]
    dot_general x4 -> x2, matrix products: 35.7 us -> 7.88 us  [matmul(): lax.dot_general(left, right, (((1,), (0,)), ((), ())), preferred_element_...]
    unnamed x134 -> x208, local copies, waits for them, and re-layouts: 25.5 us -> 41.5 us
    ppermute x37 -> x41, starting transfers between devices: 63.1 us -> 64.1 us  [flip(): lax.ppermute(block, 'context', [(i, i ^ mask) for i in range(self.n_c)])]
    ppermute x12 -> x13, starting transfers between devices: 14.4 us -> 14.5 us  [swap(): return lax.ppermute(block, 'tensor', [(0, 1), (1, 0)])]
  transfers between devices with their start and end apart: 56 -> 62, of which waited for: 27 -> 32; matrix products, arithmetic and copies ran while one was open for 21% -> 14% of each run, Pallas kernels for 4% -> 8%
where the time goes in v3:
time: 662 us; the launch traced here: 654 us
  waiting for transfers between devices  328 us (50%)
  Pallas kernels  84 us (13%)
  starting transfers between devices  79.3 us (12%)
  local copies, waits for them, and re-layouts  61.4 us (9%)
  other arithmetic  49.4 us (7%)
  matrix products  36.2 us (5%)
  between operations  16.5 us (2%)
    ppermute x41, waiting for transfers between devices, flip(): lax.ppermute(block, 'context', [(i, i ^ mask) for i in range(self.n_c)])  319 us
    ppermute x41, starting transfers between devices, flip(): lax.ppermute(block, 'context', [(i, i ^ mask) for i in range(self.n_c)])  64.1 us
    unnamed x208, local copies, waits for them, and re-layouts  41.5 us
    dot_general x4, matrix products, outer(): lax.dot_general(left, right, (((0,), (0,)), ((), ())), preferred_element_...  28.3 us
    pallas_call x1, Pallas kernels, feed_forward(): pl.pallas_call(feed_forward_kernel, grid=(hidden // HID,), in_specs=[once...  20.3 us
    pallas_call x3, Pallas kernels, partial_rows(): pl.pallas_call(near_kernel, grid=grid, in_specs=[pl.BlockSpec((rows, dept...  17.7 us
    pallas_call x1, Pallas kernels, attention_back(): pl.pallas_call(attention_back_kernel, grid=(tokens // ROWS,), in_specs=sp...  15.4 us
    pallas_call x3, Pallas kernels, partial_rows(): pl.pallas_call(far_kernel, grid=grid, in_specs=[pl.BlockSpec((rows, depth...  15 us
  transfers between devices with their start and end apart: 62, of which 32 were waited for; matrix products, arithmetic and copies ran while one was open for 14% of the time, Pallas kernels for 8%

profile of v3, /device:TPU:1, one launch (start us, length us, event | category | flops | bytes accessed | tf_op | source)
XLA Modules:
  0.0 654.5 jit_solution(422185336004844883)
XLA Ops:
  23.0 11.4 %collective-permute-done.2 = bf16[128,512]{1,0:T(8,128)(2,1)S(1)} collective-permute-done((bf16[128,512]{1,0:T(8,128)(2,1)S(1)}, bf16[128,512]{1,0:T(8,128)(2,1)S(1)}, u32[]{:S(2)}, u32[]{:S(2)}) %collective-permute-start.2) | collective-permute-done | bytes 131104 | tf_op jit(solution)/shard_map/ppermute | solution.py:69
  41.8 5.9 collective-permute-done.4
  47.7 14.9 %collective-permute-done.7 = bf16[128,2048]{1,0:T(8,128)(2,1)S(1)} collective-permute-done((bf16[128,2048]{1,0:T(8,128)(2,1)S(1)}, bf16[128,2048]{1,0:T(8,128)(2,1)S(1)}, u32[]{:S(2)}, u32[]{:S(2)}) %collective-permute-start.7) | collective-permute-done | bytes 524320 | tf_op jit(solution)/shard_map/ppermute | solution.py:69
  62.6 17.9 %collective-permute-done.5 = bf16[128,2048]{1,0:T(8,128)(2,1)S(1)} collective-permute-done((bf16[128,2048]{1,0:T(8,128)(2,1)S(1)}, bf16[128,2048]{1,0:T(8,128)(2,1)S(1)}, u32[]{:S(2)}, u32[]{:S(2)}) %collective-permute-start.5) | collective-permute-done | bytes 524320 | tf_op jit(solution)/shard_map/ppermute | solution.py:69
  96.4 17.3 %collective-permute-done.8 = bf16[128,2048]{1,0:T(8,128)(2,1)S(1)} collective-permute-done((bf16[128,2048]{1,0:T(8,128)(2,1)S(1)}, bf16[128,2048]{1,0:T(8,128)(2,1)S(1)}, u32[]{:S(2)}, u32[]{:S(2)}) %collective-permute-start.8) | collective-permute-done | bytes 524320 | tf_op jit(solution)/shard_map/ppermute | solution.py:69
  123.2 26.2 %collective-permute-done.12 = bf16[128,1024]{1,0:T(8,128)(2,1)S(1)} collective-permute-done((bf16[128,1024]{1,0:T(8,128)(2,1)S(1)}, bf16[128,1024]{1,0:T(8,128)(2,1)S(1)}, u32[]{:S(2)}, u32[]{:S(2)}) %collective-permute-start.12) | collective-permute-done | bytes 262176 | tf_op jit(solution)/shard_map/ppermute | solution.py:69
  151.1 5.6 collective-permute-done.10
  173.7 4.1 fusion.10.q_ref.kv_ref
  177.9 11.5 %attention.1 = (bf16[1024,256]{1,0:T(8,128)(2,1)S(1)}, bf16[1024,128]{1,0:T(8,128)(2,1)S(1)}, bf16[1024,256]{1,0:T(8,128)(2,1)S(1)}, f32[8,1024]{1,0:T(8,128)S(1)}) custom-call(s32[1]{0:T(128)S(6)} %copy.71.prefix, s32[1,1024]{1,0:T(1,128)S(1)} %bitcast.124, s32[1024,1]{1,0:T(8,128)S(1)} %copy.43.key_pos_ref, f32[1024,128]{1,0:T(8,128)S(1)} %copy-done.21, ...), custom_call_target="tpu_custom_call" | custom-call | flops 2147483648 | bytes 3145728 | tf_op jit(solution)/shard_map/attention/pallas_call | solution.py:264
  196.9 5.6 collective-permute-done.17
  217.9 30.7 %collective-permute-done.20 = bf16[256,2048]{1,0:T(8,128)(2,1)S(1)} collective-permute-done((bf16[256,2048]{1,0:T(8,128)(2,1)S(1)}, bf16[256,2048]{1,0:T(8,128)(2,1)S(1)}, u32[]{:S(2)}, u32[]{:S(2)}) %collective-permute-start.20) | collective-permute-done | bytes 1048608 | tf_op jit(solution)/shard_map/ppermute | solution.py:69
  253.3 23.3 %collective-permute-done.21.refs_1_ = bf16[256,2048]{1,0:T(8,128)(2,1)S(1)} collective-permute-done((bf16[256,2048]{1,0:T(8,128)(2,1)S(1)}, bf16[256,2048]{1,0:T(8,128)(2,1)S(1)}, u32[]{:S(2)}, u32[]{:S(2)}) %collective-permute-start.21) | collective-permute-done | bytes 1048608 | tf_op jit(solution)/shard_map/ppermute | solution.py:69
  290.2 20.3 %feed_forward.1 = (bf16[1024,1024]{1,0:T(8,128)(2,1)}, bf16[1024,2048]{1,0:T(8,128)(2,1)}) custom-call(bf16[256,2048]{1,0:T(8,128)(2,1)S(1)} %copy-done.15, bf16[256,2048]{1,0:T(8,128)(2,1)S(1)} %copy-done.29, bf16[256,2048]{1,0:T(8,128)(2,1)S(1)} %copy-done.32, bf16[256,2048]{1,0:T(8,128)(2,1)S(1)} %copy-done.35, bf16[1024,2048]{1,0:T(8,128)(2,1)} %copy-done.88, ...), custom_call_target="tpu_custom_call" | custom-call | flops 12884901888 | bytes 20971520 | tf_op jit(solution)/shard_map/feed_forward/pallas_call | solution.py:330
  312.8 6.4 far_rows.3
  323.7 6.5 near_rows.3
  332.6 13.5 %convolution_convert_fusion = bf16[2048,2048]{1,0:T(8,128)(2,1)} fusion(bf16[1024,2048]{1,0:T(8,128)(2,1)} %get-tuple-element.137.left, bf16[256,2048]{1,0:T(8,128)(2,1)S(1)} %copy-done.36, bf16[256,2048]{1,0:T(8,128)(2,1)S(1)} %copy-done.33, bf16[256,2048]{1,0:T(8,128)(2,1)S(1)} %copy-done.30, bf16[256,2048]{1,0:T(8,128)(2,1)S(1)} %copy-done.16), kind=kOutput, calls=%fused_computation.5 | convolution fusion | flops 8610906112 | bytes 16777216 | tf_op jit(solution)/shard_map/dot_general | solution.py:40
  358.2 4.4 near_rows.4
  364.8 14.3 %collective-permute-done.27 = bf16[256,2048]{1,0:T(8,128)(2,1)S(1)} collective-permute-done((bf16[256,2048]{1,0:T(8,128)(2,1)S(1)}, bf16[256,2048]{1,0:T(8,128)(2,1)S(1)}, u32[]{:S(2)}, u32[]{:S(2)}) %collective-permute-start.27) | collective-permute-done | bytes 1048608 | tf_op jit(solution)/shard_map/ppermute | solution.py:69
  380.1 6.2 convolution_convert_fusion.2
  392.1 28.5 %collective-permute-done.28 = bf16[128,2048]{1,0:T(8,128)(2,1)S(1)} collective-permute-done((bf16[128,2048]{1,0:T(8,128)(2,1)S(1)}, bf16[128,2048]{1,0:T(8,128)(2,1)S(1)}, u32[]{:S(2)}, u32[]{:S(2)}) %collective-permute-start.28) | collective-permute-done | bytes 524320 | tf_op jit(solution)/shard_map/ppermute | solution.py:69
  429.9 16.6 %collective-permute-done.31 = bf16[128,2048]{1,0:T(8,128)(2,1)} collective-permute-done((bf16[128,2048]{1,0:T(8,128)(2,1)S(1)}, bf16[128,2048]{1,0:T(8,128)(2,1)}, u32[]{:S(2)}, u32[]{:S(2)}) %collective-permute-start.31) | collective-permute-done | bytes 524320 | tf_op jit(solution)/shard_map/ppermute | solution.py:69
  455.0 5.1 collective-permute-start.35
  462.9 5.6 collective-permute-done.34.refs_2_
  477.7 15.4 %attention_back.1.left = bf16[1024,384]{1,0:T(8,128)(2,1)S(1)} custom-call(s32[1]{0:T(128)S(6)} %copy.71.prefix, s32[1,1024]{1,0:T(1,128)S(1)} %bitcast.125, s32[1024,1]{1,0:T(8,128)S(1)} %copy-done.20, f32[1024,128]{1,0:T(8,128)S(1)} %copy-done.22, f32[1024,128]{1,0:T(8,128)S(1)} %copy-done.24, f32[1024,128]{1,0:T(8,128)S(1)} %copy-done.26, ...), custom_call_target="tpu_custom_call" | custom-call | flops 5368709120 | bytes 3145728 | tf_op jit(solution)/shard_map/attention_back/pallas_call | solution.py:286
  493.1 5.4 convolution_convert_fusion.3
  499.4 20.5 %collective-permute-done.37 = bf16[128,2048]{1,0:T(8,128)(2,1)} collective-permute-done((bf16[128,2048]{1,0:T(8,128)(2,1)}, bf16[128,2048]{1,0:T(8,128)(2,1)}, u32[]{:S(2)}, u32[]{:S(2)}) %collective-permute-start.37) | collective-permute-done | bytes 524320 | tf_op jit(solution)/shard_map/ppermute | solution.py:69
  521.1 4.6 far_rows.5
  536.1 6.8 %near_rows.5 = (f32[256,2048]{1,0:T(8,128)S(1)}, bf16[256,2048]{1,0:T(8,128)(2,1)}) custom-call(bf16[1024,384]{1,0:T(8,128)(2,1)S(1)} %copy-done.8, bf16[2048,512]{1,0:T(8,128)(2,1)S(1)} %copy-done.2, bf16[512,2048]{1,0:T(8,128)(2,1)} %collective-permute-done.39.far), custom_call_target="tpu_custom_call" | custom-call | flops 805306368 | bytes 1572864 | tf_op jit(solution)/shard_map/near_rows/pallas_call | solution.py:385
  549.9 4.3 collective-permute-done.42
  554.2 18.6 %collective-permute-done.40 = bf16[256,2048]{1,0:T(8,128)(2,1)} collective-permute-done((bf16[256,2048]{1,0:T(8,128)(2,1)}, bf16[256,2048]{1,0:T(8,128)(2,1)}, u32[]{:S(2)}, u32[]{:S(2)}) %collective-permute-start.40) | collective-permute-done | bytes 1048608 | tf_op jit(solution)/shard_map/ppermute | solution.py:69
  585.2 26.9 %collective-permute-done.46 = bf16[128,1024]{1,0:T(8,128)(2,1)} collective-permute-done((bf16[128,1024]{1,0:T(8,128)(2,1)}, bf16[128,1024]{1,0:T(8,128)(2,1)}, u32[]{:S(2)}, u32[]{:S(2)}) %collective-permute-start.46) | collective-permute-done | bytes 262176 | tf_op jit(solution)/shard_map/ppermute | solution.py:69
  612.0 11.1 %collective-permute-done.44 = bf16[128,2048]{1,0:T(8,128)(2,1)S(1)} collective-permute-done((bf16[128,2048]{1,0:T(8,128)(2,1)}, bf16[128,2048]{1,0:T(8,128)(2,1)S(1)}, u32[]{:S(2)}, u32[]{:S(2)}) %collective-permute-start.44) | collective-permute-done | bytes 524320 | tf_op jit(solution)/shard_map/ppermute | solution.py:69
  (449 shorter events, 222.7 us)
Async XLA Ops:
  7.2 161.0 %all-gather.5.cloned.1.call-start = ((), (), s32[]{:S(2)}) async-start(), calls=%async_computation.4 | async-start | bytes 2621440 | tf_op jit(solution)/shard_map/all_gather | solution.py:472
  8.3 26.1 %collective-permute-start = (bf16[128,1024]{1,0:T(8,128)(2,1)S(1)}, bf16[128,1024]{1,0:T(8,128)(2,1)S(1)}, u32[]{:S(2)}, u32[]{:S(2)}) collective-permute-start(bf16[128,1024]{1,0:T(8,128)(2,1)S(1)} %convert_element_type.165), channel_id=1, source_target_pairs={{0,4},{2,6},{4,0},{6,2},{1,5},{3,7},{5,1},{7,3},{8,12},{10,14},{12... | collective-permute-start | bytes 786440 | tf_op jit(solution)/shard_map/ppermute | solution.py:69
  35.3 168.0 %all-gather.7.cloned.1.call-start = ((), (), s32[]{:S(2)}) async-start(), calls=%async_computation.5 | async-start | bytes 5242880 | tf_op jit(solution)/shard_map/all_gather | solution.py:472
  37.4 25.2 %collective-permute-start.7 = (bf16[128,2048]{1,0:T(8,128)(2,1)S(1)}, bf16[128,2048]{1,0:T(8,128)(2,1)S(1)}, u32[]{:S(2)}, u32[]{:S(2)}) collective-permute-start(bf16[128,2048]{1,0:T(8,128)(2,1)S(1)} %get-tuple-element.210), channel_id=1, source_target_pairs={{0,6},{2,4},{4,2},{6,0},{1,7},{3,5},{5,3},{7,1},{8,14},{10,12},{12... | collective-permute-start | bytes 1572872 | tf_op jit(solution)/shard_map/ppermute | solution.py:69
  41.5 39.1 %collective-permute-start.5 = (bf16[128,2048]{1,0:T(8,128)(2,1)S(1)}, bf16[128,2048]{1,0:T(8,128)(2,1)S(1)}, u32[]{:S(2)}, u32[]{:S(2)}) collective-permute-start(bf16[128,2048]{1,0:T(8,128)(2,1)S(1)} %get-tuple-element.212), channel_id=1, source_target_pairs={{0,2},{2,0},{4,6},{6,4},{1,3},{3,1},{5,7},{7,5},{8,10},{10,8},{12,... | collective-permute-start | bytes 1572872 | tf_op jit(solution)/shard_map/ppermute | solution.py:69
  41.5 39.8 %collective-permute-start.6 = (bf16[128,2048]{1,0:T(8,128)(2,1)S(1)}, bf16[128,2048]{1,0:T(8,128)(2,1)S(1)}, u32[]{:S(2)}, u32[]{:S(2)}) collective-permute-start(bf16[128,2048]{1,0:T(8,128)(2,1)S(1)} %get-tuple-element.213), channel_id=1, source_target_pairs={{0,4},{2,6},{4,0},{6,2},{1,5},{3,7},{5,1},{7,3},{8,12},{10,14},{12... | collective-permute-start | bytes 1572872 | tf_op jit(solution)/shard_map/ppermute | solution.py:69
  82.5 201.1 %all-gather.9.cloned.1.call-start = ((), (), s32[]{:S(2)}) async-start(), calls=%async_computation.6 | async-start | bytes 10485760 | tf_op jit(solution)/shard_map/all_gather | solution.py:472
  84.4 200.9 %all-gather.11.cloned.1.call-start = ((), (), s32[]{:S(2)}) async-start(), calls=%async_computation.7 | async-start | bytes 5242880 | tf_op jit(solution)/shard_map/all_gather | solution.py:472
  113.9 42.9 %collective-permute-start.9 = (bf16[256,2048]{1,0:T(8,128)(2,1)S(1)}, bf16[256,2048]{1,0:T(8,128)(2,1)S(1)}, u32[]{:S(2)}, u32[]{:S(2)}) collective-permute-start(bf16[256,2048]{1,0:T(8,128)(2,1)S(1)} %pad_maximum_fusion.3), channel_id=1, source_target_pairs={{0,2},{2,0},{4,6},{6,4},{1,3},{3,1},{5,7},{7,5},{8,10},{10,8},{12,... | collective-permute-start | bytes 3145736 | tf_op jit(solution)/shard_map/ppermute | solution.py:69
  117.9 31.4 %collective-permute-start.12 = (bf16[128,1024]{1,0:T(8,128)(2,1)S(1)}, bf16[128,1024]{1,0:T(8,128)(2,1)S(1)}, u32[]{:S(2)}, u32[]{:S(2)}) collective-permute-start(bf16[128,1024]{1,0:T(8,128)(2,1)S(1)} %get-tuple-element.237), channel_id=1, source_target_pairs={{0,6},{2,4},{4,2},{6,0},{1,7},{3,5},{5,3},{7,1},{8,14},{10,12},{12... | collective-permute-start | bytes 786440 | tf_op jit(solution)/shard_map/ppermute | solution.py:69
  120.9 30.3 %collective-permute-start.11 = (bf16[128,1024]{1,0:T(8,128)(2,1)S(1)}, bf16[128,1024]{1,0:T(8,128)(2,1)S(1)}, u32[]{:S(2)}, u32[]{:S(2)}) collective-permute-start(bf16[128,1024]{1,0:T(8,128)(2,1)S(1)} %get-tuple-element.238), channel_id=1, source_target_pairs={{0,4},{2,6},{4,0},{6,2},{1,5},{3,7},{5,1},{7,3},{8,12},{10,14},{12... | collective-permute-start | bytes 786440 | tf_op jit(solution)/shard_map/ppermute | solution.py:69
  121.2 35.6 %collective-permute-start.10 = (bf16[128,1024]{1,0:T(8,128)(2,1)S(1)}, bf16[128,1024]{1,0:T(8,128)(2,1)S(1)}, u32[]{:S(2)}, u32[]{:S(2)}) collective-permute-start(bf16[128,1024]{1,0:T(8,128)(2,1)S(1)} %get-tuple-element.239), channel_id=1, source_target_pairs={{0,2},{2,0},{4,6},{6,4},{1,3},{3,1},{5,7},{7,5},{8,10},{10,8},{12,... | collective-permute-start | bytes 786440 | tf_op jit(solution)/shard_map/ppermute | solution.py:69
  162.9 26.8 %collective-permute-start.14 = (bf16[128,2048]{1,0:T(8,128)(2,1)}, bf16[128,2048]{1,0:T(8,128)(2,1)}, u32[]{:S(2)}, u32[]{:S(2)}) collective-permute-start(bf16[128,2048]{1,0:T(8,128)(2,1)} %get-tuple-element.120), channel_id=1, source_target_pairs={{0,4},{2,6},{4,0},{6,2},{1,5},{3,7},{5,1},{7,3},{8,12},{10,14},{12... | collective-permute-start | bytes 1572872 | tf_op jit(solution)/shard_map/ppermute | solution.py:69
  168.2 302.8 %reduce-scatter.5.cloned.1.call-start = ((), (), s32[]{:S(2)}) async-start(), calls=%async_computation.8 | async-start | bytes 10485760 | tf_op jit(solution)/shard_map/reduce_scatter | solution.py:588
  211.5 37.0 %collective-permute-start.20 = (bf16[256,2048]{1,0:T(8,128)(2,1)S(1)}, bf16[256,2048]{1,0:T(8,128)(2,1)S(1)}, u32[]{:S(2)}, u32[]{:S(2)}) collective-permute-start(bf16[256,2048]{1,0:T(8,128)(2,1)S(1)} %pad_maximum_fusion.5), channel_id=1, source_target_pairs={{0,2},{2,0},{4,6},{6,4},{1,3},{3,1},{5,7},{7,5},{8,10},{10,8},{12,... | collective-permute-start | bytes 3145736 | tf_op jit(solution)/shard_map/ppermute | solution.py:69
  216.8 31.7 %collective-permute-start.19 = (bf16[128,2048]{1,0:T(8,128)(2,1)S(1)}, bf16[128,2048]{1,0:T(8,128)(2,1)S(1)}, u32[]{:S(2)}, u32[]{:S(2)}) collective-permute-start(bf16[128,2048]{1,0:T(8,128)(2,1)S(1)} %multiply_convert_fusion), channel_id=1, source_target_pairs={{0,4},{2,6},{4,0},{6,2},{1,5},{3,7},{5,1},{7,3},{8,12},{10,14},{12... | collective-permute-start | bytes 1572872 | tf_op jit(solution)/shard_map/ppermute | solution.py:69
  249.9 29.5 %collective-permute-start.24 = (bf16[512,2048]{1,0:T(8,128)(2,1)S(1)}, bf16[512,2048]{1,0:T(8,128)(2,1)S(1)}, u32[]{:S(2)}, u32[]{:S(2)}) collective-permute-start(bf16[512,2048]{1,0:T(8,128)(2,1)S(1)} %pad_maximum_fusion.2), channel_id=1, source_target_pairs={{0,1},{1,0},{2,3},{3,2},{4,5},{5,4},{6,7},{7,6},{8,9},{9,8},{10,11... | collective-permute-start | bytes 6291464 | tf_op jit(solution)/shard_map/ppermute | solution.py:72
  250.6 26.1 %collective-permute-start.21 = (bf16[256,2048]{1,0:T(8,128)(2,1)S(1)}, bf16[256,2048]{1,0:T(8,128)(2,1)S(1)}, u32[]{:S(2)}, u32[]{:S(2)}) collective-permute-start(bf16[256,2048]{1,0:T(8,128)(2,1)S(1)} %pad_maximum_fusion.6.refs_0_), channel_id=1, source_target_pairs={{0,2},{2,0},{4,6},{6,4},{1,3},{3,1},{5,7},{7,5},{8,10},{10,8},{12,... | collective-permute-start | bytes 3145736 | tf_op jit(solution)/shard_map/ppermute | solution.py:69
  253.0 26.6 %collective-permute-start.22 = (bf16[256,2048]{1,0:T(8,128)(2,1)S(1)}, bf16[256,2048]{1,0:T(8,128)(2,1)S(1)}, u32[]{:S(2)}, u32[]{:S(2)}) collective-permute-start(bf16[256,2048]{1,0:T(8,128)(2,1)S(1)} %pad_maximum_fusion.6.refs_0_), channel_id=1, source_target_pairs={{0,1},{1,0},{2,3},{3,2},{4,5},{5,4},{6,7},{7,6},{8,9},{9,8},{10,11... | collective-permute-start | bytes 3145736 | tf_op jit(solution)/shard_map/ppermute | solution.py:72
  346.1 153.3 %reduce-scatter.7.cloned.1.call-start = ((), (), s32[]{:S(2)}) async-start(), calls=%async_computation.9 | async-start | bytes 5242880 | tf_op jit(solution)/shard_map/reduce_scatter | solution.py:588
  354.4 24.7 %collective-permute-start.27 = (bf16[256,2048]{1,0:T(8,128)(2,1)S(1)}, bf16[256,2048]{1,0:T(8,128)(2,1)S(1)}, u32[]{:S(2)}, u32[]{:S(2)}) collective-permute-start(bf16[256,2048]{1,0:T(8,128)(2,1)S(1)} %copy-done.38), channel_id=1, source_target_pairs={{0,2},{2,0},{4,6},{6,4},{1,3},{3,1},{5,7},{7,5},{8,10},{10,8},{12,... | collective-permute-start | bytes 3145736 | tf_op jit(solution)/shard_map/ppermute | solution.py:69
  386.3 163.7 %reduce-scatter.9.cloned.1.call-start = ((), (), s32[]{:S(2)}) async-start(), calls=%async_computation.10 | async-start | bytes 5242880 | tf_op jit(solution)/shard_map/reduce_scatter | solution.py:588
  386.3 35.4 %collective-permute-start.29 = (bf16[256,2048]{1,0:T(8,128)(2,1)}, bf16[256,2048]{1,0:T(8,128)(2,1)S(1)}, u32[]{:S(2)}, u32[]{:S(2)}) collective-permute-start(bf16[256,2048]{1,0:T(8,128)(2,1)} %copy-done.39), channel_id=1, source_target_pairs={{0,2},{2,0},{4,6},{6,4},{1,3},{3,1},{5,7},{7,5},{8,10},{10,8},{12,... | collective-permute-start | bytes 3145736 | tf_op jit(solution)/shard_map/ppermute | solution.py:69
  389.9 30.7 %collective-permute-start.28 = (bf16[128,2048]{1,0:T(8,128)(2,1)S(1)}, bf16[128,2048]{1,0:T(8,128)(2,1)S(1)}, u32[]{:S(2)}, u32[]{:S(2)}) collective-permute-start(bf16[128,2048]{1,0:T(8,128)(2,1)S(1)} %slice.253), channel_id=1, source_target_pairs={{0,4},{2,6},{4,0},{6,2},{1,5},{3,7},{5,1},{7,3},{8,12},{10,14},{12... | collective-permute-start | bytes 1572872 | tf_op jit(solution)/shard_map/ppermute | solution.py:69
  450.7 134.5 %reduce-scatter.11.cloned.1.call-start = ((), (), s32[]{:S(2)}) async-start(), calls=%async_computation.11 | async-start | bytes 1966080 | tf_op jit(solution)/shard_map/reduce_scatter | solution.py:588
  474.0 25.3 %collective-permute-start.38 = (bf16[128,2048]{1,0:T(8,128)(2,1)}, bf16[128,2048]{1,0:T(8,128)(2,1)}, u32[]{:S(2)}, u32[]{:S(2)}) collective-permute-start(bf16[128,2048]{1,0:T(8,128)(2,1)} %get-tuple-element.202), channel_id=1, source_target_pairs={{0,6},{2,4},{4,2},{6,0},{1,7},{3,5},{5,3},{7,1},{8,14},{10,12},{12... | collective-permute-start | bytes 1572872 | tf_op jit(solution)/shard_map/ppermute | solution.py:69
  474.7 45.2 %collective-permute-start.37 = (bf16[128,2048]{1,0:T(8,128)(2,1)}, bf16[128,2048]{1,0:T(8,128)(2,1)}, u32[]{:S(2)}, u32[]{:S(2)}) collective-permute-start(bf16[128,2048]{1,0:T(8,128)(2,1)} %get-tuple-element.203), channel_id=1, source_target_pairs={{0,4},{2,6},{4,0},{6,2},{1,5},{3,7},{5,1},{7,3},{8,12},{10,14},{12... | collective-permute-start | bytes 1572872 | tf_op jit(solution)/shard_map/ppermute | solution.py:69
  475.0 44.9 %collective-permute-start.36 = (bf16[128,2048]{1,0:T(8,128)(2,1)}, bf16[128,2048]{1,0:T(8,128)(2,1)}, u32[]{:S(2)}, u32[]{:S(2)}) collective-permute-start(bf16[128,2048]{1,0:T(8,128)(2,1)} %get-tuple-element.204), channel_id=1, source_target_pairs={{0,2},{2,0},{4,6},{6,4},{1,3},{3,1},{5,7},{7,5},{8,10},{10,8},{12,... | collective-permute-start | bytes 1572872 | tf_op jit(solution)/shard_map/ppermute | solution.py:69
  543.0 29.8 %collective-permute-start.40 = (bf16[256,2048]{1,0:T(8,128)(2,1)}, bf16[256,2048]{1,0:T(8,128)(2,1)}, u32[]{:S(2)}, u32[]{:S(2)}) collective-permute-start(bf16[256,2048]{1,0:T(8,128)(2,1)} %get-tuple-element.159), channel_id=1, source_target_pairs={{0,2},{2,0},{4,6},{6,4},{1,3},{3,1},{5,7},{7,5},{8,10},{10,8},{12,... | collective-permute-start | bytes 3145736 | tf_op jit(solution)/shard_map/ppermute | solution.py:69
  577.5 34.5 %collective-permute-start.46 = (bf16[128,1024]{1,0:T(8,128)(2,1)}, bf16[128,1024]{1,0:T(8,128)(2,1)}, u32[]{:S(2)}, u32[]{:S(2)}) collective-permute-start(bf16[128,1024]{1,0:T(8,128)(2,1)} %get-tuple-element.221), channel_id=1, source_target_pairs={{0,4},{2,6},{4,0},{6,2},{1,5},{3,7},{5,1},{7,3},{8,12},{10,14},{12... | collective-permute-start | bytes 786440 | tf_op jit(solution)/shard_map/ppermute | solution.py:69
  577.6 34.5 %collective-permute-start.45 = (bf16[128,1024]{1,0:T(8,128)(2,1)}, bf16[128,1024]{1,0:T(8,128)(2,1)}, u32[]{:S(2)}, u32[]{:S(2)}) collective-permute-start(bf16[128,1024]{1,0:T(8,128)(2,1)} %get-tuple-element.222), channel_id=1, source_target_pairs={{0,2},{2,0},{4,6},{6,4},{1,3},{3,1},{5,7},{7,5},{8,10},{10,8},{12,... | collective-permute-start | bytes 786440 | tf_op jit(solution)/shard_map/ppermute | solution.py:69
  581.0 42.2 %collective-permute-start.44 = (bf16[128,2048]{1,0:T(8,128)(2,1)}, bf16[128,2048]{1,0:T(8,128)(2,1)S(1)}, u32[]{:S(2)}, u32[]{:S(2)}) collective-permute-start(bf16[128,2048]{1,0:T(8,128)(2,1)} %slice.251), channel_id=1, source_target_pairs={{0,4},{2,6},{4,0},{6,2},{1,5},{3,7},{5,1},{7,3},{8,12},{10,14},{12... | collective-permute-start | bytes 1572872 | tf_op jit(solution)/shard_map/ppermute | solution.py:69
  (128 other events, 1226.9 us)
Sparse Core Ops, SparseCore 0:
  35.4 37.0 all-gather.4
  82.7 58.1 all-gather.6
  143.2 87.5 all-gather.8
  232.6 52.6 all-gather.10
  346.2 86.0 reduce-scatter.4
  435.4 52.7 reduce-scatter.6
  491.1 52.6 reduce-scatter.8
  547.1 30.9 reduce-scatter.10

commit v4 on v3

--- a/solution.py
+++ b/solution.py
@@ -65,8 +65,40 @@
         for bit in self.bits:
             self.order = self.order + [o ^ bit for o in self.order]
 
-    def flip(self, block, mask):
-        return lax.ppermute(block, "context", [(i, i ^ mask) for i in range(self.n_c)])
+    def flip(self, block, mask, axis="context"):
+        return lax.ppermute(block, axis, [(i, i ^ mask) for i in range(lax.axis_size(axis))])
+
+    def fsdp_parts(self, part):
+        f = lax.axis_index("fsdp")
+        blocks = part.reshape(self.n_f, part.shape[0] // self.n_f, part.shape[1])
+        blocks = [lax.dynamic_index_in_dim(blocks, f ^ mask, 0, keepdims=False) for mask in range(self.n_f)]
+        cut = blocks[0].shape[0] // 2
+        return [{mask: b[:cut] for mask, b in enumerate(blocks)}, {mask: b[cut:] for mask, b in enumerate(blocks)}]
+
+    def fsdp_bits(self, place):
+        count = self.n_f.bit_length() - 1
+        return (1 << place, self.n_f >> (place + 1)) if count else ()
+
+    def fsdp_send(self, parts, place):
+        sent = []
+        for part, bit in zip(parts, self.fsdp_bits(place)):
+            away = [part[mask].astype(LOW) for mask in sorted(part) if mask & bit]
+            sent.append(self.flip(jnp.concatenate(away, axis=0), bit, "fsdp"))
+        return sent
+
+    def fsdp_add(self, parts, sent, place):
+        out = []
+        for part, got, bit in zip(parts, sent, self.fsdp_bits(place)):
+            kept = [mask for mask in sorted(part) if not mask & bit]
+            count = got.shape[0] // len(kept)
+            order = sorted(mask | bit for mask in kept)
+            out.append(
+                {
+                    mask: part[mask].astype(WIDE) + got[order.index(mask | bit) * count :][:count].astype(WIDE)
+                    for mask in kept
+                }
+            )
+        return out
 
     def swap(self, block):
         return lax.ppermute(block, "tensor", [(0, 1), (1, 0)])
@@ -483,7 +515,9 @@
         wide = q_cols + 2 * kv_cols
         gains = jnp.pad(jnp.stack([attn_gain, mlp_gain], axis=1).astype(LOW), ((0, 0), (0, 126)))
         gain_blocks = jnp.broadcast_to(gains[None], (n_c, *gains.shape))
-        qkv_got = g.exchange(jnp.concatenate([by_dest(q_weight, n_c), *kv_blocks, gain_blocks], axis=2))
+        qkv_blocks = jnp.concatenate([by_dest(q_weight, n_c), *kv_blocks], axis=2)
+        qkv_rows = qkv_blocks.transpose(1, 0, 2).reshape(rows, n_c * wide)
+        qkv_got = g.exchange(jnp.concatenate([qkv_blocks, gain_blocks], axis=2))
         o_near = output_weight.astype(LOW)
         beside = g.gather_step(o_near, 0)
         beside, qkv_got = lax.optimization_barrier((beside, qkv_got))
@@ -522,12 +556,19 @@
                 down_blocks = by_dest(after(down_weight, gu_got), n_c)
                 there, tables, down_blocks = lax.optimization_barrier((there, tables, down_blocks))
                 down_got = g.exchange(down_blocks)
+                qkv_rows = after(qkv_rows, there)
+                back_got = g.gather_step(qkv_rows, 0)
             if place == steps - 1:
-                there, down_got = lax.optimization_barrier((there, down_got))
+                there, down_got, back_got = lax.optimization_barrier((there, down_got, back_got))
             x_near = joined(x_near, there)
         down_full = join_weight(down_got)
         cot_near = after(cot_mine, x_near)
         cot_got = g.gather_step(cot_near, 0)
+        back_near = after(joined(qkv_rows, back_got), x_near)
+        for place in range(1, steps):
+            back_got = g.gather_step(back_near, place)
+            if place < steps - 1:
+                back_near = joined(back_near, back_got)
         x_all = g.with_far(x_near)
         gains_all = qkv_full[:, wide : wide + 2].T.astype(WIDE)
         gain_one, gain_two = gains_all[0:1], gains_all[1:2]
@@ -537,7 +578,7 @@
         normed_one = (hidden_in * rms_one * gain_one).astype(LOW)
         qkv = matmul(normed_one, qkv_full[:, :wide])
         query_rot, kv_rot, attended, logs = attention(qkv, tables)
-        attended, cot_got = lax.optimization_barrier((attended, cot_got))
+        attended, cot_got, back_got = lax.optimization_barrier((attended, cot_got, back_got))
         mixed_own = jnp.concatenate(
             g.by_source(g.exchange_pieces(lambda mask: g.of_device(attended, mask))), axis=1
         )
@@ -556,7 +597,7 @@
                 there = beside(there, steps - 1)
             return near, there, g.swap(near), g.swap(there)
 
-        state = {"cot": joined(cot_near, cot_got)}
+        state = {"cot": joined(cot_near, cot_got), "back": joined(back_near, back_got)}
 
         def with_cot(there, place):
             if place < steps - 1:
@@ -565,10 +606,12 @@
             return there
 
         n2_pieces = gather_pieces((resid * rms_two * gain_two).astype(LOW), with_cot)
+        back_near = state["back"]
         n2_pieces, gu_full = lax.optimization_barrier((n2_pieces, gu_full))
         cot_all = g.with_far(state["cot"])
         normed_two = jnp.concatenate(n2_pieces, axis=0)
 
+        back_full = join_weight(g.by_mask(back_near))
         inner, grad_gu = feed_forward(n2_pieces, cot_all, gu_full, down_full)
         keep, send = partial_rows(g, grad_gu, gu_full, 2 * hid)
         gu_part = outer(normed_two, after(grad_gu, send)).astype(LOW)
@@ -576,7 +619,7 @@
             got = g.scatter_step(send, place)
             if place == 0:
                 out_keep, out_send = partial_rows(g, after(inner, gu_part), down_full, hid)
-                got, out_send = lax.optimization_barrier((got, out_send))
+                got, out_send, back_full = lax.optimization_barrier((got, out_send, back_full))
                 down_part = outer(cot_all, after(inner, got)).astype(LOW)
             if place == steps - 1:
                 got, out_got, _ = lax.optimization_barrier((got, g.scatter_step(out_send, 0), down_part))
@@ -591,7 +634,8 @@
             return g.exchange(mine.reshape(n_c, rows, mine.shape[1]))
 
         gu_sum = sum_weight(gu_part)
-        down_sum = sum_weight(down_part)
+        down_sums = g.fsdp_parts(down_part)
+        stages = g.n_f.bit_length() - 1
         def cols(blocks, start, size):
             return jnp.concatenate([b[:, start : start + size] for b in blocks], axis=1).astype(WIDE)
 
@@ -600,7 +644,11 @@
             out_total = out_keep + out_got.astype(WIDE)
             cut = out_total.shape[0] // 2
             out_keep, out_got = out_total[:cut], g.scatter_step(out_total[cut:].astype(LOW), place)
-        branch_far, out_got = lax.optimization_barrier((g.swap(branch_mine), out_got))
+        for place in range(stages - 1):
+            sent = g.fsdp_send(down_sums, place)
+            down_sums = g.fsdp_add(down_sums, sent, place)
+        branch_far, out_got, down_sums = lax.optimization_barrier((g.swap(branch_mine), out_got, down_sums))
+        down_sent = g.fsdp_send(down_sums, stages - 1)
         branch_own = joined(branch_mine, branch_far)
         grad_mixed = matmul(branch_own, o_full).astype(LOW)
         o_part = outer(branch_own, mixed_own).astype(LOW)
@@ -608,24 +656,22 @@
             lambda mask: lax.dynamic_slice_in_dim(grad_mixed, (g.c ^ mask) * q_cols, q_cols, 1)
         )
         grad_att = [grad_att[mask] for mask in g.order]
-        grad_att, _, gu_sum = lax.optimization_barrier((grad_att, o_part, gu_sum))
+        grad_att, _, gu_sum, down_sent = lax.optimization_barrier((grad_att, o_part, gu_sum, down_sent))
+        down_sums = g.fsdp_add(down_sums, down_sent, stages - 1)
+        down_sum = jnp.concatenate([part[0].astype(LOW) for part in down_sums], axis=0)
         o_sum = sum_weight(o_part)
         gu_got = return_weight(gu_sum)
         grad_qkv = attention_back(query_rot, kv_rot, logs, grad_att, tables)
         qkv_part = outer(normed_one, grad_qkv).astype(LOW)
-        grad_qkv, gu_got, down_sum, _ = lax.optimization_barrier((grad_qkv, gu_got, down_sum, qkv_part))
+        grad_qkv, gu_got, o_sum, _ = lax.optimization_barrier((grad_qkv, gu_got, o_sum, qkv_part))
+        o_got = return_weight(o_sum)
         qkv_sum = sum_weight(qkv_part)
         down_got = return_weight(down_sum)
-        keep, send = partial_rows(g, grad_qkv, qkv_full, wide)
-        for place in range(steps):
-            got = g.scatter_step(send, place)
-            if place == 0:
-                got, down_got, o_sum = lax.optimization_barrier((got, down_got, o_sum))
-                o_got = return_weight(o_sum)
-            if place == steps - 1:
-                got, o_got, qkv_sum = lax.optimization_barrier((got, o_got, qkv_sum))
-            total = keep + got.astype(WIDE)
-            keep, send = total[: total.shape[0] // 2], total[total.shape[0] // 2 :].astype(LOW)
+        grad_own = jnp.concatenate(
+            g.by_source(g.exchange_pieces(lambda mask: g.of_device(grad_qkv, mask))), axis=1
+        )
+        total = own_rows(g, grad_own, back_full)
+        total, down_got, o_got = lax.optimization_barrier((total, down_got, o_got))
         out_total = out_keep + out_got.astype(WIDE)
         layer_output = g.both_halves((resid + out_total).astype(LOW))
         grad_normed_one = total

time: 662 us -> 639 us (0.965)
  waiting for transfers between devices: 328 us -> 291 us
  starting transfers between devices: 79.3 us -> 106 us
  local copies, waits for them, and re-layouts: 61.4 us -> 52.1 us
    ppermute x41 -> x48, waiting for transfers between devices: 319 us -> 277 us  [flip(): lax.ppermute(block, axis, [(i, i ^ mask) for i in range(lax.axis_size(axi...]
    ppermute x41 -> x48, starting transfers between devices: 64.1 us -> 77.6 us  [flip(): lax.ppermute(block, axis, [(i, i ^ mask) for i in range(lax.axis_size(axi...]
    ppermute x13, starting transfers between devices: 14.5 us -> 26.7 us  [swap(): return lax.ppermute(block, 'tensor', [(0, 1), (1, 0)])]
    unnamed x208 -> x200, local copies, waits for them, and re-layouts: 41.5 us -> 37.2 us
    pallas_call x3 -> x2, Pallas kernels: 17.7 us -> 13.6 us  [partial_rows(): pl.pallas_call(near_kernel, grid=grid, in_specs=[pl.BlockSpec((rows, dept...]
    pallas_call x3 -> x2, Pallas kernels: 15 us -> 11.4 us  [partial_rows(): pl.pallas_call(far_kernel, grid=grid, in_specs=[pl.BlockSpec((rows, depth...]
  transfers between devices with their start and end apart: 62 -> 69, of which waited for: 32 -> 30; matrix products, arithmetic and copies ran while one was open for 14% -> 17% of each run, Pallas kernels for 8% -> 13%
where the time goes in v4:
time: 639 us; the launch traced here: 632 us
  waiting for transfers between devices  291 us (46%)
  starting transfers between devices  106 us (17%)
  Pallas kernels  82.1 us (13%)
  other arithmetic  52.1 us (8%)
  local copies, waits for them, and re-layouts  52.1 us (8%)
  matrix products  32.6 us (5%)
  between operations  16.8 us (3%)
    ppermute x48, waiting for transfers between devices, flip(): lax.ppermute(block, axis, [(i, i ^ mask) for i in range(lax.axis_size(axi...  277 us
    ppermute x48, starting transfers between devices, flip(): lax.ppermute(block, axis, [(i, i ^ mask) for i in range(lax.axis_size(axi...  77.6 us
    unnamed x200, local copies, waits for them, and re-layouts  37.2 us
    ppermute x13, starting transfers between devices, swap(): return lax.ppermute(block, 'tensor', [(0, 1), (1, 0)])  26.7 us
    dot_general x4, matrix products, outer(): lax.dot_general(left, right, (((0,), (0,)), ((), ())), preferred_element_...  25 us
    pallas_call x1, Pallas kernels, feed_forward(): pl.pallas_call(feed_forward_kernel, grid=(hidden // HID,), in_specs=[once...  20.3 us
    pallas_call x1, Pallas kernels, attention_back(): pl.pallas_call(attention_back_kernel, grid=(tokens // ROWS,), in_specs=sp...  15.6 us
    pallas_call x2, Pallas kernels, partial_rows(): pl.pallas_call(near_kernel, grid=grid, in_specs=[pl.BlockSpec((rows, dept...  13.6 us
  transfers between devices with their start and end apart: 69, of which 30 were waited for; matrix products, arithmetic and copies ran while one was open for 17% of the time, Pallas kernels for 13%

profile of v4, /device:TPU:1, one launch (start us, length us, event | category | flops | bytes accessed | tf_op | source)
XLA Modules:
  0.0 632.2 jit_solution(8262947055969791597)
XLA Ops:
  20.6 5.6 collective-permute-done.1
  26.2 5.4 collective-permute-done.2
  41.8 18.0 %collective-permute-done.4 = bf16[256,1024]{1,0:T(8,128)(2,1)S(1)} collective-permute-done((bf16[256,1024]{1,0:T(8,128)(2,1)S(1)}, bf16[256,1024]{1,0:T(8,128)(2,1)S(1)}, u32[]{:S(2)}, u32[]{:S(2)}) %collective-permute-start.4) | collective-permute-done | bytes 524320 | tf_op jit(solution)/shard_map/ppermute | solution.py:69
  59.8 11.3 %collective-permute-done.5 = bf16[128,2048]{1,0:T(8,128)(2,1)S(1)} collective-permute-done((bf16[128,2048]{1,0:T(8,128)(2,1)S(1)}, bf16[128,2048]{1,0:T(8,128)(2,1)S(1)}, u32[]{:S(2)}, u32[]{:S(2)}) %collective-permute-start.5) | collective-permute-done | bytes 524320 | tf_op jit(solution)/shard_map/ppermute | solution.py:69
  71.2 13.9 %collective-permute-done.7 = bf16[128,2048]{1,0:T(8,128)(2,1)S(1)} collective-permute-done((bf16[128,2048]{1,0:T(8,128)(2,1)S(1)}, bf16[128,2048]{1,0:T(8,128)(2,1)S(1)}, u32[]{:S(2)}, u32[]{:S(2)}) %collective-permute-start.7) | collective-permute-done | bytes 524320 | tf_op jit(solution)/shard_map/ppermute | solution.py:69
  100.9 16.4 %collective-permute-done.8 = bf16[128,2048]{1,0:T(8,128)(2,1)S(1)} collective-permute-done((bf16[128,2048]{1,0:T(8,128)(2,1)S(1)}, bf16[128,2048]{1,0:T(8,128)(2,1)S(1)}, u32[]{:S(2)}, u32[]{:S(2)}) %collective-permute-start.8) | collective-permute-done | bytes 524320 | tf_op jit(solution)/shard_map/ppermute | solution.py:69
  124.2 43.6 %collective-permute-done.10 = bf16[128,1024]{1,0:T(8,128)(2,1)S(1)} collective-permute-done((bf16[128,1024]{1,0:T(8,128)(2,1)S(1)}, bf16[128,1024]{1,0:T(8,128)(2,1)S(1)}, u32[]{:S(2)}, u32[]{:S(2)}) %collective-permute-start.10) | collective-permute-done | bytes 262176 | tf_op jit(solution)/shard_map/ppermute | solution.py:69
  186.0 11.5 %attention.1 = (bf16[1024,256]{1,0:T(8,128)(2,1)S(1)}, bf16[1024,128]{1,0:T(8,128)(2,1)S(1)}, bf16[1024,256]{1,0:T(8,128)(2,1)S(1)}, f32[8,1024]{1,0:T(8,128)S(1)}) custom-call(s32[1]{0:T(128)S(6)} %copy.72.prefix, s32[1,1024]{1,0:T(1,128)S(1)} %bitcast.159, s32[1024,1]{1,0:T(8,128)S(1)} %copy.43.key_pos_ref, f32[1024,128]{1,0:T(8,128)S(1)} %copy.44.cos_ref, ...), custom_call_target="tpu_custom_call" | custom-call | flops 2147483648 | bytes 3145728 | tf_op jit(solution)/shard_map/attention/pallas_call | solution.py:296
  199.8 7.7 %collective-permute-done.16 = bf16[256,1536]{1,0:T(8,128)(2,1)} collective-permute-done((bf16[256,1536]{1,0:T(8,128)(2,1)}, bf16[256,1536]{1,0:T(8,128)(2,1)}, u32[]{:S(2)}, u32[]{:S(2)}) %collective-permute-start.16) | collective-permute-done | bytes 786464 | tf_op jit(solution)/shard_map/ppermute | solution.py:69
  236.1 28.5 %collective-permute-done.22 = bf16[256,2048]{1,0:T(8,128)(2,1)} collective-permute-done((bf16[256,2048]{1,0:T(8,128)(2,1)}, bf16[256,2048]{1,0:T(8,128)(2,1)}, u32[]{:S(2)}, u32[]{:S(2)}) %collective-permute-start.22) | collective-permute-done | bytes 1048608 | tf_op jit(solution)/shard_map/ppermute | solution.py:69
  267.7 24.1 %collective-permute-done.23.refs_1_ = bf16[256,2048]{1,0:T(8,128)(2,1)S(1)} collective-permute-done((bf16[256,2048]{1,0:T(8,128)(2,1)S(1)}, bf16[256,2048]{1,0:T(8,128)(2,1)S(1)}, u32[]{:S(2)}, u32[]{:S(2)}) %collective-permute-start.23) | collective-permute-done | bytes 1048608 | tf_op jit(solution)/shard_map/ppermute | solution.py:69
  301.8 20.3 %feed_forward.1 = (bf16[1024,1024]{1,0:T(8,128)(2,1)}, bf16[1024,2048]{1,0:T(8,128)(2,1)}) custom-call(bf16[256,2048]{1,0:T(8,128)(2,1)S(1)} %pad_maximum_fusion.7.refs_0_, bf16[256,2048]{1,0:T(8,128)(2,1)S(1)} %collective-permute-done.23.refs_1_, bf16[256,2048]{1,0:T(8,128)(2,1)S(1)} %copy-done.20, bf16[256,2048]{1,0:T(8,128)(2,1)S(1)} %copy-done.25, ...), custom_call_target="tpu_custom_call" | custom-call | flops 12884901888 | bytes 20971520 | tf_op jit(solution)/shard_map/feed_forward/pallas_call | solution.py:362
  325.2 6.2 far_rows.2
  335.7 7.1 %near_rows.2 = (f32[256,2048]{1,0:T(8,128)S(1)}, bf16[256,2048]{1,0:T(8,128)(2,1)}) custom-call(bf16[1024,2048]{1,0:T(8,128)(2,1)S(1)} %copy-done.28, bf16[2048,2048]{1,0:T(8,128)(2,1)S(1)} %copy-done.18, bf16[512,2048]{1,0:T(8,128)(2,1)S(1)} %collective-permute-done.27.far), custom_call_target="tpu_custom_call" | custom-call | flops 4294967296 | bytes 8388608 | tf_op jit(solution)/shard_map/near_rows/pallas_call | solution.py:417
  344.1 11.4 %convolution_convert_fusion = bf16[2048,2048]{1,0:T(8,128)(2,1)} fusion(bf16[1024,2048]{1,0:T(8,128)(2,1)S(1)} %copy-done.28, bf16[256,2048]{1,0:T(8,128)(2,1)S(1)} %copy-done.26, bf16[256,2048]{1,0:T(8,128)(2,1)S(1)} %copy-done.21, bf16[256,2048]{1,0:T(8,128)(2,1)S(1)} %collective-permute-done.23.refs_1_, bf16[256,2048]{1,0:T(8,128)(2,1)S(1)} %pad_maximum_fusion.7.refs_0_), kind=kOutput, calls=%fused_computation.5 | convolution fusion | flops 8610906112 | bytes 16777216 | tf_op jit(solution)/shard_map/dot_general | solution.py:40
  359.3 5.2 far_rows.3
  371.2 6.4 %near_rows.3 = (f32[256,2048]{1,0:T(8,128)S(1)}, bf16[256,2048]{1,0:T(8,128)(2,1)S(1)}) custom-call(bf16[1024,1024]{1,0:T(8,128)(2,1)S(1)} %copy-done.4, bf16[2048,1024]{1,0:T(8,128)(2,1)S(1)} %copy-done.3, bf16[512,2048]{1,0:T(8,128)(2,1)} %collective-permute-done.28.far), custom_call_target="tpu_custom_call" | custom-call | flops 2147483648 | bytes 4194304 | tf_op jit(solution)/shard_map/near_rows/pallas_call | solution.py:417
  379.9 9.4 %collective-permute-done.29 = bf16[256,2048]{1,0:T(8,128)(2,1)} collective-permute-done((bf16[256,2048]{1,0:T(8,128)(2,1)}, bf16[256,2048]{1,0:T(8,128)(2,1)}, u32[]{:S(2)}, u32[]{:S(2)}) %collective-permute-start.29) | collective-permute-done | bytes 1048608 | tf_op jit(solution)/shard_map/ppermute | solution.py:69
  394.3 4.9 convolution_convert_fusion.2
  402.2 15.6 %collective-permute-done.30 = bf16[128,2048]{1,0:T(8,128)(2,1)S(1)} collective-permute-done((bf16[128,2048]{1,0:T(8,128)(2,1)S(1)}, bf16[128,2048]{1,0:T(8,128)(2,1)S(1)}, u32[]{:S(2)}, u32[]{:S(2)}) %collective-permute-start.30) | collective-permute-done | bytes 524320 | tf_op jit(solution)/shard_map/ppermute | solution.py:69
  417.8 10.8 %collective-permute-done.31 = bf16[256,2048]{1,0:T(8,128)(2,1)S(1)} collective-permute-done((bf16[256,2048]{1,0:T(8,128)(2,1)S(1)}, bf16[256,2048]{1,0:T(8,128)(2,1)S(1)}, u32[]{:S(2)}, u32[]{:S(2)}) %collective-permute-start.31) | collective-permute-done | bytes 1048608 | tf_op jit(solution)/shard_map/ppermute | solution.py:69
  439.5 19.8 %collective-permute-done.33 = bf16[128,2048]{1,0:T(8,128)(2,1)S(1)} collective-permute-done((bf16[128,2048]{1,0:T(8,128)(2,1)S(1)}, bf16[128,2048]{1,0:T(8,128)(2,1)S(1)}, u32[]{:S(2)}, u32[]{:S(2)}) %collective-permute-start.33) | collective-permute-done | bytes 524320 | tf_op jit(solution)/shard_map/ppermute | solution.py:69
  473.0 4.6 collective-permute-done.37.refs_1_
  493.8 15.6 %attention_back.1 = bf16[1024,384]{1,0:T(8,128)(2,1)S(1)} custom-call(s32[1]{0:T(128)S(6)} %copy.72.prefix, s32[1,1024]{1,0:T(1,128)S(1)} %bitcast.160, s32[1024,1]{1,0:T(8,128)S(1)} %copy-done.11, f32[1024,128]{1,0:T(8,128)S(1)} %copy-done.13, f32[1024,128]{1,0:T(8,128)S(1)} %copy-done.15, f32[1024,128]{1,0:T(8,128)S(1)} %copy-done.17, ...), custom_call_target="tpu_custom_call" | custom-call | flops 5368709120 | bytes 3145728 | tf_op jit(solution)/shard_map/attention_back/pallas_call | solution.py:318
  509.4 5.4 convolution_convert_fusion.3
  514.8 5.1 reduce-scatter.6.cloned.1.call-done
  521.9 16.9 %collective-permute-start.46 = (bf16[256,384]{1,0:T(8,128)(2,1)S(1)}, bf16[256,384]{1,0:T(8,128)(2,1)S(1)}, u32[]{:S(2)}, u32[]{:S(2)}) collective-permute-start(bf16[256,384]{1,0:T(8,128)(2,1)S(1)} %pad_maximum_fusion.25), channel_id=1, source_target_pairs={{0,4},{2,6},{4,0},{6,2},{1,5},{3,7},{5,1},{7,3},{8,12},{10,14},{12... | collective-permute-start | bytes 589832 | tf_op jit(solution)/shard_map/ppermute | solution.py:69
  541.1 9.1 %collective-permute-done.46 = bf16[256,384]{1,0:T(8,128)(2,1)S(1)} collective-permute-done((bf16[256,384]{1,0:T(8,128)(2,1)S(1)}, bf16[256,384]{1,0:T(8,128)(2,1)S(1)}, u32[]{:S(2)}, u32[]{:S(2)}) %collective-permute-start.46) | collective-permute-done | bytes 196640 | tf_op jit(solution)/shard_map/ppermute | solution.py:69
  556.7 13.5 %collective-permute-start.48 = (bf16[128,2048]{1,0:T(8,128)(2,1)S(1)}, bf16[128,2048]{1,0:T(8,128)(2,1)S(1)}, u32[]{:S(2)}, u32[]{:S(2)}) collective-permute-start(bf16[128,2048]{1,0:T(8,128)(2,1)S(1)} %far_own.3), channel_id=1, source_target_pairs={{0,1},{1,0},{2,3},{3,2},{4,5},{5,4},{6,7},{7,6},{8,9},{9,8},{10,11... | collective-permute-start | bytes 1572872 | tf_op jit(solution)/shard_map/ppermute | solution.py:104
  582.6 4.7 collective-permute-done.52
  587.4 8.2 %collective-permute-done.54 = bf16[128,1024]{1,0:T(8,128)(2,1)S(1)} collective-permute-done((bf16[128,1024]{1,0:T(8,128)(2,1)S(1)}, bf16[128,1024]{1,0:T(8,128)(2,1)S(1)}, u32[]{:S(2)}, u32[]{:S(2)}) %collective-permute-start.54) | collective-permute-done | bytes 262176 | tf_op jit(solution)/shard_map/ppermute | solution.py:69
  605.3 4.8 collective-permute-start.56
  (475 shorter events, 224.1 us)
Async XLA Ops:
  7.2 170.3 %all-gather.6.cloned.1.call-start = ((), (), s32[]{:S(2)}) async-start(), calls=%async_computation.3 | async-start | bytes 2621440 | tf_op jit(solution)/shard_map/all_gather | solution.py:504
  32.6 187.1 %all-gather.8.cloned.1.call-start = ((), (), s32[]{:S(2)}) async-start(), calls=%async_computation.4 | async-start | bytes 5242880 | tf_op jit(solution)/shard_map/all_gather | solution.py:504
  32.7 27.1 %collective-permute-start.4 = (bf16[256,1024]{1,0:T(8,128)(2,1)S(1)}, bf16[256,1024]{1,0:T(8,128)(2,1)S(1)}, u32[]{:S(2)}, u32[]{:S(2)}) collective-permute-start(bf16[256,1024]{1,0:T(8,128)(2,1)S(1)} %pad_maximum_fusion.18), channel_id=1, source_target_pairs={{0,2},{2,0},{4,6},{6,4},{1,3},{3,1},{5,7},{7,5},{8,10},{10,8},{12,... | collective-permute-start | bytes 1572872 | tf_op jit(solution)/shard_map/ppermute | solution.py:69
  37.3 33.8 %collective-permute-start.5 = (bf16[128,2048]{1,0:T(8,128)(2,1)S(1)}, bf16[128,2048]{1,0:T(8,128)(2,1)S(1)}, u32[]{:S(2)}, u32[]{:S(2)}) collective-permute-start(bf16[128,2048]{1,0:T(8,128)(2,1)S(1)} %get-tuple-element.232), channel_id=1, source_target_pairs={{0,2},{2,0},{4,6},{6,4},{1,3},{3,1},{5,7},{7,5},{8,10},{10,8},{12,... | collective-permute-start | bytes 1572872 | tf_op jit(solution)/shard_map/ppermute | solution.py:69
  38.7 32.5 %collective-permute-start.6 = (bf16[128,2048]{1,0:T(8,128)(2,1)S(1)}, bf16[128,2048]{1,0:T(8,128)(2,1)S(1)}, u32[]{:S(2)}, u32[]{:S(2)}) collective-permute-start(bf16[128,2048]{1,0:T(8,128)(2,1)S(1)} %get-tuple-element.233), channel_id=1, source_target_pairs={{0,4},{2,6},{4,0},{6,2},{1,5},{3,7},{5,1},{7,3},{8,12},{10,14},{12... | collective-permute-start | bytes 1572872 | tf_op jit(solution)/shard_map/ppermute | solution.py:69
  40.8 44.3 %collective-permute-start.7 = (bf16[128,2048]{1,0:T(8,128)(2,1)S(1)}, bf16[128,2048]{1,0:T(8,128)(2,1)S(1)}, u32[]{:S(2)}, u32[]{:S(2)}) collective-permute-start(bf16[128,2048]{1,0:T(8,128)(2,1)S(1)} %get-tuple-element.230), channel_id=1, source_target_pairs={{0,6},{2,4},{4,2},{6,0},{1,7},{3,5},{5,3},{7,1},{8,14},{10,12},{12... | collective-permute-start | bytes 1572872 | tf_op jit(solution)/shard_map/ppermute | solution.py:69
  86.4 213.0 %all-gather.10.cloned.1.call-start = ((), (), s32[]{:S(2)}) async-start(), calls=%async_computation.5 | async-start | bytes 10485760 | tf_op jit(solution)/shard_map/all_gather | solution.py:504
  88.3 211.1 %all-gather.12.cloned.1.call-start = ((), (), s32[]{:S(2)}) async-start(), calls=%async_computation.6 | async-start | bytes 5242880 | tf_op jit(solution)/shard_map/all_gather | solution.py:504
  118.3 49.5 %collective-permute-start.9 = (bf16[256,2048]{1,0:T(8,128)(2,1)S(1)}, bf16[256,2048]{1,0:T(8,128)(2,1)S(1)}, u32[]{:S(2)}, u32[]{:S(2)}) collective-permute-start(bf16[256,2048]{1,0:T(8,128)(2,1)S(1)} %pad_maximum_fusion.4), channel_id=1, source_target_pairs={{0,2},{2,0},{4,6},{6,4},{1,3},{3,1},{5,7},{7,5},{8,10},{10,8},{12,... | collective-permute-start | bytes 3145736 | tf_op jit(solution)/shard_map/ppermute | solution.py:69
  118.7 49.1 %collective-permute-start.10 = (bf16[128,1024]{1,0:T(8,128)(2,1)S(1)}, bf16[128,1024]{1,0:T(8,128)(2,1)S(1)}, u32[]{:S(2)}, u32[]{:S(2)}) collective-permute-start(bf16[128,1024]{1,0:T(8,128)(2,1)S(1)} %get-tuple-element.263), channel_id=1, source_target_pairs={{0,2},{2,0},{4,6},{6,4},{1,3},{3,1},{5,7},{7,5},{8,10},{10,8},{12,... | collective-permute-start | bytes 786440 | tf_op jit(solution)/shard_map/ppermute | solution.py:69
  120.2 47.6 %collective-permute-start.11 = (bf16[128,1024]{1,0:T(8,128)(2,1)S(1)}, bf16[128,1024]{1,0:T(8,128)(2,1)S(1)}, u32[]{:S(2)}, u32[]{:S(2)}) collective-permute-start(bf16[128,1024]{1,0:T(8,128)(2,1)S(1)} %get-tuple-element.262), channel_id=1, source_target_pairs={{0,4},{2,6},{4,0},{6,2},{1,5},{3,7},{5,1},{7,3},{8,12},{10,14},{12... | collective-permute-start | bytes 786440 | tf_op jit(solution)/shard_map/ppermute | solution.py:69
  120.2 47.6 %collective-permute-start.12 = (bf16[128,1024]{1,0:T(8,128)(2,1)S(1)}, bf16[128,1024]{1,0:T(8,128)(2,1)S(1)}, u32[]{:S(2)}, u32[]{:S(2)}) collective-permute-start(bf16[128,1024]{1,0:T(8,128)(2,1)S(1)} %get-tuple-element.261), channel_id=1, source_target_pairs={{0,6},{2,4},{4,2},{6,0},{1,7},{3,5},{5,3},{7,1},{8,14},{10,12},{12... | collective-permute-start | bytes 786440 | tf_op jit(solution)/shard_map/ppermute | solution.py:69
  122.4 45.5 %collective-permute-start.13 = (bf16[128,1536]{1,0:T(8,128)(2,1)S(1)}, bf16[128,1536]{1,0:T(8,128)(2,1)S(1)}, u32[]{:S(2)}, u32[]{:S(2)}) collective-permute-start(bf16[128,1536]{1,0:T(8,128)(2,1)S(1)} %bitcast.177), channel_id=1, source_target_pairs={{0,4},{2,6},{4,0},{6,2},{1,5},{3,7},{5,1},{7,3},{8,12},{10,14},{12... | collective-permute-start | bytes 1179656 | tf_op jit(solution)/shard_map/ppermute | solution.py:69
  171.6 208.3 %all-gather.14.cloned.1.call-start = ((), (), s32[]{:S(2)}) async-start(), calls=%async_computation.7 | async-start | bytes 7864320 | tf_op jit(solution)/shard_map/all_gather | solution.py:504
  177.4 30.1 %collective-permute-start.16 = (bf16[256,1536]{1,0:T(8,128)(2,1)}, bf16[256,1536]{1,0:T(8,128)(2,1)}, u32[]{:S(2)}, u32[]{:S(2)}) collective-permute-start(bf16[256,1536]{1,0:T(8,128)(2,1)} %pad_maximum_fusion.13), channel_id=1, source_target_pairs={{0,2},{2,0},{4,6},{6,4},{1,3},{3,1},{5,7},{7,5},{8,10},{10,8},{12,... | collective-permute-start | bytes 2359304 | tf_op jit(solution)/shard_map/ppermute | solution.py:69
  228.0 36.6 %collective-permute-start.22 = (bf16[256,2048]{1,0:T(8,128)(2,1)}, bf16[256,2048]{1,0:T(8,128)(2,1)}, u32[]{:S(2)}, u32[]{:S(2)}) collective-permute-start(bf16[256,2048]{1,0:T(8,128)(2,1)} %pad_maximum_fusion.6), channel_id=1, source_target_pairs={{0,2},{2,0},{4,6},{6,4},{1,3},{3,1},{5,7},{7,5},{8,10},{10,8},{12,... | collective-permute-start | bytes 3145736 | tf_op jit(solution)/shard_map/ppermute | solution.py:69
  231.0 251.1 %reduce-scatter.4.cloned.1.call-start = ((), (), s32[]{:S(2)}) async-start(), calls=%async_computation.8 | async-start | bytes 10485760 | tf_op jit(solution)/shard_map/reduce_scatter | solution.py:631
  236.0 28.6 %collective-permute-start.21 = (bf16[128,2048]{1,0:T(8,128)(2,1)S(1)}, bf16[128,2048]{1,0:T(8,128)(2,1)S(1)}, u32[]{:S(2)}, u32[]{:S(2)}) collective-permute-start(bf16[128,2048]{1,0:T(8,128)(2,1)S(1)} %multiply_convert_fusion), channel_id=1, source_target_pairs={{0,4},{2,6},{4,0},{6,2},{1,5},{3,7},{5,1},{7,3},{8,12},{10,14},{12... | collective-permute-start | bytes 1572872 | tf_op jit(solution)/shard_map/ppermute | solution.py:69
  266.1 29.0 %collective-permute-start.26 = (bf16[512,2048]{1,0:T(8,128)(2,1)S(1)}, bf16[512,2048]{1,0:T(8,128)(2,1)S(1)}, u32[]{:S(2)}, u32[]{:S(2)}) collective-permute-start(bf16[512,2048]{1,0:T(8,128)(2,1)S(1)} %pad_maximum_fusion.2), channel_id=1, source_target_pairs={{0,1},{1,0},{2,3},{3,2},{4,5},{5,4},{6,7},{7,6},{8,9},{9,8},{10,11... | collective-permute-start | bytes 6291464 | tf_op jit(solution)/shard_map/ppermute | solution.py:104
  267.4 28.0 %collective-permute-start.24 = (bf16[256,2048]{1,0:T(8,128)(2,1)S(1)}, bf16[256,2048]{1,0:T(8,128)(2,1)S(1)}, u32[]{:S(2)}, u32[]{:S(2)}) collective-permute-start(bf16[256,2048]{1,0:T(8,128)(2,1)S(1)} %pad_maximum_fusion.7.refs_0_), channel_id=1, source_target_pairs={{0,1},{1,0},{2,3},{3,2},{4,5},{5,4},{6,7},{7,6},{8,9},{9,8},{10,11... | collective-permute-start | bytes 3145736 | tf_op jit(solution)/shard_map/ppermute | solution.py:104
  355.5 164.5 %reduce-scatter.6.cloned.1.call-start = ((), (), s32[]{:S(2)}) async-start(), calls=%async_computation.9 | async-start | bytes 5242880 | tf_op jit(solution)/shard_map/reduce_scatter | solution.py:631
  394.3 34.3 %collective-permute-start.31 = (bf16[256,2048]{1,0:T(8,128)(2,1)S(1)}, bf16[256,2048]{1,0:T(8,128)(2,1)S(1)}, u32[]{:S(2)}, u32[]{:S(2)}) collective-permute-start(bf16[256,2048]{1,0:T(8,128)(2,1)S(1)} %copy-done.23), channel_id=1, source_target_pairs={{0,2},{2,0},{4,6},{6,4},{1,3},{3,1},{5,7},{7,5},{8,10},{10,8},{12,... | collective-permute-start | bytes 3145736 | tf_op jit(solution)/shard_map/ppermute | solution.py:69
  399.5 37.3 %collective-permute-start.35 = (bf16[512,1024]{1,0:T(8,128)(2,1)S(1)}, bf16[512,1024]{1,0:T(8,128)(2,1)S(1)}, u32[]{:S(2)}, u32[]{:S(2)}) collective-permute-start(bf16[512,1024]{1,0:T(8,128)(2,1)S(1)} %pad_maximum_fusion.10), channel_id=1, source_target_pairs={{0,16},{8,24},{16,0},{24,8},{1,17},{9,25},{17,1},{25,9},{2,18},{10... | collective-permute-start | bytes 3145736 | tf_op jit(solution)/shard_map/ppermute | solution.py:69
  400.9 35.9 %collective-permute-start.34 = (bf16[512,1024]{1,0:T(8,128)(2,1)S(1)}, bf16[512,1024]{1,0:T(8,128)(2,1)S(1)}, u32[]{:S(2)}, u32[]{:S(2)}) collective-permute-start(bf16[512,1024]{1,0:T(8,128)(2,1)S(1)} %pad_maximum_fusion.9), channel_id=1, source_target_pairs={{0,8},{8,0},{16,24},{24,16},{1,9},{9,1},{17,25},{25,17},{2,10},{10... | collective-permute-start | bytes 3145736 | tf_op jit(solution)/shard_map/ppermute | solution.py:69
  463.4 140.7 %reduce-scatter.8.cloned.1.call-start = ((), (), s32[]{:S(2)}) async-start(), calls=%async_computation.10 | async-start | bytes 1966080 | tf_op jit(solution)/shard_map/reduce_scatter | solution.py:631
  485.0 35.0 %collective-permute-start.42 = (bf16[128,2048]{1,0:T(8,128)(2,1)}, bf16[128,2048]{1,0:T(8,128)(2,1)}, u32[]{:S(2)}, u32[]{:S(2)}) collective-permute-start(bf16[128,2048]{1,0:T(8,128)(2,1)} %get-tuple-element.224), channel_id=1, source_target_pairs={{0,2},{2,0},{4,6},{6,4},{1,3},{3,1},{5,7},{7,5},{8,10},{10,8},{12,... | collective-permute-start | bytes 1572872 | tf_op jit(solution)/shard_map/ppermute | solution.py:69
  485.6 34.4 %collective-permute-start.43 = (bf16[128,2048]{1,0:T(8,128)(2,1)}, bf16[128,2048]{1,0:T(8,128)(2,1)}, u32[]{:S(2)}, u32[]{:S(2)}) collective-permute-start(bf16[128,2048]{1,0:T(8,128)(2,1)} %get-tuple-element.223), channel_id=1, source_target_pairs={{0,4},{2,6},{4,0},{6,2},{1,5},{3,7},{5,1},{7,3},{8,12},{10,14},{12... | collective-permute-start | bytes 1572872 | tf_op jit(solution)/shard_map/ppermute | solution.py:69
  486.7 35.1 %collective-permute-start.44 = (bf16[128,2048]{1,0:T(8,128)(2,1)}, bf16[128,2048]{1,0:T(8,128)(2,1)}, u32[]{:S(2)}, u32[]{:S(2)}) collective-permute-start(bf16[128,2048]{1,0:T(8,128)(2,1)} %get-tuple-element.222), channel_id=1, source_target_pairs={{0,6},{2,4},{4,2},{6,0},{1,7},{3,5},{5,3},{7,1},{8,14},{10,12},{12... | collective-permute-start | bytes 1572872 | tf_op jit(solution)/shard_map/ppermute | solution.py:69
  492.1 82.2 %collective-permute-start.49 = (bf16[128,1024]{1,0:T(8,128)(2,1)}, bf16[128,1024]{1,0:T(8,128)(2,1)}, u32[]{:S(2)}, u32[]{:S(2)}) collective-permute-start(bf16[128,1024]{1,0:T(8,128)(2,1)} %get-tuple-element.250), channel_id=1, source_target_pairs={{0,2},{2,0},{4,6},{6,4},{1,3},{3,1},{5,7},{7,5},{8,10},{10,8},{12,... | collective-permute-start | bytes 786440 | tf_op jit(solution)/shard_map/ppermute | solution.py:69
  492.1 90.5 %collective-permute-start.50 = (bf16[128,1024]{1,0:T(8,128)(2,1)}, bf16[128,1024]{1,0:T(8,128)(2,1)}, u32[]{:S(2)}, u32[]{:S(2)}) collective-permute-start(bf16[128,1024]{1,0:T(8,128)(2,1)} %get-tuple-element.249), channel_id=1, source_target_pairs={{0,4},{2,6},{4,0},{6,2},{1,5},{3,7},{5,1},{7,3},{8,12},{10,14},{12... | collective-permute-start | bytes 786440 | tf_op jit(solution)/shard_map/ppermute | solution.py:69
  521.9 28.4 %collective-permute-start.46 = (bf16[256,384]{1,0:T(8,128)(2,1)S(1)}, bf16[256,384]{1,0:T(8,128)(2,1)S(1)}, u32[]{:S(2)}, u32[]{:S(2)}) collective-permute-start(bf16[256,384]{1,0:T(8,128)(2,1)S(1)} %pad_maximum_fusion.25), channel_id=1, source_target_pairs={{0,4},{2,6},{4,0},{6,2},{1,5},{3,7},{5,1},{7,3},{8,12},{10,14},{12... | collective-permute-start | bytes 589832 | tf_op jit(solution)/shard_map/ppermute | solution.py:69
  550.2 32.4 %collective-permute-start.51 = (bf16[128,1024]{1,0:T(8,128)(2,1)S(1)}, bf16[128,1024]{1,0:T(8,128)(2,1)S(1)}, u32[]{:S(2)}, u32[]{:S(2)}) collective-permute-start(bf16[128,1024]{1,0:T(8,128)(2,1)S(1)} %copy-done.84), channel_id=1, source_target_pairs={{0,6},{2,4},{4,2},{6,0},{1,7},{3,5},{5,3},{7,1},{8,14},{10,12},{12... | collective-permute-start | bytes 786440 | tf_op jit(solution)/shard_map/ppermute | solution.py:69
  (131 other events, 1585.2 us)
Sparse Core Ops, SparseCore 0:
  32.7 38.9 all-gather.5
  86.5 54.7 all-gather.7
  143.7 87.5 all-gather.9
  233.0 52.6 all-gather.11
  288.0 70.1 all-gather.13
  361.1 100.1 reduce-scatter.3
  464.6 55.3 reduce-scatter.5
  523.0 30.9 reduce-scatter.7
